TPU v7x, 32 devices: a whole 2x2x4 slice. The times are simulated.
32 devices in a mesh: seq: 8 (over z, y), fsdp: 4 (over x, core).
Axes of the slice: x: 2, y: 2, z: 4, core: 2. Of those that a mesh axis runs over, the one named last changes fastest.
Arguments:
- patches: bfloat16 [32, 1472, 1152], P('fsdp', 'seq'), may hold values from -6 to 6
- key_mask: int32 [32, 1472], P('fsdp'), may hold values from 0 to 1, as said below
- attn_norm_gain: bfloat16 [1152], P('fsdp'), may hold values from 0.5 to 1.5
- attn_norm_bias: bfloat16 [1152], P('fsdp'), may hold values from -3 to 3
- query_weight: bfloat16 [1152, 1152], P('fsdp'), may hold values from -0.1875 to 0.1875
- query_bias: bfloat16 [1152], P('fsdp'), may hold values from -3 to 3
- key_weight: bfloat16 [1152, 1152], P('fsdp'), may hold values from -0.1875 to 0.1875
- value_weight: bfloat16 [1152, 1152], P('fsdp'), may hold values from -0.1875 to 0.1875
- value_bias: bfloat16 [1152], P('fsdp'), may hold values from -3 to 3
- out_weight: bfloat16 [1152, 1152], P('fsdp'), may hold values from -1.5 to 1.5
- out_bias: bfloat16 [1152], P('fsdp'), may hold values from -3 to 3
- mlp_norm_gain: bfloat16 [1152], P('fsdp'), may hold values from 0.5 to 1.5
- mlp_norm_bias: bfloat16 [1152], P('fsdp'), may hold values from -3 to 3
- up_weight: bfloat16 [1152, 4304], P('fsdp'), may hold values from -0.1875 to 0.1875
- up_bias: bfloat16 [4304], P('fsdp'), may hold values from -3 to 3
- down_weight: bfloat16 [4304, 1152], P(None, 'fsdp'), may hold values from -0.09375 to 0.09375
- down_bias: bfloat16 [1152], P('fsdp'), may hold values from -3 to 3
- cotangent: bfloat16 [32, 1472, 1152], P('fsdp', 'seq'), may hold values from -6 to 6
Outputs:
- output: bfloat16 [32, 1472, 1152], P('fsdp', 'seq')
- input_grad: bfloat16 [32, 1472, 1152], P('fsdp', 'seq')
- attn_norm_gain_grad: float32 [1152], P('fsdp')
- attn_norm_bias_grad: float32 [1152], P('fsdp')
- query_weight_grad: float32 [1152, 1152], P('fsdp')
- query_bias_grad: float32 [1152], P('fsdp')
- key_weight_grad: float32 [1152, 1152], P('fsdp')
- value_weight_grad: float32 [1152, 1152], P('fsdp')
- value_bias_grad: float32 [1152], P('fsdp')
- out_weight_grad: float32 [1152, 1152], P('fsdp')
- out_bias_grad: float32 [1152], P('fsdp')
- mlp_norm_gain_grad: float32 [1152], P('fsdp')
- mlp_norm_bias_grad: float32 [1152], P('fsdp')
- up_weight_grad: float32 [1152, 4304], P('fsdp')
- up_bias_grad: float32 [4304], P('fsdp')
- down_weight_grad: float32 [4304, 1152], P(None, 'fsdp')
- down_bias_grad: float32 [1152], P('fsdp')
Inputs may be any that keep to these rules, and one draw needn't show every extreme that they name: `key_mask`: in each image (each run of 736 positions of a row) exactly 729 positions hold 1 and the others 0.
All inputs are finite; a program needn't handle non-finite values.
Results may differ from a plain program's by a relative error of at most 0.019.
Values may be sent and summed in bfloat16 or wider, within the bound.
No kernel may reach another device: no remote copies, remote signals or barrier semaphores. Data moves between devices by JAX's collectives and lax.ppermute only.
A program may use at most 320 MiB of HBM per device.

v0:
```python
import math

import jax
import jax.numpy as jnp
from jax import lax
from jax.sharding import PartitionSpec as P

H = 16
HD = 72
SEQ = 736


epsilon = 1e-06


def layer_norm(values, norm_gain, norm_shift):
    center = values - jnp.mean(values, -1, keepdims=True)
    spread = jnp.mean(center * center, -1, keepdims=True)
    return center * lax.rsqrt(spread + epsilon) * norm_gain + norm_shift


def gelu_tanh(values):
    return jax.nn.gelu(values, approximate=True)


def matmul(left_side, right_side):
    return jnp.dot(left_side, right_side, preferred_element_type=jnp.float32)


def inner_rows(left_side, right_side):
    return lax.dot_general(
        left_side, right_side, (((0,), (0,)), ((), ())), preferred_element_type=jnp.float32
    )


def inner_cols(left_side, right_side):
    return lax.dot_general(
        left_side, right_side, (((1,), (1,)), ((), ())), preferred_element_type=jnp.float32
    )


def column_sum(values):
    return jnp.sum(values.astype(jnp.float32), 0)


def head_scores(query_rows, key_rows, key_keep, head_count, score_scale):
    query_heads = query_rows.reshape(query_rows.shape[0], head_count, -1)
    key_heads = key_rows.reshape(key_rows.shape[0], head_count, -1)
    raw_scores = jnp.einsum(
        "qhd,khd->hqk", query_heads, key_heads, preferred_element_type=jnp.float32
    )
    scores = jnp.where(key_keep[None, None, :] > 0, raw_scores * score_scale, -1e30)
    return (scores, query_heads, key_heads)


def attend_forward(query_rows, key_rows, value_rows, key_keep, head_count, score_scale):
    scores, query_heads, key_heads = head_scores(
        query_rows, key_rows, key_keep, head_count, score_scale
    )
    top_score = jnp.max(scores, -1, keepdims=True)
    log_total = top_score + jnp.log(jnp.sum(jnp.exp(scores - top_score), -1, keepdims=True))
    attn_probs = jnp.exp(scores - log_total).astype(jnp.bfloat16)
    value_heads = value_rows.reshape(value_rows.shape[0], head_count, -1)
    context = jnp.einsum(
        "hqk,khd->qhd", attn_probs, value_heads, preferred_element_type=jnp.float32
    )
    return (context.reshape(query_rows.shape[0], -1).astype(jnp.bfloat16), log_total[:, :, 0])


def attend_backward(
    query_rows, key_rows, value_rows, context_grad, log_total, key_keep, head_count, score_scale
):
    scores, query_heads, key_heads = head_scores(
        query_rows, key_rows, key_keep, head_count, score_scale
    )
    attn_probs = jnp.exp(scores - log_total[:, :, None])
    value_heads = value_rows.reshape(value_rows.shape[0], head_count, -1)
    grad_heads = context_grad.reshape(context_grad.shape[0], head_count, -1)
    prob_grad = jnp.einsum(
        "qhd,khd->hqk", grad_heads, value_heads, preferred_element_type=jnp.float32
    )
    row_dot = jnp.sum(attn_probs * prob_grad, -1, keepdims=True)
    score_grad = (attn_probs * (prob_grad - row_dot) * score_scale).astype(jnp.bfloat16)
    query_grad = jnp.einsum(
        "hqk,khd->qhd", score_grad, key_heads, preferred_element_type=jnp.float32
    )
    key_grad = jnp.einsum(
        "hqk,qhd->khd", score_grad, query_heads, preferred_element_type=jnp.float32
    )
    value_grad = jnp.einsum(
        "hqk,qhd->khd",
        attn_probs.astype(jnp.bfloat16),
        grad_heads,
        preferred_element_type=jnp.float32,
    )
    length = query_rows.shape[0]
    return (
        query_grad.reshape(length, -1).astype(jnp.bfloat16),
        key_grad.reshape(length, -1).astype(jnp.bfloat16),
        value_grad.reshape(length, -1).astype(jnp.bfloat16),
    )


def body(
    patches,
    key_mask,
    attn_norm_gain,
    attn_norm_bias,
    query_weight,
    query_bias,
    key_weight,
    value_weight,
    value_bias,
    out_weight,
    out_bias,
    mlp_norm_gain,
    mlp_norm_bias,
    up_weight,
    up_bias,
    down_weight,
    down_bias,
    cotangent,
):
    row_groups = patches.shape[0]
    local_len = patches.shape[1]
    model_width = patches.shape[2]
    full_len = key_mask.shape[1]
    pack_count = full_len // SEQ
    image_count = row_groups * pack_count
    row_count = row_groups * local_len
    seq_count = lax.axis_size("seq")
    head_count = H // seq_count
    score_scale = 1.0 / math.sqrt(HD)
    attn_full = (
        lax.all_gather(attn_norm_gain, "fsdp", axis=0, tiled=True),
        lax.all_gather(attn_norm_bias, "fsdp", axis=0, tiled=True),
        lax.all_gather(query_weight, "fsdp", axis=0, tiled=True),
        lax.all_gather(query_bias, "fsdp", axis=0, tiled=True),
        lax.all_gather(key_weight, "fsdp", axis=0, tiled=True),
        lax.all_gather(value_weight, "fsdp", axis=0, tiled=True),
        lax.all_gather(value_bias, "fsdp", axis=0, tiled=True),
        lax.all_gather(out_weight, "fsdp", axis=0, tiled=True),
        lax.all_gather(out_bias, "fsdp", axis=0, tiled=True),
        lax.all_gather(mlp_norm_gain, "fsdp", axis=0, tiled=True),
        lax.all_gather(mlp_norm_bias, "fsdp", axis=0, tiled=True),
    )
    mlp_full = (
        lax.all_gather(up_weight, "fsdp", axis=0, tiled=True),
        lax.all_gather(up_bias, "fsdp", axis=0, tiled=True),
        lax.all_gather(down_weight, "fsdp", axis=1, tiled=True),
        lax.all_gather(down_bias, "fsdp", axis=0, tiled=True),
    )
    (
        first_gain,
        first_shift,
        query_full,
        query_shift,
        key_full,
        value_full,
        value_shift,
        out_full,
        out_shift,
        second_gain,
        second_shift,
    ) = attn_full
    up_full, up_shift, down_full, down_shift = mlp_full
    first_token = lax.axis_index("seq") * local_len
    local_keep = lax.dynamic_slice_in_dim(key_mask, first_token, local_len, 1)
    image_keep = key_mask.reshape(image_count, SEQ)
    inputs = patches.reshape(row_count, model_width).astype(jnp.float32)
    normed_one = layer_norm(inputs, first_gain.astype(jnp.float32), first_shift.astype(jnp.float32))
    normed_low = normed_one.astype(jnp.bfloat16)
    queries = (matmul(normed_low, query_full) + query_shift.astype(jnp.float32)).astype(
        jnp.bfloat16
    )
    key_rows = matmul(normed_low, key_full).astype(jnp.bfloat16)
    value_rows = (matmul(normed_low, value_full) + value_shift.astype(jnp.float32)).astype(
        jnp.bfloat16
    )
    head_query, head_key, head_value = (
        lax.all_to_all(
            queries.reshape(row_groups, local_len, model_width),
            "seq",
            split_axis=2,
            concat_axis=1,
            tiled=True,
        ),
        lax.all_to_all(
            key_rows.reshape(row_groups, local_len, model_width),
            "seq",
            split_axis=2,
            concat_axis=1,
            tiled=True,
        ),
        lax.all_to_all(
            value_rows.reshape(row_groups, local_len, model_width),
            "seq",
            split_axis=2,
            concat_axis=1,
            tiled=True,
        ),
    )
    head_query = head_query.reshape(image_count, SEQ, -1)
    head_key = head_key.reshape(image_count, SEQ, -1)
    head_value = head_value.reshape(image_count, SEQ, -1)

    def forward_image(bundle):
        return attend_forward(bundle[0], bundle[1], bundle[2], bundle[3], head_count, score_scale)

    head_context, log_totals = lax.map(
        forward_image, (head_query, head_key, head_value, image_keep)
    )
    head_context = head_context.reshape(row_groups, full_len, -1)
    context_tok = lax.all_to_all(
        head_context, "seq", split_axis=1, concat_axis=2, tiled=True
    ).reshape(row_count, model_width)
    hidden = inputs + matmul(context_tok, out_full) + out_shift.astype(jnp.float32)
    normed_two = layer_norm(
        hidden, second_gain.astype(jnp.float32), second_shift.astype(jnp.float32)
    )
    normed_two_low = normed_two.astype(jnp.bfloat16)
    preact = matmul(normed_two_low, up_full) + up_shift.astype(jnp.float32)
    active_low = gelu_tanh(preact).astype(jnp.bfloat16)
    output = hidden + matmul(active_low, down_full) + down_shift.astype(jnp.float32)
    out_grad = cotangent.reshape(row_count, model_width).astype(jnp.float32) * local_keep.reshape(
        row_count, 1
    ).astype(jnp.float32)
    out_grad_low = out_grad.astype(jnp.bfloat16)
    down_weight_grad = inner_rows(active_low, out_grad_low)
    down_bias_grad = column_sum(out_grad_low)
    active_grad = inner_cols(out_grad_low, down_full)
    pre_grad = jax.vjp(gelu_tanh, preact)[1](active_grad)[0].astype(jnp.bfloat16)
    up_weight_grad = inner_rows(normed_two_low, pre_grad)
    up_bias_grad = column_sum(pre_grad)
    up_into, up_bias_into, down_into, down_bias_into = (
        up_weight_grad,
        up_bias_grad,
        down_weight_grad,
        down_bias_grad,
    )
    up_owned_weight, up_owned_bias, down_owned_weight, down_owned_bias = (
        lax.psum_scatter(
            up_into.astype(jnp.bfloat16), "fsdp", scatter_dimension=0, tiled=True
        ).astype(jnp.float32),
        lax.psum_scatter(
            up_bias_into.astype(jnp.bfloat16), "fsdp", scatter_dimension=0, tiled=True
        ).astype(jnp.float32),
        lax.psum_scatter(
            down_into.astype(jnp.bfloat16), "fsdp", scatter_dimension=1, tiled=True
        ).astype(jnp.float32),
        lax.psum_scatter(
            down_bias_into.astype(jnp.bfloat16), "fsdp", scatter_dimension=0, tiled=True
        ).astype(jnp.float32),
    )
    up_owned_weight, up_owned_bias, down_owned_weight, down_owned_bias = (
        lax.psum(up_owned_weight.astype(jnp.bfloat16), "seq").astype(jnp.float32),
        lax.psum(up_owned_bias.astype(jnp.bfloat16), "seq").astype(jnp.float32),
        lax.psum(down_owned_weight.astype(jnp.bfloat16), "seq").astype(jnp.float32),
        lax.psum(down_owned_bias.astype(jnp.bfloat16), "seq").astype(jnp.float32),
    )
    normed_two_grad = inner_cols(pre_grad, up_full)
    norm_two_pull = jax.vjp(
        layer_norm, hidden, second_gain.astype(jnp.float32), second_shift.astype(jnp.float32)
    )[1]
    hidden_part, second_gain_grad, second_shift_grad = norm_two_pull(normed_two_grad)
    hidden_grad = out_grad + hidden_part
    attn_grad_low = hidden_grad.astype(jnp.bfloat16)
    out_weight_grad = inner_rows(context_tok, attn_grad_low)
    out_bias_grad = column_sum(attn_grad_low)
    context_grad = inner_cols(attn_grad_low, out_full).astype(jnp.bfloat16)
    head_context_grad = lax.all_to_all(
        context_grad.reshape(row_groups, local_len, model_width),
        "seq",
        split_axis=2,
        concat_axis=1,
        tiled=True,
    ).reshape(image_count, SEQ, -1)

    def backward_image(bundle):
        return attend_backward(
            bundle[0],
            bundle[1],
            bundle[2],
            bundle[3],
            bundle[4],
            bundle[5],
            head_count,
            score_scale,
        )

    query_grad_h, key_grad_h, value_grad_h = lax.map(
        backward_image,
        (head_query, head_key, head_value, head_context_grad, log_totals, image_keep),
    )
    query_grad_h = query_grad_h.reshape(row_groups, full_len, -1)
    key_grad_h = key_grad_h.reshape(row_groups, full_len, -1)
    value_grad_h = value_grad_h.reshape(row_groups, full_len, -1)
    query_grad_t, key_grad_t, value_grad_t = (
        lax.all_to_all(query_grad_h, "seq", split_axis=1, concat_axis=2, tiled=True),
        lax.all_to_all(key_grad_h, "seq", split_axis=1, concat_axis=2, tiled=True),
        lax.all_to_all(value_grad_h, "seq", split_axis=1, concat_axis=2, tiled=True),
    )
    query_grad_t = query_grad_t.reshape(row_count, model_width)
    key_grad_t = key_grad_t.reshape(row_count, model_width)
    value_grad_t = value_grad_t.reshape(row_count, model_width)
    query_weight_grad = inner_rows(normed_low, query_grad_t)
    query_bias_grad = column_sum(query_grad_t)
    key_weight_grad = inner_rows(normed_low, key_grad_t)
    value_weight_grad = inner_rows(normed_low, value_grad_t)
    value_bias_grad = column_sum(value_grad_t)
    normed_one_grad = (
        inner_cols(query_grad_t, query_full)
        + inner_cols(key_grad_t, key_full)
        + inner_cols(value_grad_t, value_full)
    )
    norm_one_pull = jax.vjp(
        layer_norm, inputs, first_gain.astype(jnp.float32), first_shift.astype(jnp.float32)
    )[1]
    input_part, first_gain_grad, first_shift_grad = norm_one_pull(normed_one_grad)
    input_grad = (
        (hidden_grad + input_part).astype(jnp.bfloat16).reshape(row_groups, local_len, model_width)
    )
    (
        gain_one_owned,
        shift_one_owned,
        query_owned,
        query_bias_owned,
        key_owned,
        value_owned,
        value_bias_owned,
        out_owned,
        out_bias_owned,
        gain_two_owned,
        shift_two_owned,
    ) = (
        lax.psum_scatter(
            first_gain_grad.astype(jnp.bfloat16), "fsdp", scatter_dimension=0, tiled=True
        ).astype(jnp.float32),
        lax.psum_scatter(
            first_shift_grad.astype(jnp.bfloat16), "fsdp", scatter_dimension=0, tiled=True
        ).astype(jnp.float32),
        lax.psum_scatter(
            query_weight_grad.astype(jnp.bfloat16), "fsdp", scatter_dimension=0, tiled=True
        ).astype(jnp.float32),
        lax.psum_scatter(
            query_bias_grad.astype(jnp.bfloat16), "fsdp", scatter_dimension=0, tiled=True
        ).astype(jnp.float32),
        lax.psum_scatter(
            key_weight_grad.astype(jnp.bfloat16), "fsdp", scatter_dimension=0, tiled=True
        ).astype(jnp.float32),
        lax.psum_scatter(
            value_weight_grad.astype(jnp.bfloat16), "fsdp", scatter_dimension=0, tiled=True
        ).astype(jnp.float32),
        lax.psum_scatter(
            value_bias_grad.astype(jnp.bfloat16), "fsdp", scatter_dimension=0, tiled=True
        ).astype(jnp.float32),
        lax.psum_scatter(
            out_weight_grad.astype(jnp.bfloat16), "fsdp", scatter_dimension=0, tiled=True
        ).astype(jnp.float32),
        lax.psum_scatter(
            out_bias_grad.astype(jnp.bfloat16), "fsdp", scatter_dimension=0, tiled=True
        ).astype(jnp.float32),
        lax.psum_scatter(
            second_gain_grad.astype(jnp.bfloat16), "fsdp", scatter_dimension=0, tiled=True
        ).astype(jnp.float32),
        lax.psum_scatter(
            second_shift_grad.astype(jnp.bfloat16), "fsdp", scatter_dimension=0, tiled=True
        ).astype(jnp.float32),
    )
    (
        gain_one_owned,
        shift_one_owned,
        query_owned,
        query_bias_owned,
        key_owned,
        value_owned,
        value_bias_owned,
        out_owned,
        out_bias_owned,
        gain_two_owned,
        shift_two_owned,
    ) = (
        lax.psum(gain_one_owned.astype(jnp.bfloat16), "seq").astype(jnp.float32),
        lax.psum(shift_one_owned.astype(jnp.bfloat16), "seq").astype(jnp.float32),
        lax.psum(query_owned.astype(jnp.bfloat16), "seq").astype(jnp.float32),
        lax.psum(query_bias_owned.astype(jnp.bfloat16), "seq").astype(jnp.float32),
        lax.psum(key_owned.astype(jnp.bfloat16), "seq").astype(jnp.float32),
        lax.psum(value_owned.astype(jnp.bfloat16), "seq").astype(jnp.float32),
        lax.psum(value_bias_owned.astype(jnp.bfloat16), "seq").astype(jnp.float32),
        lax.psum(out_owned.astype(jnp.bfloat16), "seq").astype(jnp.float32),
        lax.psum(out_bias_owned.astype(jnp.bfloat16), "seq").astype(jnp.float32),
        lax.psum(gain_two_owned.astype(jnp.bfloat16), "seq").astype(jnp.float32),
        lax.psum(shift_two_owned.astype(jnp.bfloat16), "seq").astype(jnp.float32),
    )
    output_low = output.astype(jnp.bfloat16).reshape(row_groups, local_len, model_width)
    return (
        output_low,
        input_grad,
        gain_one_owned,
        shift_one_owned,
        query_owned,
        query_bias_owned,
        key_owned,
        value_owned,
        value_bias_owned,
        out_owned,
        out_bias_owned,
        gain_two_owned,
        shift_two_owned,
        up_owned_weight,
        up_owned_bias,
        down_owned_weight,
        down_owned_bias,
    )


def solution(mesh):
    in_specs = (
        P("fsdp", "seq", None),
        P("fsdp", None),
        P("fsdp"),
        P("fsdp"),
        P("fsdp", None),
        P("fsdp"),
        P("fsdp", None),
        P("fsdp", None),
        P("fsdp"),
        P("fsdp", None),
        P("fsdp"),
        P("fsdp"),
        P("fsdp"),
        P("fsdp", None),
        P("fsdp"),
        P(None, "fsdp"),
        P("fsdp"),
        P("fsdp", "seq", None),
    )
    out_specs = (
        P("fsdp", "seq", None),
        P("fsdp", "seq", None),
        P("fsdp"),
        P("fsdp"),
        P("fsdp", None),
        P("fsdp"),
        P("fsdp", None),
        P("fsdp", None),
        P("fsdp"),
        P("fsdp", None),
        P("fsdp"),
        P("fsdp"),
        P("fsdp"),
        P("fsdp", None),
        P("fsdp"),
        P(None, "fsdp"),
        P("fsdp"),
    )
    return jax.shard_map(body, mesh=mesh, in_specs=in_specs, out_specs=out_specs, check_vma=False)
```

profile of v0, /device:TPU:0, one launch (start us, length us, event | category | flops | bytes accessed | tf_op | source)
XLA Modules:
  0.0 2363.4 jit_solution(10971464620655402643)
XLA Ops:
  15.8 14.3 all-reduce.21
  38.6 8.6 fusion.42
  66.2 8.6 fusion.43
  81.9 82.9 %all-to-all-done = bf16[8,184,1152]{1,0,2:T(8,128)(2,1)} async-done(((bf16[8,184,1152]{1,0,2:T(8,128)(2,1)}), bf16[8,184,1152]{1,0,2:T(8,128)(2,1)}, u32[]{:S(2)}, u32[]{:S(2)}) %all-to-all-start) | async-done | bytes 3391520 | tf_op jit(solution)/shard_map/all_to_all | solution.py:195
  169.7 8.6 convolution_convert_fusion.3
  185.4 88.2 %all-to-all-done.1 = bf16[8,184,1152]{1,0,2:T(8,128)(2,1)} async-done(((bf16[8,184,1152]{1,0,2:T(8,128)(2,1)}), bf16[8,184,1152]{1,0,2:T(8,128)(2,1)}, u32[]{:S(2)}, u32[]{:S(2)}) %all-to-all-start.1) | async-done | bytes 3391520 | tf_op jit(solution)/shard_map/all_to_all | solution.py:181
  279.5 9.6 copy.107
  289.1 10.3 reshape.392
  304.5 9.7 copy.110
  314.1 10.4 reshape.395
  329.4 52.5 %all-to-all-done.2 = bf16[8,184,1152]{1,0,2:T(8,128)(2,1)} async-done(((bf16[8,184,1152]{1,0,2:T(8,128)(2,1)}), bf16[8,184,1152]{1,0,2:T(8,128)(2,1)}, u32[]{:S(2)}, u32[]{:S(2)}) %all-to-all-start.2) | async-done | bytes 3391520 | tf_op jit(solution)/shard_map/all_to_all | solution.py:188
  382.0 9.6 copy.113
  391.6 9.9 reshape.397
  408.5 105.7 %while.26 = (s32[]{:T(128)}, bf16[16,736,144]{1,2,0:T(8,128)(2,1)}, f32[16,2,736]{2,1,0:T(2,128)}, bf16[16,736,144]{1,2,0:T(8,128)(2,1)}, s32[16,736]{1,0:T(8,12...) while((s32[]{:T(128)}, bf16[16,736,144]{1,2,0:T(8,128)(2,1)}, ...), condition=%wide.region_5.6_spmd, body=%wide.region_2.5_spmd.sunk | while | flops 324039456 | bytes 15607905 | solution.py:210
  526.1 9.4 copy.118
  545.3 24.1 %fusion.59 = f32[1472,4304]{1,0:T(8,128)} fusion(bf16[1472,1152]{1,0:T(8,128)(2,1)} %fusion.45, bf16[4304,1152]{0,1:T(8,128)(2,1)} %all-gather.17.cloned.1.call-done), kind=kOutput, calls=%fused_computation.113 | convolution fusion | flops 14596964352 | bytes 38649856 | tf_op jit(solution)/shard_map/dot_general | solution.py:37
  569.4 103.0 %all-to-all-done.3 = bf16[8,1472,144]{2,0,1:T(8,128)(2,1)} async-done(((bf16[8,1472,144]{2,0,1:T(8,128)(2,1)}), bf16[8,1472,144]{2,0,1:T(8,128)(2,1)}, u32[]{:S(2)}, u32[]{:S(2)}) %all-to-all-start.3) | async-done | bytes 3391520 | tf_op jit(solution)/shard_map/all_to_all | solution.py:214
  672.4 10.7 copy.119
  683.1 8.6 reshape.399
  691.7 8.7 fusion.57
  704.2 43.1 %fusion.51 = (bf16[4304]{0:T(1024)(128)(2,1)}, bf16[1472,4304]{1,0:T(8,128)(2,1)}, f32[1472,4304]{1,0:T(8,128)}) fusion(f32[1472,4304]{1,0:T(8,128)} %fusion.59, f32[4304]{0:T(1024)S(1)} %convert_element_type.312, bf16[1152,4304]{1,0:T(8,128)(2,1)} %all-gather.15.cloned.1.call-done, f32[1472,1152]{1,0:T(8,128)} %copy-done.5, ...), kind=kOutput, calls=%fused_computation.107 | convolution fusion | flops 14744819712 | bytes 80101088 | tf_op jit(solution)/shard_map/dot_general | solution.py:27
  747.2 26.0 %multiply_reduce_fusion.1 = (bf16[1152]{0:T(1024)(128)(2,1)}, f32[1472]{0:T(1024)S(1)}, bf16[1152]{0:T(1024)(128)(2,1)}, f32[1472,1152]{1,0:T(8,128)}) fusion(f32[1472,1152]{1,0:T(8,128)} %copy-done.5, f32[1472]{0:T(1024)S(1)} %fusion.48, f32[1472]{0:T(1024)S(1)} %broadcast_multiply_fusion, f32[1152]{0:T(1024)S(1)} %convert_element_type.309, ...), kind=kOutput, calls=%fused_computation.78 | convolution fusion | flops 14610527232 | bytes 36180224 | tf_op jit(solution)/shard_map/dot_general | solution.py:37
  794.1 108.2 %all_to_all.120 = bf16[8,184,1152]{1,0,2:T(8,128)(2,1)S(1)} all-to-all(bf16[8,184,1152]{1,0,2:T(8,128)(2,1)} %copy.120), channel_id=1, replica_groups=mesh['seq'=8,'fsdp'=4] {'seq'}, dimensions={2} | all-to-all | bytes 6782976 | tf_op jit(solution)/shard_map/all_to_all | solution.py:271
  909.7 8.6 reshape.402
  927.4 499.2 %while.27 = (s32[]{:T(128)}, bf16[16,736,144]{1,2,0:T(8,128)(2,1)}, bf16[16,736,144]{1,2,0:T(8,128)(2,1)}, bf16[16,736,144]{1,2,0:T(8,128)(2,1)}, bf16[16,736,14...) while((s32[]{:T(128)}, bf16[16,736,144]{1,2,0:T(8,128)(2,1)}, ...), condition=%wide.region_12.13_spmd, body=%wide.region_10.12_spmd.sunk | while | flops 795532800 | bytes 35473092 | solution.py:291
  939.1 7.5 fusion.140
  970.3 7.5 fusion.140
  1001.5 7.5 fusion.140
  1032.7 7.5 fusion.140
  1063.9 7.5 fusion.140
  1095.1 7.5 fusion.140
  1126.3 7.5 fusion.140
  1157.4 7.5 fusion.140
  1188.6 7.5 fusion.140
  1219.8 7.5 fusion.140
  1313.4 7.5 fusion.140
  1406.9 7.5 fusion.140
  1434.0 9.4 copy.134
  1448.5 8.0 convolution_convert_fusion.4
  1464.0 9.6 copy.128
  1473.5 106.4 %all-to-all-done.7 = bf16[8,1472,144]{2,0,1:T(8,128)(2,1)} async-done(((bf16[8,1472,144]{2,0,1:T(8,128)(2,1)}), bf16[8,1472,144]{2,0,1:T(8,128)(2,1)}, u32[]{:S(2)}, u32[]{:S(2)}) %all-to-all-start.7) | async-done | bytes 3391520 | tf_op jit(solution)/shard_map/all_to_all | solution.py:301
  1587.6 10.8 copy.135
  1598.4 8.6 reshape.408
  1607.0 9.5 convolution_convert_fusion.5
  1628.4 9.5 copy.131
  1637.9 78.5 %all-to-all-done.5 = bf16[8,1472,144]{2,0,1:T(8,128)(2,1)} async-done(((bf16[8,1472,144]{2,0,1:T(8,128)(2,1)}), bf16[8,1472,144]{2,0,1:T(8,128)(2,1)}, u32[]{:S(2)}, u32[]{:S(2)}) %all-to-all-start.5) | async-done | bytes 3391520 | tf_op jit(solution)/shard_map/all_to_all | solution.py:299
  1721.2 11.0 copy.129
  1732.2 8.7 reshape.404
  1740.9 9.4 convolution_convert_fusion.7
  1750.3 102.4 %all-to-all-done.6 = bf16[8,1472,144]{2,0,1:T(8,128)(2,1)} async-done(((bf16[8,1472,144]{2,0,1:T(8,128)(2,1)}), bf16[8,1472,144]{2,0,1:T(8,128)(2,1)}, u32[]{:S(2)}, u32[]{:S(2)}) %all-to-all-start.6) | async-done | bytes 3391520 | tf_op jit(solution)/shard_map/all_to_all | solution.py:300
  1852.7 11.2 copy.132
  1863.9 8.6 reshape.406
  1872.5 9.5 convolution_convert_fusion.6
  1882.2 24.5 %convolution_convert_fusion = bf16[1152,4304]{1,0:T(8,128)(2,1)} fusion(bf16[1472,4304]{1,0:T(8,128)(2,1)} %get-tuple-element.241, f32[1472,1152]{1,0:T(8,128)} %copy-done.5, f32[1152]{0:T(1024)S(1)} %copy-done.46, f32[1152]{0:T(1024)S(1)} %copy-done.40, f32[1472]{0:T(1024)S(1)} %copy-done.42, f32[1472]{0:T(1024)S(1)} %copy-done.32), kind=kOutput, calls=%fused_computation.54 | convolution fusion | flops 14610401280 | bytes 29391360 | tf_op jit(solution)/shard_map/dot_general | solution.py:31
  1906.7 26.3 %convolution_convert_fusion.1 = bf16[4304,1152]{0,1:T(8,128)(2,1)} fusion(bf16[1472,1152]{1,0:T(8,128)(2,1)} %fusion.45, f32[1472,4304]{1,0:T(8,128)} %get-tuple-element.260), kind=kOutput, calls=%fused_computation.55 | convolution fusion | flops 14658941952 | bytes 38649856 | tf_op jit(solution)/shard_map/dot_general | solution.py:31
  1948.5 8.3 fusion.60
  1956.8 7.9 convolution_add_fusion.3
  1964.8 14.8 fusion.50
  1979.7 12.2 all-reduce.20
  1992.6 35.4 %all-reduce.18 = (bf16[288]{0:T(512)(128)(2,1)S(1)}, bf16[288]{0:T(512)(128)(2,1)S(1)}, bf16[288]{0:T(512)(128)(2,1)S(1)}, bf16[288]{0:T(512)(128)(2,1)S(1)}, bf...) all-reduce(bf16[288]{0:T(512)(128)(2,1)S(1)} %dynamic-slice.10, ...), channel_id=1, replica_groups=mesh['seq'=8,'fsdp'=4] {'seq'}, use_global_device_ids=true, to_apply=%region_17.18 | all-reduce | flops 3380 | bytes 13520 | tf_op jit(solution)/shard_map/psum | solution.py:383
  2033.5 52.7 %reduce-scatter.17.cloned.1.call-done = bf16[4304,288]{0,1:T(8,128)(2,1)} async-done(((bf16[4304,1152]{0,1:T(8,128)(2,1)}), bf16[4304,288]{0,1:T(8,128)(2,1)}) %reduce-scatter.17.cloned.1.call-update) | async-done | bytes 2479120 | tf_op jit(solution)/shard_map/reduce_scatter | solution.py:248
  2095.8 8.1 add_convert_fusion.1
  2103.9 25.6 %fusion.44 = bf16[1472,1152]{1,0:T(8,128)(2,1)} fusion(f32[1472,1152]{1,0:T(8,128)} %copy-done.5, bf16[4304,1152]{0,1:T(8,128)(2,1)} %all-gather.17.cloned.1.call-done, f32[1152]{0:T(1024)S(1)} %convert_element_type.314, f32[1472,4304]{1,0:T(8,128)} %get-tuple-element.260), kind=kOutput, calls=%fused_computation.70 | convolution fusion | flops 14659070976 | bytes 45437440 | tf_op jit(solution)/shard_map/dot_general | solution.py:27
  2129.5 215.5 %all-reduce.24.cloned.1.call-done = (bf16[288,1152]{1,0:T(8,128)(2,1)}, bf16[288,1152]{1,0:T(8,128)(2,1)}, bf16[288,1152]{1,0:T(8,128)(2,1)}, bf16[288,1152]{1,0...) async-done(((bf16[288,1152]{1,0:T(8,128)(2,1)}, bf16[288,1152]{1,0:T(8,128)(2,1)}, bf16[288,1152]{1,0:T(8,128)(2,1)}, bf16[288,1152]{1,0:T(8,128)(2,1)}, ...) | async-done | bytes 7612432 | tf_op jit(solution)/shard_map/psum | solution.py:385
  (599 shorter events, 739.0 us)
Async XLA Ops:
  7.2 31.4 %all-gather.7.cloned.1.call-start = ((), (), s32[]{:S(2)}) async-start(), calls=%async_computation.14 | async-start | bytes 3317760 | tf_op jit(solution)/shard_map/all_gather | solution.py:140
  7.9 58.3 %all-gather.9.cloned.1.call-start = ((), (), s32[]{:S(2)}) async-start(), calls=%async_computation.15 | async-start | bytes 3317760 | tf_op jit(solution)/shard_map/all_gather | solution.py:137
  8.7 161.0 %all-gather.11.cloned.1.call-start = ((), (), s32[]{:S(2)}) async-start(), calls=%async_computation.16 | async-start | bytes 3317760 | tf_op jit(solution)/shard_map/all_gather | solution.py:139
  9.5 4.8 copy-start.53
  9.5 5.1 copy-start.54
  9.5 5.3 copy-start.55
  9.5 5.6 copy-start.56
  9.5 5.8 copy-start.57
  9.5 6.0 copy-start.49
  9.5 535.8 %all-gather.17.cloned.1.call-start = ((), (), s32[]{:S(2)}) async-start(), calls=%async_computation.19 | async-start | bytes 12533760 | tf_op jit(solution)/shard_map/all_gather | solution.py:150
  10.7 19.5 copy-start.20
  11.8 23.8 %copy-start.23 = (f32[1472]{0:T(1024)}, f32[1472]{0:T(1024)S(1)}, u32[]{:S(2)}) copy-start(f32[1472]{0:T(1024)S(1)} %div.43) | copy-start | bytes 17668
  30.2 5.4 copy-start.15
  30.2 5.4 copy-start.29
  54.3 110.5 %all-to-all-start = ((bf16[8,184,1152]{1,0,2:T(8,128)(2,1)}), bf16[8,184,1152]{1,0,2:T(8,128)(2,1)}, u32[]{:S(2)}, u32[]{:S(2)}) async-start(bf16[8,184,1152]{1,0,2:T(8,128)(2,1)} %copy.105), calls=%async_computation | async-start | bytes 9437184 | tf_op jit(solution)/shard_map/all_to_all | solution.py:195
  164.8 108.8 %all-to-all-start.1 = ((bf16[8,184,1152]{1,0,2:T(8,128)(2,1)}), bf16[8,184,1152]{1,0,2:T(8,128)(2,1)}, u32[]{:S(2)}, u32[]{:S(2)}) async-start(bf16[8,184,1152]{1,0,2:T(8,128)(2,1)} %copy.108), calls=%async_computation.1 | async-start | bytes 9437184 | tf_op jit(solution)/shard_map/all_to_all | solution.py:181
  185.4 94.0 %copy-start.37 = (s32[8,1472]{1,0:T(8,128)S(1)}, s32[8,1472]{1,0:T(8,128)}, u32[]{:S(2)}) copy-start(s32[8,1472]{1,0:T(8,128)} %param.23) | copy-start | bytes 141316
  273.6 108.3 %all-to-all-start.2 = ((bf16[8,184,1152]{1,0,2:T(8,128)(2,1)}), bf16[8,184,1152]{1,0,2:T(8,128)(2,1)}, u32[]{:S(2)}, u32[]{:S(2)}) async-start(bf16[8,184,1152]{1,0,2:T(8,128)(2,1)} %copy.111), calls=%async_computation.2 | async-start | bytes 9437184 | tf_op jit(solution)/shard_map/all_to_all | solution.py:188
  278.2 413.5 %all-gather.13.cloned.1.call-start = ((), (), s32[]{:S(2)}) async-start(), calls=%async_computation.17 | async-start | bytes 3317760 | tf_op jit(solution)/shard_map/all_gather | solution.py:142
  278.8 425.3 %all-gather.15.cloned.1.call-start = ((), (), s32[]{:S(2)}) async-start(), calls=%async_computation.18 | async-start | bytes 12533760 | tf_op jit(solution)/shard_map/all_gather | solution.py:148
  514.2 11.9 copy-start.22
  535.6 136.8 %all-to-all-start.3 = ((bf16[8,1472,144]{2,0,1:T(8,128)(2,1)}), bf16[8,1472,144]{2,0,1:T(8,128)(2,1)}, u32[]{:S(2)}, u32[]{:S(2)}) async-start(bf16[8,1472,144]{2,0,1:T(8,128)(2,1)} %copy.118), calls=%async_computation.3 | async-start | bytes 12058624 | tf_op jit(solution)/shard_map/all_to_all | solution.py:214
  540.7 232.5 %copy-start.39 = (f32[1152]{0:T(1024)}, f32[1152]{0:T(1024)S(1)}, u32[]{:S(2)}) copy-start(f32[1152]{0:T(1024)S(1)} %convert_element_type.309) | copy-start | bytes 13828
  540.7 163.4 %copy-start.45 = (f32[1152]{0:T(1024)}, f32[1152]{0:T(1024)S(1)}, u32[]{:S(2)}) copy-start(f32[1152]{0:T(1024)S(1)} %convert_element_type.310) | copy-start | bytes 13828
  540.8 28.5 %copy-start.35 = (f32[8,184]{1,0:T(8,128)}, f32[8,184]{1,0:T(8,128)S(1)}, u32[]{:S(2)}) copy-start(f32[8,184]{1,0:T(8,128)S(1)} %dynamic-slice_convert_fusion) | copy-start | bytes 17668
  540.9 28.4 %copy-start.17 = (f32[1472]{0:T(1024)}, f32[1472]{0:T(1024)S(1)}, u32[]{:S(2)}) copy-start(f32[1472]{0:T(1024)S(1)} %convert_element_type.319) | copy-start | bytes 17668
  700.4 72.8 %copy-start.31 = (f32[1472]{0:T(1024)}, f32[1472]{0:T(1024)S(1)}, u32[]{:S(2)}) copy-start(f32[1472]{0:T(1024)S(1)} %broadcast_multiply_fusion) | copy-start | bytes 17668
  704.1 69.1 %copy-start.41 = (f32[1472]{0:T(1024)}, f32[1472]{0:T(1024)S(1)}, u32[]{:S(2)}) copy-start(f32[1472]{0:T(1024)S(1)} %fusion.48) | copy-start | bytes 17668
  773.3 6.9 copy-start.3
  773.3 6.9 copy-start.18
  783.4 5.8 copy-start.9
  1443.4 5.1 copy-start.6
  1443.4 136.5 %all-to-all-start.7 = ((bf16[8,1472,144]{2,0,1:T(8,128)(2,1)}), bf16[8,1472,144]{2,0,1:T(8,128)(2,1)}, u32[]{:S(2)}, u32[]{:S(2)}) async-start(bf16[8,1472,144]{2,0,1:T(8,128)(2,1)} %copy.134), calls=%async_computation.7 | async-start | bytes 12058624 | tf_op jit(solution)/shard_map/all_to_all | solution.py:301
  1448.4 584.9 %reduce-scatter.13.cloned.1.call-start = ((), (), s32[]{:S(2)}) async-start(), calls=%async_computation.23 | async-start | bytes 3317760 | tf_op jit(solution)/shard_map/reduce_scatter | solution.py:357
  1473.5 111.2 %copy-start.1 = (bf16[8,184,1152]{2,1,0:T(8,128)(2,1)S(1)}, bf16[8,184,1152]{2,1,0:T(8,128)(2,1)}, u32[]{:S(2)}) copy-start(bf16[8,184,1152]{2,1,0:T(8,128)(2,1)} %param.22) | copy-start | bytes 10174468
  1473.5 111.2 %copy-start.16 = (f32[1152]{0:T(1024)S(1)}, f32[1152]{0:T(1024)}, u32[]{:S(2)}) copy-start(f32[1152]{0:T(1024)} %copy-done.15) | copy-start | bytes 13828
  1473.5 111.2 %copy-start.21 = (f32[8,184]{1,0:T(8,128)S(1)}, f32[8,184]{1,0:T(8,128)}, u32[]{:S(2)}) copy-start(f32[8,184]{1,0:T(8,128)} %copy-done.20) | copy-start | bytes 17668
  1473.5 111.2 %copy-start.30 = (f32[1152]{0:T(1024)S(1)}, f32[1152]{0:T(1024)}, u32[]{:S(2)}) copy-start(f32[1152]{0:T(1024)} %copy-done.29) | copy-start | bytes 13828
  1473.5 111.2 %copy-start.38 = (f32[8,184]{1,0:T(8,128)S(1)}, f32[8,184]{1,0:T(8,128)}, u32[]{:S(2)}) copy-start(f32[8,184]{1,0:T(8,128)} %get-tuple-element.254) | copy-start | bytes 17668
  1579.9 136.4 %all-to-all-start.5 = ((bf16[8,1472,144]{2,0,1:T(8,128)(2,1)}), bf16[8,1472,144]{2,0,1:T(8,128)(2,1)}, u32[]{:S(2)}, u32[]{:S(2)}) async-start(bf16[8,1472,144]{2,0,1:T(8,128)(2,1)} %copy.128), calls=%async_computation.5 | async-start | bytes 12058624 | tf_op jit(solution)/shard_map/all_to_all | solution.py:299
  1584.7 448.7 %reduce-scatter.11.cloned.1.call-start = ((), (), s32[]{:S(2)}) async-start(), calls=%async_computation.22 | async-start | bytes 3317760 | tf_op jit(solution)/shard_map/reduce_scatter | solution.py:351
  1716.4 136.4 %all-to-all-start.6 = ((bf16[8,1472,144]{2,0,1:T(8,128)(2,1)}), bf16[8,1472,144]{2,0,1:T(8,128)(2,1)}, u32[]{:S(2)}, u32[]{:S(2)}) async-start(bf16[8,1472,144]{2,0,1:T(8,128)(2,1)} %copy.131), calls=%async_computation.6 | async-start | bytes 12058624 | tf_op jit(solution)/shard_map/all_to_all | solution.py:300
  1721.1 312.3 %reduce-scatter.7.cloned.1.call-start = ((), (), s32[]{:S(2)}) async-start(), calls=%async_computation.20 | async-start | bytes 3317760 | tf_op jit(solution)/shard_map/reduce_scatter | solution.py:342
  1750.2 283.2 %reduce-scatter.9.cloned.1.call-start = ((), (), s32[]{:S(2)}) async-start(), calls=%async_computation.21 | async-start | bytes 3317760 | tf_op jit(solution)/shard_map/reduce_scatter | solution.py:348
  1872.5 9.6 copy-start.32
  1872.5 9.6 copy-start.40
  1872.5 9.6 copy-start.42
  1872.5 9.6 copy-start.46
  1882.1 151.4 %reduce-scatter.15.cloned.1.call-start = ((), (), s32[]{:S(2)}) async-start(), calls=%async_computation.24 | async-start | bytes 12533760 | tf_op jit(solution)/shard_map/reduce_scatter | solution.py:242
  1906.6 179.5 %reduce-scatter.17.cloned.1.call-start = ((), (), s32[]{:S(2)}) async-start(), calls=%async_computation.25 | async-start | bytes 12533760 | tf_op jit(solution)/shard_map/reduce_scatter | solution.py:248
  1933.0 412.0 %all-reduce.24.cloned.1.call-start = ((), (), s32[]{:S(2)}) async-start(), calls=%async_computation.26 | async-start | bytes 15335424 | tf_op jit(solution)/shard_map/psum | solution.py:385
  1948.5 8.3 copy-start.8
  1948.5 8.3 copy-start.59
  1948.5 16.3 slice-start
  1956.8 8.0 slice-start.1
  1956.8 7.9 copy-start.7
  1956.8 7.9 copy-start.24
  1956.8 7.9 copy-start.26
  1964.8 14.9 copy-start.43
  1964.8 14.9 copy-start.44
  1964.8 14.9 copy-start.47
  1964.8 14.9 copy-start.48
  1964.8 68.5 %copy-start.34 = (f32[1472]{0:T(1024)S(1)}, f32[1472]{0:T(1024)}, u32[]{:S(2)}) copy-start(f32[1472]{0:T(1024)} %copy-done.33) | copy-start | bytes 17668
  2349.5 4.9 copy-start.12
  (19 other events, 66.1 us)
Sparse Core Ops, SparseCore 0:
  9.6 28.9 all-gather.6
  40.2 25.9 all-gather.8
  67.8 25.7 all-gather.10
  94.9 67.5 all-gather.16
  280.3 26.5 all-gather.12
  308.3 67.5 all-gather.14
  1456.6 35.6 reduce-scatter.12
  1616.6 35.6 reduce-scatter.10
  1750.4 35.6 reduce-scatter.6
  1882.2 33.3 reduce-scatter.8
  1918.2 83.0 reduce-scatter.14
  2003.8 82.3 reduce-scatter.16
  2091.4 253.5 all-reduce.23
where the time goes:
time: 2380 us; the launch traced here: 2360 us
  waiting for transfers between devices  895 us (38%)
  matrix products  702 us (29%)
  local copies, waits for them, and re-layouts  432 us (18%)
  blocking collectives  170 us (7%)
  other arithmetic  110 us (5%)
  starting transfers between devices  35.1 us (1%)
    psum x1, waiting for transfers between devices, body(): lax.psum(query_owned.astype(jnp.bfloat16), 'seq').astype(jnp.float32)  216 us
    dot_general x16, matrix products, attend_backward(): jnp.einsum('hqk,qhd->khd', score_grad, query_heads, preferred_element_typ...  120 us
    dot_general x16, matrix products, attend_backward(): jnp.einsum('hqk,khd->qhd', score_grad, key_heads, preferred_element_type=...  120 us
    all_to_all x1, blocking collectives, body(): lax.all_to_all(context_grad.reshape(row_groups, local_len, model_width),...  108 us
    all_to_all x1, waiting for transfers between devices, body(): lax.all_to_all(value_grad_h, 'seq', split_axis=1, concat_axis=2, tiled=True)  106 us
    dot_general x6, matrix products, matmul(): return jnp.dot(left_side, right_side, preferred_element_type=jnp.float32)  103 us
    all_to_all x1, waiting for transfers between devices, body(): lax.all_to_all(head_context, 'seq', split_axis=1, concat_axis=2, tiled=True)  103 us
    all_to_all x1, waiting for transfers between devices, body(): lax.all_to_all(key_grad_h, 'seq', split_axis=1, concat_axis=2, tiled=True)  102 us
  transfers between devices with their start and end apart: 20, of which 11 were waited for; matrix products, arithmetic and copies ran while one was open for 25% of the time, Pallas kernels for 0%

commit v1 on v0

v1 whole, which is shorter than its diff:
```python
import functools
import math

import jax
import jax.numpy as jnp
from jax import lax
from jax.experimental import pallas as pl
from jax.experimental.pallas import tpu as pltpu
from jax.sharding import PartitionSpec as P

HD = 72
SEQ = 736
EPS = 1e-06
SCALE = 1.0 / math.sqrt(HD)
SCALE_LOG2 = SCALE * math.log2(math.e)
QUERY_BLOCK = 736

f32 = jnp.float32
bf16 = jnp.bfloat16


def dot2(a, b, ca, cb):
    return lax.dot_general(a, b, (((ca,), (cb,)), ((), ())), preferred_element_type=f32)


def split3(v):
    high = v.astype(bf16).astype(f32)
    mid = (v - high).astype(bf16).astype(f32)
    return [high, mid, v - high - mid]


def rows8(rows, length):
    row = lax.broadcasted_iota(jnp.int32, (8, length), 0)
    out = jnp.zeros((8, length), f32)
    for j, value in enumerate(rows):
        out = jnp.where(row == j, value, out)
    return out


def query_blocks(length):
    return [(s, min(QUERY_BLOCK, length - s)) for s in range(0, length, QUERY_BLOCK)]


def attend_forward_kernel(q_ref, k_ref, v_ref, mask_ref, context_ref, lse_ref):
    length = q_ref.shape[-1]
    keys = k_ref[0].astype(f32)
    bias = jnp.where(mask_ref[0] > 0, 0.0, -1e30).astype(f32)
    one = jnp.ones((1, length), f32)
    zeros = jnp.zeros((8, length), f32)
    key_side = jnp.concatenate([keys, rows8([bias], length), keys, zeros], 0).T.astype(bf16)
    scaled = q_ref[0].astype(f32) * SCALE_LOG2
    high = scaled.astype(bf16).astype(f32)
    query_side = jnp.concatenate([high, rows8([one], length), scaled - high, zeros], 0).astype(bf16)
    value_side = jnp.concatenate([v_ref[0].astype(f32), jnp.ones((8, length), f32)], 0).astype(bf16)
    for s, n in query_blocks(length):
        scores = dot2(key_side, query_side[:, s : s + n], 1, 0)
        top = jnp.max(scores, 0, keepdims=True)
        probs = jnp.exp2(scores - top).astype(bf16)
        summed = dot2(value_side, probs, 1, 0)
        total = summed[HD : HD + 1]
        context_ref[0, :, s : s + n] = (summed[:HD] * (1.0 / total)).astype(bf16)
        lse_ref[0, 0, :, s : s + n] = top + jnp.log2(total)


def attend_forward(queries, keys, values, mask):
    images, width, length = queries.shape
    heads = width // HD
    block = pl.BlockSpec((1, HD, length), lambda i, h: (i, h, 0))
    return pl.pallas_call(
        attend_forward_kernel,
        grid=(images, heads),
        in_specs=[block, block, block, pl.BlockSpec((1, 1, length), lambda i, h: (i, 0, 0))],
        out_specs=[block, pl.BlockSpec((1, 1, 1, length), lambda i, h: (i, h, 0, 0))],
        out_shape=[
            jax.ShapeDtypeStruct((images, width, length), bf16),
            jax.ShapeDtypeStruct((images, heads, 1, length), f32),
        ],
        compiler_params=pltpu.CompilerParams(vmem_limit_bytes=50 << 20),
        cost_estimate=pl.CostEstimate(
            flops=images * heads * length * length * 1024,
            bytes_accessed=images * width * length * 8,
            transcendentals=images * heads * length * length,
        ),
        name="attend_forward",
    )(queries, keys, values, mask)


def attend_backward_kernel(
    q_ref, k_ref, v_ref, context_ref, grad_ref, lse_ref, mask_ref, dq_ref, dk_ref, dv_ref
):
    length = q_ref.shape[-1]
    key_low = k_ref[0]
    keys = key_low.astype(f32)
    bias = jnp.where(mask_ref[0] > 0, 0.0, -1e30).astype(f32)
    one = jnp.ones((1, length), f32)
    zeros = jnp.zeros((8, length), f32)
    key_side = jnp.concatenate(
        [keys, rows8([bias, one, one, one], length), keys, zeros], 0
    ).T.astype(bf16)
    queries = q_ref[0].astype(f32)
    scaled = queries * SCALE_LOG2
    high = scaled.astype(bf16).astype(f32)
    query_side = jnp.concatenate(
        [high, rows8([one] + split3(-lse_ref[0, 0]), length), scaled - high, zeros], 0
    ).astype(bf16)
    grads = grad_ref[0].astype(f32)
    row_dot = jnp.sum(grads * context_ref[0].astype(f32), 0, keepdims=True)
    grad_side = jnp.concatenate([grads, rows8(split3(-row_dot), length)], 0).astype(bf16)
    value_side = jnp.concatenate(
        [v_ref[0].astype(f32), rows8([one, one, one], length)], 0
    ).T.astype(bf16)
    query_rows = queries.T.astype(bf16)
    grad_rows = grads.T.astype(bf16)
    dk = jnp.zeros((length, HD), f32)
    dv = jnp.zeros((length, HD), f32)
    for s, n in query_blocks(length):
        probs = jnp.exp2(dot2(key_side, query_side[:, s : s + n], 1, 0))
        prob_grads = dot2(value_side, grad_side[:, s : s + n], 1, 0)
        score_grads = (probs * prob_grads).astype(bf16)
        dv += dot2(probs.astype(bf16), grad_rows[s : s + n], 1, 0)
        dk += dot2(score_grads, query_rows[s : s + n], 1, 0)
        dq_ref[0, :, s : s + n] = (dot2(key_low, score_grads, 1, 0) * SCALE).astype(bf16)
    dk_ref[0] = (dk * SCALE).T.astype(bf16)
    dv_ref[0] = dv.T.astype(bf16)


def attend_backward(queries, keys, values, context, grads, lse, mask):
    images, width, length = queries.shape
    heads = width // HD
    block = pl.BlockSpec((1, HD, length), lambda i, h: (i, h, 0))
    out = jax.ShapeDtypeStruct((images, width, length), bf16)
    return pl.pallas_call(
        attend_backward_kernel,
        grid=(images, heads),
        in_specs=[block] * 5
        + [
            pl.BlockSpec((1, 1, 1, length), lambda i, h: (i, h, 0, 0)),
            pl.BlockSpec((1, 1, length), lambda i, h: (i, 0, 0)),
        ],
        out_specs=[block] * 3,
        out_shape=[out, out, out],
        compiler_params=pltpu.CompilerParams(vmem_limit_bytes=50 << 20),
        cost_estimate=pl.CostEstimate(
            flops=images * heads * length * length * 2560,
            bytes_accessed=images * width * length * 16,
            transcendentals=images * heads * length * length,
        ),
        name="attend_backward",
    )(queries, keys, values, context, grads, lse, mask)


def swap(values, axis, bits):
    return lax.ppermute(values, axis, [(i, i ^ bits) for i in range(lax.axis_size(axis))])


def take_block(values, index, size):
    return lax.dynamic_slice_in_dim(values, index * size, size, 0)


def tokens_to_images(tokens, member, group):
    share = tokens.shape[0] // group
    blocks = [take_block(tokens, member ^ j, share) for j in range(group)]
    return jnp.concatenate(
        [blocks[0]] + [swap(blocks[j], "seq", j) for j in range(1, group)], axis=1
    )


def images_to_tokens(images, member, group):
    share, length, width = images.shape
    local = length // group
    out = jnp.zeros((share * group, local, width), images.dtype)
    for j in range(group):
        block = images[:, j * local : (j + 1) * local]
        if j:
            block = swap(block, "seq", j)
        out = lax.dynamic_update_slice_in_dim(out, block, (member ^ j) * share, 0)
    return out


def gather_small(local):
    me = lax.axis_index("fsdp")
    count = lax.axis_size("fsdp")
    held = local[None]
    bit = 1
    while bit < count:
        held = jnp.concatenate([held, swap(held, "fsdp", bit)], 0)
        bit *= 2
    return jnp.concatenate([take_block(held, me ^ j, 1) for j in range(count)], 0)


def sum_everywhere(values):
    for axis in ("fsdp", "seq"):
        bit = 1
        while bit < lax.axis_size(axis):
            values = values + swap(values, axis, bit)
            bit *= 2
    return values


def merge(mine, other, bit):
    return jnp.where(
        bit == 0, jnp.concatenate([mine, other], 0), jnp.concatenate([other, mine], 0)
    )


def sum_seq(values, order):
    me = lax.axis_index("seq")
    halved = []
    for step in order:
        rows = values.shape[0]
        bit = (me // step) % 2
        if rows % 16 == 0 and step != order[-1]:
            half = rows // 2
            sent = take_block(values, 1 - bit, half)
            kept = take_block(values, bit, half)
            halved.append((step, bit))
        else:
            sent = kept = values
        values = (kept.astype(f32) + swap(sent, "seq", step).astype(f32)).astype(bf16)
    for step, bit in reversed(halved):
        values = merge(values, swap(values, "seq", step), bit)
    return values


def seq_bits():
    bits, bit = [], 1
    while bit < lax.axis_size("seq"):
        bits.append(bit)
        bit *= 2
    return bits


def own_grad(full, order):
    mine = lax.psum_scatter(full.astype(bf16), "fsdp", scatter_dimension=0, tiled=True)
    return sum_seq(mine, order).astype(f32)


def norm_parts(values):
    center = values - jnp.mean(values, -1, keepdims=True)
    spread = jnp.mean(center * center, -1, keepdims=True)
    scale = lax.rsqrt(spread + EPS)
    return center * scale, scale


def norm_grad(grad, hat, scale, gain):
    e = grad * gain
    return scale * (
        e - jnp.mean(e, -1, keepdims=True) - hat * jnp.mean(e * hat, -1, keepdims=True)
    )


def ein(spec, a, b):
    return jnp.einsum(spec, a, b, preferred_element_type=f32)


def token_sum(values):
    return jnp.sum(values.astype(f32), (0, 1))


def body(
    patches,
    key_mask,
    attn_norm_gain,
    attn_norm_bias,
    query_weight,
    query_bias,
    key_weight,
    value_weight,
    value_bias,
    out_weight,
    out_bias,
    mlp_norm_gain,
    mlp_norm_bias,
    up_weight,
    up_bias,
    down_weight,
    down_bias,
    cotangent,
):
    rows, local, width = patches.shape
    group = SEQ // local
    share = rows // group
    shard = lax.axis_index("fsdp")
    seq = lax.axis_index("seq")
    member = seq % group
    bits = seq_bits()
    order_a = bits
    order_b = [bits[1], bits[0]] + bits[2:] if len(bits) > 1 else bits

    inputs_low = tokens_to_images(patches, member, group)

    small = [
        attn_norm_gain,
        attn_norm_bias,
        query_bias,
        value_bias,
        out_bias,
        mlp_norm_gain,
        mlp_norm_bias,
        down_bias,
        up_bias,
    ]
    gathered = gather_small(jnp.concatenate(small)).astype(f32)
    starts = [0]
    for v in small:
        starts.append(starts[-1] + v.shape[0])
    (
        first_gain,
        first_shift,
        query_shift,
        value_shift,
        out_shift,
        second_gain,
        second_shift,
        down_shift,
        up_shift,
    ) = (gathered[:, a:b].reshape(-1) for a, b in zip(starts[:-1], starts[1:]))

    def whole(weight):
        return lax.all_gather(weight, "fsdp", axis=0, tiled=True)

    query_full = whole(query_weight)
    key_full = whole(key_weight)
    value_full = whole(value_weight)
    out_full = whole(out_weight)
    up_full = whole(up_weight)
    down_full = whole(down_weight.T)

    cotangent_low = tokens_to_images(cotangent, member, group)
    image_mask = lax.dynamic_slice(
        key_mask, (member * share, (seq // group) * SEQ), (share, SEQ)
    )
    image_mask = jnp.concatenate(
        [
            lax.dynamic_slice_in_dim(image_mask, (member ^ j) * local, local, 1)
            for j in range(group)
        ],
        axis=1,
    )
    key_keep = image_mask[:, None, :]

    inputs = inputs_low.astype(f32)
    hat_one, _ = norm_parts(inputs)
    normed_one = (hat_one * first_gain + first_shift).astype(bf16)
    queries = (ein("itd,dn->int", normed_one, query_full) + query_shift[:, None]).astype(bf16)
    keys = ein("itd,dn->int", normed_one, key_full).astype(bf16)
    values = (ein("itd,dn->int", normed_one, value_full) + value_shift[:, None]).astype(bf16)
    context, lse = attend_forward(queries, keys, values, key_keep)
    hidden = inputs + ein("int,nd->itd", context, out_full) + out_shift
    hat_two, scale_two = norm_parts(hidden)
    normed_two = (hat_two * second_gain + second_shift).astype(bf16)
    pre = ein("itd,df->itf", normed_two, up_full) + up_shift
    tanh = jnp.tanh(math.sqrt(2 / math.pi) * (pre + 0.044715 * pre * pre * pre))
    active = (0.5 * pre * (1.0 + tanh)).astype(bf16)
    slope = (
        0.5 * (1.0 + tanh)
        + 0.5
        * pre
        * (1.0 - tanh * tanh)
        * (math.sqrt(2 / math.pi) * (1.0 + 3 * 0.044715 * pre * pre))
    ).astype(bf16)
    output = (hidden + ein("itf,df->itd", active, down_full) + down_shift).astype(bf16)
    output = images_to_tokens(output, member, group)

    out_grad_low = jnp.where(image_mask[:, :, None] > 0, cotangent_low, 0).astype(bf16)
    down_grad = ein("itd,itf->df", out_grad_low, active)
    down_bias_grad = token_sum(out_grad_low)
    down_owned = own_grad(down_grad, order_a).T
    pre_grad = (ein("itd,df->itf", out_grad_low, down_full) * slope.astype(f32)).astype(bf16)
    up_grad = ein("itd,itf->df", normed_two, pre_grad)
    up_bias_grad = token_sum(pre_grad)
    up_owned = own_grad(up_grad, order_b)
    normed_two_grad = ein("itf,df->itd", pre_grad, up_full)
    hidden_grad = out_grad_low.astype(f32) + norm_grad(
        normed_two_grad, hat_two, scale_two, second_gain
    )
    second_gain_grad = jnp.sum(normed_two_grad * hat_two, (0, 1))
    second_shift_grad = jnp.sum(normed_two_grad, (0, 1))

    attn_grad_low = hidden_grad.astype(bf16)
    context_grad = ein("itd,nd->int", attn_grad_low, out_full).astype(bf16)
    out_grad = ein("int,itd->nd", context, attn_grad_low)
    out_bias_grad = token_sum(attn_grad_low)
    out_owned = own_grad(out_grad, order_a)
    dq, dk, dv = attend_backward(queries, keys, values, context, context_grad, lse, key_keep)
    query_owned = own_grad(ein("itd,int->dn", normed_one, dq), order_b)
    key_owned = own_grad(ein("itd,int->dn", normed_one, dk), order_a)
    value_owned = own_grad(ein("itd,int->dn", normed_one, dv), order_b)
    query_bias_grad = jnp.sum(dq.astype(f32), (0, 2))
    value_bias_grad = jnp.sum(dv.astype(f32), (0, 2))
    normed_one_grad = (
        ein("int,dn->itd", dq, query_full)
        + ein("int,dn->itd", dk, key_full)
        + ein("int,dn->itd", dv, value_full)
    )
    hat_one, scale_one = norm_parts(inputs_low.astype(f32))
    first_gain_grad = jnp.sum(normed_one_grad * hat_one, (0, 1))
    first_shift_grad = jnp.sum(normed_one_grad, (0, 1))
    input_grad = (
        hidden_grad + norm_grad(normed_one_grad, hat_one, scale_one, first_gain)
    ).astype(bf16)
    input_grad = images_to_tokens(input_grad, member, group)

    small_grads = [
        first_gain_grad,
        first_shift_grad,
        query_bias_grad,
        value_bias_grad,
        out_bias_grad,
        second_gain_grad,
        second_shift_grad,
        down_bias_grad,
        up_bias_grad,
    ]
    count = lax.axis_size("fsdp")
    packed = jnp.concatenate([v.reshape(count, -1) for v in small_grads], 1)
    packed = take_block(sum_everywhere(packed), shard, 1)[0]
    (
        first_gain_owned,
        first_shift_owned,
        query_bias_owned,
        value_bias_owned,
        out_bias_owned,
        second_gain_owned,
        second_shift_owned,
        down_bias_owned,
        up_bias_owned,
    ) = (packed[a:b] for a, b in zip(starts[:-1], starts[1:]))
    return (
        output,
        input_grad,
        first_gain_owned,
        first_shift_owned,
        query_owned,
        query_bias_owned,
        key_owned,
        value_owned,
        value_bias_owned,
        out_owned,
        out_bias_owned,
        second_gain_owned,
        second_shift_owned,
        up_owned,
        up_bias_owned,
        down_owned,
        down_bias_owned,
    )


def solution(mesh):
    tokens, vector, matrix = P("fsdp", "seq", None), P("fsdp"), P("fsdp", None)
    in_specs = (
        tokens,
        matrix,
        vector,
        vector,
        matrix,
        vector,
        matrix,
        matrix,
        vector,
        matrix,
        vector,
        vector,
        vector,
        matrix,
        vector,
        P(None, "fsdp"),
        vector,
        tokens,
    )
    out_specs = (
        tokens,
        tokens,
        vector,
        vector,
        matrix,
        vector,
        matrix,
        matrix,
        vector,
        matrix,
        vector,
        vector,
        vector,
        matrix,
        vector,
        P(None, "fsdp"),
        vector,
    )
    return jax.shard_map(body, mesh=mesh, in_specs=in_specs, out_specs=out_specs, check_vma=False)
```

time: 2380 us -> 884 us (0.37)
  waiting for transfers between devices: 895 us -> 326 us
  matrix products: 702 us -> 275 us
  local copies, waits for them, and re-layouts: 432 us -> 57.9 us
  blocking collectives: 170 us -> 0 us
  Pallas kernels: 0 us -> 87.8 us
  other arithmetic: 110 us -> 51.2 us
  starting transfers between devices: 35.1 us -> 65.5 us
    all_to_all x7 -> x0, waiting for transfers between devices: 614 us -> none  [the longest x1 106 us: body(): lax.all_to_all(value_grad_h, 'seq', split_axis=1, concat_axis=2, tiled=True)]
    dot_general x130 -> x18, matrix products: 702 us -> 275 us  [ein(): return jnp.einsum(spec, a, b, preferred_element_type=f32)]
    ppermute x0 -> x49, waiting for transfers between devices: none -> 224 us  [swap(): lax.ppermute(values, axis, [(i, i ^ bits) for i in range(lax.axis_size(ax...]
    psum x1 -> x0, waiting for transfers between devices: 216 us -> none  [body(): lax.psum(query_owned.astype(jnp.bfloat16), 'seq').astype(jnp.float32)]
    reshape x21 -> x9, local copies, waits for them, and re-layouts: 161 us -> 7.51 us  [body(): packed = jnp.concatenate([v.reshape(count, -1) for v in small_grads], 1)]
    all_to_all x1 -> x0, blocking collectives: 108 us -> none  [body(): lax.all_to_all(context_grad.reshape(row_groups, local_len, model_width),...]
    pallas_call x0 -> x2, Pallas kernels: none -> 87.8 us  [the longest x1 53.9 us: attend_backward(): pl.pallas_call(attend_backward_kernel, grid=(images, heads), in_specs=[bl...]
    all_to_all x8 -> x0, local copies, waits for them, and re-layouts: 80 us -> none  [the longest x1 11.2 us: body(): lax.all_to_all(key_grad_h, 'seq', split_axis=1, concat_axis=2, tiled=True)]
  transfers between devices with their start and end apart: 20 -> 61, of which waited for: 11 -> 32; matrix products, arithmetic and copies ran while one was open for 25% -> 32% of each run, Pallas kernels for 0% -> 4%
where the time goes in v1:
time: 884 us; the launch traced here: 879 us
  waiting for transfers between devices  326 us (37%)
  matrix products  275 us (31%)
  Pallas kernels  87.8 us (10%)
  starting transfers between devices  65.5 us (7%)
  local copies, waits for them, and re-layouts  57.9 us (7%)
  other arithmetic  51.2 us (6%)
  between operations  15.6 us (2%)
    dot_general x18, matrix products, ein(): return jnp.einsum(spec, a, b, preferred_element_type=f32)  275 us
    ppermute x49, waiting for transfers between devices, swap(): lax.ppermute(values, axis, [(i, i ^ bits) for i in range(lax.axis_size(ax...  224 us
    all_gather x6, waiting for transfers between devices, whole(): return lax.all_gather(weight, 'fsdp', axis=0, tiled=True)  88.2 us
    ppermute x49, starting transfers between devices, swap(): lax.ppermute(values, axis, [(i, i ^ bits) for i in range(lax.axis_size(ax...  64.3 us
    pallas_call x1, Pallas kernels, attend_backward(): pl.pallas_call(attend_backward_kernel, grid=(images, heads), in_specs=[bl...  53.9 us
    pallas_call x1, Pallas kernels, attend_forward(): pl.pallas_call(attend_forward_kernel, grid=(images, heads), in_specs=[blo...  33.9 us
    dynamic_slice x15, local copies, waits for them, and re-layouts, take_block(): return lax.dynamic_slice_in_dim(values, index * size, size, 0)  18.3 us
  transfers between devices with their start and end apart: 61, of which 32 were waited for; matrix products, arithmetic and copies ran while one was open for 32% of the time, Pallas kernels for 4%

profile of v1, /device:TPU:0, one launch (start us, length us, event | category | flops | bytes accessed | tf_op | source)
XLA Modules:
  0.0 878.9 jit_solution(3983211453159452014)
XLA Ops:
  10.6 6.3 concatenate.102
  17.6 3.7 constant_dynamic-slice_fusion.23
  21.3 3.5 collective-permute-start.2
  25.4 3.7 constant_dynamic-slice_fusion.15
  29.1 2.9 collective-permute-start.10
  40.9 3.9 collective-permute-done.2
  46.6 16.7 %collective-permute-done.1 = bf16[2,184,1152]{2,1,0:T(8,128)(2,1)S(1)} collective-permute-done((bf16[2,184,1152]{2,1,0:T(8,128)(2,1)}, bf16[2,184,1152]{2,1,0:T(8,128)(2,1)S(1)}, u32[]{:S(2)}, u32[]{:S(2)}) %collective-permute-start.1) | collective-permute-done | bytes 847904 | tf_op jit(solution)/shard_map/ppermute | solution.py:153
  65.4 8.5 convolution_convert_fusion.1
  73.9 5.8 copy.49
  79.7 8.7 fusion.38.q_ref
  88.4 4.6 all-gather.11.cloned.1.call-done
  93.1 8.8 fusion.39.v_ref
  101.9 33.9 %attend_forward.1 = (bf16[2,1152,736]{2,1,0:T(8,128)(2,1)S(1)}, f32[2,16,1,736]{3,2,1,0:T(1,128)S(1)}) custom-call(bf16[2,1152,736]{2,1,0:T(8,128)(2,1)} %fusion.38.q_ref, bf16[2,1152,736]{2,1,0:T(8,128)(2,1)} %bitcast.83, bf16[2,1152,736]{2,1,0:T(8,128)(2,1)} %fusion.39.v_ref, s32[2,1,736]{2,1,0:T(1,128)S(1)} %broadcast_in_dim.17.mask_ref), custom_call_target="tpu_custom_call" | custom-call | flops 17750294528 | bytes 13565952 | tf_op jit(solution)/shard_map/attend_forward/pallas_call | solution.py:69
  136.4 9.5 %fusion.67 = (f32[2,736]{1,0:T(2,128)S(1)}, f32[2,736,1152]{2,1,0:T(8,128)S(1)}) fusion(f32[1152]{0:T(1024)S(1)} %add.350, bf16[2,1152,736]{2,1,0:T(8,128)(2,1)S(1)} %get-tuple-element.22.context_ref, bf16[1152,1152]{1,0:T(8,128)(2,1)} %all-gather.13.cloned.1.call-done, bf16[2,184,1152]{2,1,0:T(8,128)(2,1)} %copy-done.11, ...), kind=kOutput, calls=%fused_computation.179 | convolution fusion | flops 3925645824 | bytes 16230656 | tf_op jit(solution)/shard_map/int,nd->itd/dot_general | solution.py:253
  146.0 2.7 copy-done.6
  149.6 39.7 %all-gather.15.cloned.1.call-done = bf16[1152,4304]{1,0:T(8,128)(2,1)} async-done(((bf16[288,4304]{1,0:T(8,128)(2,1)}), bf16[1152,4304]{1,0:T(8,128)(2,1)}) %all-gather.15.cloned.1.call-update) | async-done | bytes 9916432 | tf_op jit(solution)/shard_map/all_gather | solution.py:320
  189.3 25.1 %fusion.14 = f32[2,736,4304]{2,1,0:T(8,128)} fusion(bf16[1152,4304]{1,0:T(8,128)(2,1)} %all-gather.15.cloned.1.call-done, f32[2,736,1152]{2,1,0:T(8,128)} %copy-done.6, f32[1152]{0:T(1024)S(1)} %copy-done.43, f32[1152]{0:T(1024)S(1)} %copy-done.34, f32[2,736]{1,0:T(2,128)S(1)} %add_rsqrt_fusion, f32[2,736]{1,0:T(2,128)S(1)} %broadcast_multiply_fusion.4), kind=kOutput, calls=%fused_computation.24 | convolution fusion | flops 14605443072 | bytes 42062336 | tf_op jit(solution)/shard_map/itd,df->itf/dot_general | solution.py:253
  214.5 43.9 %all-gather.17.cloned.1.call-done = bf16[1152,4304]{1,0:T(8,128)(2,1)} async-done(((bf16[288,4304]{1,0:T(8,128)(2,1)}), bf16[1152,4304]{1,0:T(8,128)(2,1)}) %all-gather.17.cloned.1.call-update) | async-done | bytes 9916432 | tf_op jit(solution)/shard_map/all_gather | solution.py:320
  258.4 38.3 %convert_reduce_fusion = (f32[4304]{0:T(1024)}, bf16[2,736,4304]{2,1,0:T(8,128)(2,1)}) fusion(f32[2,736,4304]{2,1,0:T(8,128)} %fusion.14, f32[4304]{0:T(1024)S(1)} %copy-done.41, bf16[1152,4304]{1,0:T(8,128)(2,1)} %all-gather.17.cloned.1.call-done, bf16[2,184,1152]{2,1,0:T(8,128)(2,1)} %collective-permute-done.10, ...), kind=kOutput, calls=%fused_computation.9 | convolution fusion | flops 14764273664 | bytes 51356736 | tf_op jit(solution)/shard_map/itd,df->itf/dot_general | solution.py:253
  296.6 26.3 %multiply_reduce_fusion = (f32[1152]{0:T(1024)}, f32[2,736]{1,0:T(2,128)S(1)}, f32[2,736]{1,0:T(2,128)S(1)}, f32[1152]{0:T(1024)}, f32[2,736,1152]{2,1,0:T(8,128)}) fusion(f32[2,736,1152]{2,1,0:T(8,128)} %copy-done.6, f32[2,736]{1,0:T(2,128)S(1)} %add_rsqrt_fusion, f32[2,736]{1,0:T(2,128)S(1)} %broadcast_multiply_fusion.4, f32[1152]{0:T(1024)S(1)} %copy-done.34, ...), kind=kOutput, calls=%fused_computation.56 | convolution fusion | flops 14612221952 | bytes 36190720 | tf_op jit(solution)/shard_map/itf,df->itd/dot_general | solution.py:253
  322.9 9.1 %convert_reduce_fusion.5 = (f32[1152]{0:T(1024)}, f32[2,736,1152]{2,1,0:T(8,128)S(1)}, f32[1152]{0:T(1024)}) fusion(f32[2,736]{1,0:T(2,128)S(1)} %get-tuple-element.86, f32[2,736,1152]{2,1,0:T(8,128)} %copy-done.6, f32[2,736]{1,0:T(2,128)S(1)} %broadcast_multiply_fusion.4, f32[2,736]{1,0:T(2,128)S(1)} %get-tuple-element.87, ...), kind=kLoop, calls=%fused_computation.57 | loop fusion | flops 37304064 | bytes 23779264 | tf_op jit(solution)/shard_map/reduce_sum | solution.py:257
  332.0 2.8 copy-done.5
  334.8 5.3 convolution_convert_fusion
  340.1 3.6 copy.53
  344.7 53.9 %attend_backward.1 = (bf16[2,1152,736]{2,1,0:T(8,128)(2,1)S(1)}, bf16[2,1152,736]{2,1,0:T(8,128)(2,1)}, bf16[2,1152,736]{2,1,0:T(8,128)(2,1)}) custom-call(bf16[2,1152,736]{2,1,0:T(8,128)(2,1)} %fusion.38.q_ref, bf16[2,1152,736]{2,1,0:T(8,128)(2,1)} %bitcast.84, bf16[2,1152,736]{2,1,0:T(8,128)(2,1)} %fusion.39.v_ref, bf16[2,1152,736]{2,1,0:T(8,128)(2,1)} %copy-done.2, ...), custom_call_target="tpu_custom_call" | custom-call | flops 44375736320 | bytes 27131904 | tf_op jit(solution)/shard_map/attend_backward/pallas_call | solution.py:132
  398.6 7.1 fusion.22
  406.0 10.0 %fusion.23 = bf16[1152,1152]{1,0:T(8,128)(2,1)} fusion(bf16[2,1152,736]{2,1,0:T(8,128)(2,1)} %get-tuple-element.25, f32[1152]{0:T(1024)} %copy-done.44, f32[1152]{0:T(1024)} %copy-done.31, f32[2,736]{1,0:T(2,128)} %copy-done.35, f32[2,736]{1,0:T(2,128)S(1)} %copy-done.30, bf16[2,184,1152]{2,1,0:T(8,128)(2,1)} %copy-done.11, ...), kind=kOutput, calls=%fused_computation.39 | convolution fusion | flops 3930365952 | bytes 9458176 | tf_op jit(solution)/shard_map/itd,int->dn/dot_general | solution.py:253
  416.1 10.0 %fusion.24 = bf16[1152,1152]{1,0:T(8,128)(2,1)} fusion(bf16[2,1152,736]{2,1,0:T(8,128)(2,1)} %get-tuple-element.26, f32[1152]{0:T(1024)} %copy-done.44, f32[1152]{0:T(1024)} %copy-done.31, f32[2,736]{1,0:T(2,128)} %copy-done.35, f32[2,736]{1,0:T(2,128)S(1)} %copy-done.30, bf16[2,184,1152]{2,1,0:T(8,128)(2,1)} %copy-done.11, ...), kind=kOutput, calls=%fused_computation.40 | convolution fusion | flops 3930365952 | bytes 9458176 | tf_op jit(solution)/shard_map/itd,int->dn/dot_general | solution.py:253
  426.5 10.3 %fusion.25 = bf16[1152,1152]{1,0:T(8,128)(2,1)} fusion(bf16[2,1152,736]{2,1,0:T(8,128)(2,1)} %copy-done.2, f32[2,736,1152]{2,1,0:T(8,128)} %copy-done.5), kind=kOutput, calls=%fused_computation.41 | convolution fusion | flops 3910017024 | bytes 12828672 | tf_op jit(solution)/shard_map/int,itd->nd/dot_general | solution.py:253
  436.9 24.0 %fusion.7 = bf16[1152,4304]{1,0:T(8,128)(2,1)} fusion(bf16[2,736,4304]{2,1,0:T(8,128)(2,1)} %get-tuple-element.85, f32[2,736,1152]{2,1,0:T(8,128)} %copy-done.6, f32[1152]{0:T(1024)} %add.354, f32[1152]{0:T(1024)} %mul.246, f32[2,736]{1,0:T(2,128)} %copy-done.39, f32[2,736]{1,0:T(2,128)S(1)} %broadcast_multiply_fusion.4), kind=kOutput, calls=%fused_computation.14 | convolution fusion | flops 14610401280 | bytes 29391360 | tf_op jit(solution)/shard_map/itd,itf->df/dot_general | solution.py:253
  462.3 8.9 %fusion.47 = f32[2,736,1152]{2,1,0:T(8,128)} fusion(bf16[2,1152,736]{2,1,0:T(8,128)(2,1)S(1)} %get-tuple-element.24, bf16[1152,1152]{1,0:T(8,128)(2,1)} %all-gather.7.cloned.1.call-done), kind=kOutput, calls=%fused_computation.80 | convolution fusion | flops 3906994176 | bytes 12828672 | tf_op jit(solution)/shard_map/int,dn->itd/dot_general | solution.py:253
  471.3 7.2 fusion.44
  478.5 14.8 %fusion.33 = (f32[1152]{0:T(1024)}, f32[2,736]{1,0:T(2,128)}, f32[2,736]{1,0:T(2,128)}, f32[1152]{0:T(1024)}, f32[2,736,1152]{2,1,0:T(8,128)}) fusion(f32[2,736]{1,0:T(2,128)S(1)} %copy-done.37, f32[2,736]{1,0:T(2,128)S(1)} %copy-done.30, bf16[2,184,1152]{2,1,0:T(8,128)(2,1)S(1)} %copy-done.13, bf16[2,184,1152]{2,1,0:T(8,128)(2,1)S(1)} %copy-done.17, ...), kind=kOutput, calls=%fused_computation.53 | convolution fusion | flops 3939208192 | bytes 29823488 | tf_op jit(solution)/shard_map/int,dn->itd/dot_general | solution.py:253
  496.1 26.1 %fusion.8 = bf16[1152,4304]{1,0:T(8,128)(2,1)} fusion(bf16[2,184,1152]{2,1,0:T(8,128)(2,1)} %collective-permute-done.10, bf16[2,184,1152]{2,1,0:T(8,128)(2,1)} %collective-permute-done.9, bf16[2,184,1152]{2,1,0:T(8,128)(2,1)} %collective-permute-done.8, bf16[2,184,1152]{2,1,0:T(8,128)(2,1)} %get-tuple-element.52, pred[2,736]{1,0:T(4,128)(4,1)} %get-tuple-element.45, ...), kind=kOutput, calls=%fused_computation.15 | convolution fusion | flops 14680539136 | bytes 38668544 | tf_op jit(solution)/shard_map/itd,itf->df/dot_general | solution.py:253
  524.2 2.6 convert_reduce_fusion.3
  532.0 26.0 %add_convert_fusion.2 = bf16[2,736,1152]{2,1,0:T(8,128)(2,1)S(1)} fusion(f32[2,736,1152]{2,1,0:T(8,128)} %copy-done.6, bf16[1152,4304]{1,0:T(8,128)(2,1)} %all-gather.17.cloned.1.call-done, f32[1152]{0:T(1024)} %add.363, f32[2,736,4304]{2,1,0:T(8,128)} %fusion.14, f32[4304]{0:T(1024)} %add.357), kind=kOutput, calls=%fused_computation.60 | convolution fusion | flops 14665406464 | bytes 45454656 | tf_op jit(solution)/shard_map/itf,df->itd/dot_general | solution.py:253
  563.7 2.8 collective-permute-done.15
  568.1 13.8 %collective-permute-done.16 = f32[4,3380]{1,0:T(4,128)S(1)} collective-permute-done((f32[4,3380]{1,0:T(4,128)S(1)}, f32[4,3380]{1,0:T(4,128)S(1)}, u32[]{:S(2)}, u32[]{:S(2)}) %collective-permute-start.16) | collective-permute-done | bytes 54112 | tf_op jit(solution)/shard_map/ppermute | solution.py:153
  583.6 8.0 fusion.32
  591.6 8.8 %collective-permute-done.17 = f32[4,3380]{1,0:T(4,128)S(1)} collective-permute-done((f32[4,3380]{1,0:T(4,128)S(1)}, f32[4,3380]{1,0:T(4,128)S(1)}, u32[]{:S(2)}, u32[]{:S(2)}) %collective-permute-start.17) | collective-permute-done | bytes 54112 | tf_op jit(solution)/shard_map/ppermute | solution.py:153
  600.4 2.5 collective-permute-start.18
  609.2 15.7 %collective-permute-done.11 = bf16[2,184,1152]{2,1,0:T(8,128)(2,1)S(1)} collective-permute-done((bf16[2,184,1152]{2,1,0:T(8,128)(2,1)S(1)}, bf16[2,184,1152]{2,1,0:T(8,128)(2,1)S(1)}, u32[]{:S(2)}, u32[]{:S(2)}) %collective-permute-start.11) | collective-permute-done | bytes 847904 | tf_op jit(solution)/shard_map/ppermute | solution.py:153
  627.4 15.2 %collective-permute-done.13 = bf16[2,184,1152]{2,1,0:T(8,128)(2,1)S(1)} collective-permute-done((bf16[2,184,1152]{2,1,0:T(8,128)(2,1)S(1)}, bf16[2,184,1152]{2,1,0:T(8,128)(2,1)S(1)}, u32[]{:S(2)}, u32[]{:S(2)}) %collective-permute-start.13) | collective-permute-done | bytes 847904 | tf_op jit(solution)/shard_map/ppermute | solution.py:153
  655.0 2.4 collective-permute-start.20
  667.7 3.1 collective-permute-start.21
  670.9 3.0 collective-permute-start.31
  673.9 3.5 collective-permute-start.36
  677.4 9.4 %collective-permute-done.21 = bf16[72,1152]{1,0:T(8,128)(2,1)S(1)} collective-permute-done((bf16[72,1152]{1,0:T(8,128)(2,1)S(1)}, bf16[72,1152]{1,0:T(8,128)(2,1)S(1)}, u32[]{:S(2)}, u32[]{:S(2)}) %collective-permute-start.21) | collective-permute-done | bytes 165920 | tf_op jit(solution)/shard_map/ppermute | solution.py:153
  687.6 2.9 collective-permute-done.26
  690.6 2.8 collective-permute-done.31
  700.4 2.4 constant_dynamic-slice_fusion.3
  710.5 2.5 fusion.51
  712.9 10.7 %reduce-scatter.17.cloned.1.call-done = bf16[288,4304]{1,0:T(8,128)(2,1)} async-done(((bf16[1152,4304]{1,0:T(8,128)(2,1)}), bf16[288,4304]{1,0:T(8,128)(2,1)}) %reduce-scatter.17.cloned.1.call-update) | async-done | bytes 2479120 | tf_op jit(solution)/shard_map/reduce_scatter | solution.py:234
  726.7 10.6 %collective-permute-done.39 = bf16[144,4304]{1,0:T(8,128)(2,1)} collective-permute-done((bf16[144,4304]{1,0:T(8,128)(2,1)}, bf16[144,4304]{1,0:T(8,128)(2,1)}, u32[]{:S(2)}, u32[]{:S(2)}) %collective-permute-start.39) | collective-permute-done | bytes 1239584 | tf_op jit(solution)/shard_map/ppermute | solution.py:153
  740.4 15.3 %collective-permute-done.44 = bf16[144,4304]{1,0:T(8,128)(2,1)S(1)} collective-permute-done((bf16[144,4304]{1,0:T(8,128)(2,1)S(1)}, bf16[144,4304]{1,0:T(8,128)(2,1)S(1)}, u32[]{:S(2)}, u32[]{:S(2)}) %collective-permute-start.44) | collective-permute-done | bytes 1239584 | tf_op jit(solution)/shard_map/ppermute | solution.py:153
  757.6 10.4 %collective-permute-done.40 = bf16[72,4304]{1,0:T(8,128)(2,1)S(1)} collective-permute-done((bf16[72,4304]{1,0:T(8,128)(2,1)S(1)}, bf16[72,4304]{1,0:T(8,128)(2,1)S(1)}, u32[]{:S(2)}, u32[]{:S(2)}) %collective-permute-start.40) | collective-permute-done | bytes 619808 | tf_op jit(solution)/shard_map/ppermute | solution.py:153
  768.1 2.5 collective-permute-start.41
  772.7 39.5 %collective-permute-done.41 = bf16[72,4304]{1,0:T(8,128)(2,1)S(1)} collective-permute-done((bf16[72,4304]{1,0:T(8,128)(2,1)S(1)}, bf16[72,4304]{1,0:T(8,128)(2,1)S(1)}, u32[]{:S(2)}, u32[]{:S(2)}) %collective-permute-start.41) | collective-permute-done | bytes 619808 | tf_op jit(solution)/shard_map/ppermute | solution.py:153
  814.0 10.4 %collective-permute-done.46 = bf16[72,4304]{1,0:T(8,128)(2,1)S(1)} collective-permute-done((bf16[72,4304]{1,0:T(8,128)(2,1)S(1)}, bf16[72,4304]{1,0:T(8,128)(2,1)S(1)}, u32[]{:S(2)}, u32[]{:S(2)}) %collective-permute-start.46) | collective-permute-done | bytes 619808 | tf_op jit(solution)/shard_map/ppermute | solution.py:153
  828.0 2.5 fusion.52
  830.5 11.2 %collective-permute-done.47 = bf16[72,4304]{1,0:T(8,128)(2,1)S(1)} collective-permute-done((bf16[72,4304]{1,0:T(8,128)(2,1)S(1)}, bf16[72,4304]{1,0:T(8,128)(2,1)S(1)}, u32[]{:S(2)}, u32[]{:S(2)}) %collective-permute-start.47) | collective-permute-done | bytes 619808 | tf_op jit(solution)/shard_map/ppermute | solution.py:153
  845.7 20.6 %collective-permute-done.43 = bf16[144,4304]{1,0:T(8,128)(2,1)S(1)} collective-permute-done((bf16[144,4304]{1,0:T(8,128)(2,1)S(1)}, bf16[144,4304]{1,0:T(8,128)(2,1)S(1)}, u32[]{:S(2)}, u32[]{:S(2)}) %collective-permute-start.43) | collective-permute-done | bytes 1239584 | tf_op jit(solution)/shard_map/ppermute | solution.py:153
  866.3 2.7 fusion.50
  869.1 2.7 convert_bitcast_fusion
  (299 shorter events, 107.4 us)
Async XLA Ops:
  7.2 58.2 %all-gather.9.cloned.1.call-start = ((), (), s32[]{:S(2)}) async-start(), calls=%async_computation.7 | async-start | bytes 3317760 | tf_op jit(solution)/shard_map/all_gather | solution.py:320
  7.9 71.8 %all-gather.7.cloned.1.call-start = ((), (), s32[]{:S(2)}) async-start(), calls=%async_computation.6 | async-start | bytes 3317760 | tf_op jit(solution)/shard_map/all_gather | solution.py:320
  8.7 84.4 %all-gather.11.cloned.1.call-start = ((), (), s32[]{:S(2)}) async-start(), calls=%async_computation.8 | async-start | bytes 3317760 | tf_op jit(solution)/shard_map/all_gather | solution.py:320
  9.4 127.0 %all-gather.13.cloned.1.call-start = ((), (), s32[]{:S(2)}) async-start(), calls=%async_computation.9 | async-start | bytes 3317760 | tf_op jit(solution)/shard_map/all_gather | solution.py:320
  10.0 179.3 %all-gather.15.cloned.1.call-start = ((), (), s32[]{:S(2)}) async-start(), calls=%async_computation.10 | async-start | bytes 12533760 | tf_op jit(solution)/shard_map/all_gather | solution.py:320
  10.6 247.8 %all-gather.17.cloned.1.call-start = ((), (), s32[]{:S(2)}) async-start(), calls=%async_computation.11 | async-start | bytes 12533760 | tf_op jit(solution)/shard_map/all_gather | solution.py:320
  16.9 16.0 %collective-permute-start.3 = (bf16[1,3380]{1,0:T(2,128)(2,1)S(1)}, bf16[1,3380]{1,0:T(2,128)(2,1)S(1)}, u32[]{:S(2)}, u32[]{:S(2)}) collective-permute-start(bf16[1,3380]{1,0:T(2,128)(2,1)S(1)} %broadcast_in_dim.16), channel_id=1, source_target_pairs={{0,1},{1,0},{2,3},{3,2},{4,5},{5,4},{6,7},{7,6},{8,9},{9,8},{10,11... | collective-permute-start | bytes 20288 | tf_op jit(solution)/shard_map/ppermute | solution.py:153
  17.5 625.3 %reduce-scatter.7.cloned.1.call-start = ((), (), s32[]{:S(2)}) async-start(), calls=%async_computation.12 | async-start | bytes 3317760 | tf_op jit(solution)/shard_map/reduce_scatter | solution.py:234
  21.3 23.5 %collective-permute-start.2 = (bf16[2,184,1152]{2,1,0:T(8,128)(2,1)}, bf16[2,184,1152]{2,1,0:T(8,128)(2,1)S(1)}, u32[]{:S(2)}, u32[]{:S(2)}) collective-permute-start(bf16[2,184,1152]{2,1,0:T(8,128)(2,1)} %get-tuple-element.62), channel_id=1, source_target_pairs={{0,12},{4,8},{8,4},{12,0},{16,28},{20,24},{24,20},{28,16},{1,13},{... | collective-permute-start | bytes 2543624 | tf_op jit(solution)/shard_map/ppermute | solution.py:153
  24.8 38.5 %collective-permute-start.1 = (bf16[2,184,1152]{2,1,0:T(8,128)(2,1)}, bf16[2,184,1152]{2,1,0:T(8,128)(2,1)S(1)}, u32[]{:S(2)}, u32[]{:S(2)}) collective-permute-start(bf16[2,184,1152]{2,1,0:T(8,128)(2,1)} %get-tuple-element.63), channel_id=1, source_target_pairs={{0,8},{4,12},{8,0},{12,4},{16,24},{20,28},{24,16},{28,20},{1,9},{5... | collective-permute-start | bytes 2543624 | tf_op jit(solution)/shard_map/ppermute | solution.py:153
  25.3 38.1 %collective-permute-start = (bf16[2,184,1152]{2,1,0:T(8,128)(2,1)}, bf16[2,184,1152]{2,1,0:T(8,128)(2,1)S(1)}, u32[]{:S(2)}, u32[]{:S(2)}) collective-permute-start(bf16[2,184,1152]{2,1,0:T(8,128)(2,1)} %get-tuple-element.61), channel_id=1, source_target_pairs={{0,4},{4,0},{8,12},{12,8},{16,20},{20,16},{24,28},{28,24},{1,5},{5... | collective-permute-start | bytes 2543624 | tf_op jit(solution)/shard_map/ppermute | solution.py:153
  29.1 185.4 %collective-permute-start.10 = (bf16[2,184,1152]{2,1,0:T(8,128)(2,1)}, bf16[2,184,1152]{2,1,0:T(8,128)(2,1)}, u32[]{:S(2)}, u32[]{:S(2)}) collective-permute-start(bf16[2,184,1152]{2,1,0:T(8,128)(2,1)} %get-tuple-element.54), channel_id=1, source_target_pairs={{0,12},{4,8},{8,4},{12,0},{16,28},{20,24},{24,20},{28,16},{1,13},{... | collective-permute-start | bytes 2543624 | tf_op jit(solution)/shard_map/ppermute | solution.py:153
  33.0 3.8 collective-permute-start.4
  36.8 177.7 %collective-permute-start.9 = (bf16[2,184,1152]{2,1,0:T(8,128)(2,1)}, bf16[2,184,1152]{2,1,0:T(8,128)(2,1)}, u32[]{:S(2)}, u32[]{:S(2)}) collective-permute-start(bf16[2,184,1152]{2,1,0:T(8,128)(2,1)} %get-tuple-element.55), channel_id=1, source_target_pairs={{0,8},{4,12},{8,0},{12,4},{16,24},{20,28},{24,16},{28,20},{1,9},{5... | collective-permute-start | bytes 2543624 | tf_op jit(solution)/shard_map/ppermute | solution.py:153
  44.8 169.7 %collective-permute-start.8 = (bf16[2,184,1152]{2,1,0:T(8,128)(2,1)}, bf16[2,184,1152]{2,1,0:T(8,128)(2,1)}, u32[]{:S(2)}, u32[]{:S(2)}) collective-permute-start(bf16[2,184,1152]{2,1,0:T(8,128)(2,1)} %get-tuple-element.53), channel_id=1, source_target_pairs={{0,4},{4,0},{8,12},{12,8},{16,20},{20,16},{24,28},{28,24},{1,5},{5... | collective-permute-start | bytes 2543624 | tf_op jit(solution)/shard_map/ppermute | solution.py:153
  149.6 173.3 %copy-start.39 = (f32[2,736]{1,0:T(2,128)}, f32[2,736]{1,0:T(2,128)S(1)}, u32[]{:S(2)}) copy-start(f32[2,736]{1,0:T(2,128)S(1)} %add_rsqrt_fusion) | copy-start | bytes 17668
  149.6 108.7 %copy-start.26 = (bf16[2,184,1152]{2,1,0:T(8,128)(2,1)S(1)}, bf16[2,184,1152]{2,1,0:T(8,128)(2,1)}, u32[]{:S(2)}) copy-start(bf16[2,184,1152]{2,1,0:T(8,128)(2,1)} %get-tuple-element.52) | copy-start | bytes 2543620
  149.6 108.7 %copy-start.41 = (f32[4304]{0:T(1024)S(1)}, f32[4304]{0:T(1024)}, u32[]{:S(2)}) copy-start(f32[4304]{0:T(1024)} %add.357) | copy-start | bytes 51652
  405.7 240.5 %reduce-scatter.9.cloned.1.call-start = ((), (), s32[]{:S(2)}) async-start(), calls=%async_computation.13 | async-start | bytes 3317760 | tf_op jit(solution)/shard_map/reduce_scatter | solution.py:234
  416.0 233.4 %reduce-scatter.11.cloned.1.call-start = ((), (), s32[]{:S(2)}) async-start(), calls=%async_computation.14 | async-start | bytes 3317760 | tf_op jit(solution)/shard_map/reduce_scatter | solution.py:234
  426.1 225.6 %reduce-scatter.13.cloned.1.call-start = ((), (), s32[]{:S(2)}) async-start(), calls=%async_computation.15 | async-start | bytes 3317760 | tf_op jit(solution)/shard_map/reduce_scatter | solution.py:234
  436.8 263.6 %reduce-scatter.15.cloned.1.call-start = ((), (), s32[]{:S(2)}) async-start(), calls=%async_computation.16 | async-start | bytes 12533760 | tf_op jit(solution)/shard_map/reduce_scatter | solution.py:234
  460.9 262.7 %reduce-scatter.17.cloned.1.call-start = ((), (), s32[]{:S(2)}) async-start(), calls=%async_computation.17 | async-start | bytes 12533760 | tf_op jit(solution)/shard_map/reduce_scatter | solution.py:234
  531.7 30.6 %collective-permute-start.14 = (f32[4,3380]{1,0:T(4,128)S(1)}, f32[4,3380]{1,0:T(4,128)S(1)}, u32[]{:S(2)}, u32[]{:S(2)}) collective-permute-start(f32[4,3380]{1,0:T(4,128)S(1)} %concatenate.108), channel_id=1, source_target_pairs={{0,1},{1,0},{2,3},{3,2},{4,5},{5,4},{6,7},{7,6},{8,9},{9,8},{10,11... | collective-permute-start | bytes 162248 | tf_op jit(solution)/shard_map/ppermute | solution.py:153
  558.7 49.7 %collective-permute-start.5 = (bf16[2,184,1152]{2,1,0:T(8,128)(2,1)S(1)}, bf16[2,184,1152]{2,1,0:T(8,128)(2,1)S(1)}, u32[]{:S(2)}, u32[]{:S(2)}) collective-permute-start(bf16[2,184,1152]{2,1,0:T(8,128)(2,1)S(1)} %get-tuple-element.58), channel_id=1, source_target_pairs={{0,4},{4,0},{8,12},{12,8},{16,20},{20,16},{24,28},{28,24},{1,5},{5... | collective-permute-start | bytes 2543624 | tf_op jit(solution)/shard_map/ppermute | solution.py:153
  560.3 48.6 %collective-permute-start.6 = (bf16[2,184,1152]{2,1,0:T(8,128)(2,1)S(1)}, bf16[2,184,1152]{2,1,0:T(8,128)(2,1)S(1)}, u32[]{:S(2)}, u32[]{:S(2)}) collective-permute-start(bf16[2,184,1152]{2,1,0:T(8,128)(2,1)S(1)} %get-tuple-element.57), channel_id=1, source_target_pairs={{0,8},{4,12},{8,0},{12,4},{16,24},{20,28},{24,16},{28,20},{1,9},{5... | collective-permute-start | bytes 2543624 | tf_op jit(solution)/shard_map/ppermute | solution.py:153
  561.8 47.3 %collective-permute-start.7 = (bf16[2,184,1152]{2,1,0:T(8,128)(2,1)S(1)}, bf16[2,184,1152]{2,1,0:T(8,128)(2,1)S(1)}, u32[]{:S(2)}, u32[]{:S(2)}) collective-permute-start(bf16[2,184,1152]{2,1,0:T(8,128)(2,1)S(1)} %get-tuple-element.56), channel_id=1, source_target_pairs={{0,12},{4,8},{8,4},{12,0},{16,28},{20,24},{24,20},{28,16},{1,13},{... | collective-permute-start | bytes 2543624 | tf_op jit(solution)/shard_map/ppermute | solution.py:153
  562.2 4.2 collective-permute-start.15
  566.5 15.4 %collective-permute-start.16 = (f32[4,3380]{1,0:T(4,128)S(1)}, f32[4,3380]{1,0:T(4,128)S(1)}, u32[]{:S(2)}, u32[]{:S(2)}) collective-permute-start(f32[4,3380]{1,0:T(4,128)S(1)} %add.373), channel_id=1, source_target_pairs={{0,4},{4,0},{8,12},{12,8},{16,20},{20,16},{24,28},{28,24},{1,5},{5... | collective-permute-start | bytes 162248 | tf_op jit(solution)/shard_map/ppermute | solution.py:153
  581.9 18.4 %collective-permute-start.17 = (f32[4,3380]{1,0:T(4,128)S(1)}, f32[4,3380]{1,0:T(4,128)S(1)}, u32[]{:S(2)}, u32[]{:S(2)}) collective-permute-start(f32[4,3380]{1,0:T(4,128)S(1)} %add.374), channel_id=1, source_target_pairs={{0,8},{4,12},{8,0},{12,4},{16,24},{20,28},{24,16},{28,20},{1,9},{5... | collective-permute-start | bytes 162248 | tf_op jit(solution)/shard_map/ppermute | solution.py:153
  600.4 5.1 collective-permute-start.18
  603.5 21.4 %collective-permute-start.11 = (bf16[2,184,1152]{2,1,0:T(8,128)(2,1)S(1)}, bf16[2,184,1152]{2,1,0:T(8,128)(2,1)S(1)}, u32[]{:S(2)}, u32[]{:S(2)}) collective-permute-start(bf16[2,184,1152]{2,1,0:T(8,128)(2,1)S(1)} %get-tuple-element.50), channel_id=1, source_target_pairs={{0,4},{4,0},{8,12},{12,8},{16,20},{20,16},{24,28},{28,24},{1,5},{5... | collective-permute-start | bytes 2543624 | tf_op jit(solution)/shard_map/ppermute | solution.py:153
  605.5 21.8 %collective-permute-start.12 = (bf16[2,184,1152]{2,1,0:T(8,128)(2,1)S(1)}, bf16[2,184,1152]{2,1,0:T(8,128)(2,1)S(1)}, u32[]{:S(2)}, u32[]{:S(2)}) collective-permute-start(bf16[2,184,1152]{2,1,0:T(8,128)(2,1)S(1)} %get-tuple-element.49), channel_id=1, source_target_pairs={{0,8},{4,12},{8,0},{12,4},{16,24},{20,28},{24,16},{28,20},{1,9},{5... | collective-permute-start | bytes 2543624 | tf_op jit(solution)/shard_map/ppermute | solution.py:153
  608.3 34.3 %collective-permute-start.13 = (bf16[2,184,1152]{2,1,0:T(8,128)(2,1)S(1)}, bf16[2,184,1152]{2,1,0:T(8,128)(2,1)S(1)}, u32[]{:S(2)}, u32[]{:S(2)}) collective-permute-start(bf16[2,184,1152]{2,1,0:T(8,128)(2,1)S(1)} %get-tuple-element.48), channel_id=1, source_target_pairs={{0,12},{4,8},{8,4},{12,0},{16,28},{20,24},{24,20},{28,16},{1,13},{... | collective-permute-start | bytes 2543624 | tf_op jit(solution)/shard_map/ppermute | solution.py:153
  644.8 8.9 %collective-permute-start.19 = (bf16[144,1152]{1,0:T(8,128)(2,1)}, bf16[144,1152]{1,0:T(8,128)(2,1)}, u32[]{:S(2)}, u32[]{:S(2)}) collective-permute-start(bf16[144,1152]{1,0:T(8,128)(2,1)} %constant_dynamic-slice_fusion.11), channel_id=1, source_target_pairs={{0,8},{4,12},{8,0},{12,4},{16,24},{20,28},{24,16},{28,20},{1,9},{5... | collective-permute-start | bytes 995336 | tf_op jit(solution)/shard_map/ppermute | solution.py:153
  648.0 11.0 %collective-permute-start.24 = (bf16[144,1152]{1,0:T(8,128)(2,1)}, bf16[144,1152]{1,0:T(8,128)(2,1)}, u32[]{:S(2)}, u32[]{:S(2)}) collective-permute-start(bf16[144,1152]{1,0:T(8,128)(2,1)} %constant_dynamic-slice_fusion.9), channel_id=1, source_target_pairs={{0,4},{4,0},{8,12},{12,8},{16,20},{20,16},{24,28},{28,24},{1,5},{5... | collective-permute-start | bytes 995336 | tf_op jit(solution)/shard_map/ppermute | solution.py:153
  651.2 9.8 %collective-permute-start.29 = (bf16[144,1152]{1,0:T(8,128)(2,1)}, bf16[144,1152]{1,0:T(8,128)(2,1)}, u32[]{:S(2)}, u32[]{:S(2)}) collective-permute-start(bf16[144,1152]{1,0:T(8,128)(2,1)} %constant_dynamic-slice_fusion.7), channel_id=1, source_target_pairs={{0,8},{4,12},{8,0},{12,4},{16,24},{20,28},{24,16},{28,20},{1,9},{5... | collective-permute-start | bytes 995336 | tf_op jit(solution)/shard_map/ppermute | solution.py:153
  652.7 13.1 %collective-permute-start.34 = (bf16[144,1152]{1,0:T(8,128)(2,1)S(1)}, bf16[144,1152]{1,0:T(8,128)(2,1)S(1)}, u32[]{:S(2)}, u32[]{:S(2)}) collective-permute-start(bf16[144,1152]{1,0:T(8,128)(2,1)S(1)} %constant_dynamic-slice_fusion.5), channel_id=1, source_target_pairs={{0,4},{4,0},{8,12},{12,8},{16,20},{20,16},{24,28},{28,24},{1,5},{5... | collective-permute-start | bytes 995336 | tf_op jit(solution)/shard_map/ppermute | solution.py:153
  655.0 12.7 %collective-permute-start.20 = (bf16[72,1152]{1,0:T(8,128)(2,1)S(1)}, bf16[72,1152]{1,0:T(8,128)(2,1)S(1)}, u32[]{:S(2)}, u32[]{:S(2)}) collective-permute-start(bf16[72,1152]{1,0:T(8,128)(2,1)S(1)} %constant_dynamic-slice_fusion.10), channel_id=1, source_target_pairs={{0,4},{4,0},{8,12},{12,8},{16,20},{20,16},{24,28},{28,24},{1,5},{5... | collective-permute-start | bytes 497672 | tf_op jit(solution)/shard_map/ppermute | solution.py:153
  660.2 10.5 %collective-permute-start.25 = (bf16[72,1152]{1,0:T(8,128)(2,1)S(1)}, bf16[72,1152]{1,0:T(8,128)(2,1)S(1)}, u32[]{:S(2)}, u32[]{:S(2)}) collective-permute-start(bf16[72,1152]{1,0:T(8,128)(2,1)S(1)} %constant_dynamic-slice_fusion.8), channel_id=1, source_target_pairs={{0,8},{4,12},{8,0},{12,4},{16,24},{20,28},{24,16},{28,20},{1,9},{5... | collective-permute-start | bytes 497672 | tf_op jit(solution)/shard_map/ppermute | solution.py:153
  662.3 8.6 collective-permute-start.30
  667.0 6.9 collective-permute-start.35
  667.7 19.2 %collective-permute-start.21 = (bf16[72,1152]{1,0:T(8,128)(2,1)S(1)}, bf16[72,1152]{1,0:T(8,128)(2,1)S(1)}, u32[]{:S(2)}, u32[]{:S(2)}) collective-permute-start(bf16[72,1152]{1,0:T(8,128)(2,1)S(1)} %add_convert_fusion.21), channel_id=1, source_target_pairs={{0,16},{4,20},{8,24},{12,28},{16,0},{20,4},{24,8},{28,12},{1,17},{... | collective-permute-start | bytes 497672 | tf_op jit(solution)/shard_map/ppermute | solution.py:153
  670.8 19.7 %collective-permute-start.26 = (bf16[72,1152]{1,0:T(8,128)(2,1)S(1)}, bf16[72,1152]{1,0:T(8,128)(2,1)S(1)}, u32[]{:S(2)}, u32[]{:S(2)}) collective-permute-start(bf16[72,1152]{1,0:T(8,128)(2,1)S(1)} %add_convert_fusion.19), channel_id=1, source_target_pairs={{0,16},{4,20},{8,24},{12,28},{16,0},{20,4},{24,8},{28,12},{1,17},{... | collective-permute-start | bytes 497672 | tf_op jit(solution)/shard_map/ppermute | solution.py:153
  670.9 22.4 %collective-permute-start.31 = (bf16[72,1152]{1,0:T(8,128)(2,1)S(1)}, bf16[72,1152]{1,0:T(8,128)(2,1)S(1)}, u32[]{:S(2)}, u32[]{:S(2)}) collective-permute-start(bf16[72,1152]{1,0:T(8,128)(2,1)S(1)} %add_convert_fusion.17), channel_id=1, source_target_pairs={{0,16},{4,20},{8,24},{12,28},{16,0},{20,4},{24,8},{28,12},{1,17},{... | collective-permute-start | bytes 497672 | tf_op jit(solution)/shard_map/ppermute | solution.py:153
  673.9 21.2 %collective-permute-start.36 = (bf16[72,1152]{1,0:T(8,128)(2,1)S(1)}, bf16[72,1152]{1,0:T(8,128)(2,1)S(1)}, u32[]{:S(2)}, u32[]{:S(2)}) collective-permute-start(bf16[72,1152]{1,0:T(8,128)(2,1)S(1)} %add_convert_fusion.15), channel_id=1, source_target_pairs={{0,16},{4,20},{8,24},{12,28},{16,0},{20,4},{24,8},{28,12},{1,17},{... | collective-permute-start | bytes 497672 | tf_op jit(solution)/shard_map/ppermute | solution.py:153
  686.9 9.2 %collective-permute-start.22 = (bf16[72,1152]{1,0:T(8,128)(2,1)S(1)}, bf16[72,1152]{1,0:T(8,128)(2,1)S(1)}, u32[]{:S(2)}, u32[]{:S(2)}) collective-permute-start(bf16[72,1152]{1,0:T(8,128)(2,1)S(1)} %add_convert_fusion.20), channel_id=1, source_target_pairs={{0,4},{4,0},{8,12},{12,8},{16,20},{20,16},{24,28},{28,24},{1,5},{5... | collective-permute-start | bytes 497672 | tf_op jit(solution)/shard_map/ppermute | solution.py:153
  690.5 8.2 collective-permute-start.27
  694.1 9.0 %collective-permute-start.32 = (bf16[72,1152]{1,0:T(8,128)(2,1)}, bf16[72,1152]{1,0:T(8,128)(2,1)}, u32[]{:S(2)}, u32[]{:S(2)}) collective-permute-start(bf16[72,1152]{1,0:T(8,128)(2,1)} %add_convert_fusion.16), channel_id=1, source_target_pairs={{0,4},{4,0},{8,12},{12,8},{16,20},{20,16},{24,28},{28,24},{1,5},{5... | collective-permute-start | bytes 497672 | tf_op jit(solution)/shard_map/ppermute | solution.py:153
  695.9 10.3 %collective-permute-start.37 = (bf16[72,1152]{1,0:T(8,128)(2,1)}, bf16[72,1152]{1,0:T(8,128)(2,1)}, u32[]{:S(2)}, u32[]{:S(2)}) collective-permute-start(bf16[72,1152]{1,0:T(8,128)(2,1)} %add_convert_fusion.14), channel_id=1, source_target_pairs={{0,8},{4,12},{8,0},{12,4},{16,24},{20,28},{24,16},{28,20},{1,9},{5... | collective-permute-start | bytes 497672 | tf_op jit(solution)/shard_map/ppermute | solution.py:153
  696.9 13.6 %collective-permute-start.23 = (bf16[144,1152]{1,0:T(8,128)(2,1)}, bf16[144,1152]{1,0:T(8,128)(2,1)}, u32[]{:S(2)}, u32[]{:S(2)}) collective-permute-start(bf16[144,1152]{1,0:T(8,128)(2,1)} %maximum_select_fusion.9), channel_id=1, source_target_pairs={{0,8},{4,12},{8,0},{12,4},{16,24},{20,28},{24,16},{28,20},{1,9},{5... | collective-permute-start | bytes 995336 | tf_op jit(solution)/shard_map/ppermute | solution.py:153
  699.5 128.5 %collective-permute-start.28 = (bf16[144,1152]{1,0:T(8,128)(2,1)}, bf16[144,1152]{1,0:T(8,128)(2,1)}, u32[]{:S(2)}, u32[]{:S(2)}) collective-permute-start(bf16[144,1152]{1,0:T(8,128)(2,1)} %maximum_select_fusion.10), channel_id=1, source_target_pairs={{0,4},{4,0},{8,12},{12,8},{16,20},{20,16},{24,28},{28,24},{1,5},{5... | collective-permute-start | bytes 995336 | tf_op jit(solution)/shard_map/ppermute | solution.py:153
  702.8 34.5 %collective-permute-start.39 = (bf16[144,4304]{1,0:T(8,128)(2,1)}, bf16[144,4304]{1,0:T(8,128)(2,1)}, u32[]{:S(2)}, u32[]{:S(2)}) collective-permute-start(bf16[144,4304]{1,0:T(8,128)(2,1)} %constant_dynamic-slice_fusion.3), channel_id=1, source_target_pairs={{0,8},{4,12},{8,0},{12,4},{16,24},{20,28},{24,16},{28,20},{1,9},{5... | collective-permute-start | bytes 3718664 | tf_op jit(solution)/shard_map/ppermute | solution.py:153
  704.3 139.1 %collective-permute-start.33 = (bf16[144,1152]{1,0:T(8,128)(2,1)S(1)}, bf16[144,1152]{1,0:T(8,128)(2,1)S(1)}, u32[]{:S(2)}, u32[]{:S(2)}) collective-permute-start(bf16[144,1152]{1,0:T(8,128)(2,1)S(1)} %maximum_select_fusion.11), channel_id=1, source_target_pairs={{0,8},{4,12},{8,0},{12,4},{16,24},{20,28},{24,16},{28,20},{1,9},{5... | collective-permute-start | bytes 995336 | tf_op jit(solution)/shard_map/ppermute | solution.py:153
  707.4 137.1 %collective-permute-start.38 = (bf16[144,1152]{1,0:T(8,128)(2,1)S(1)}, bf16[144,1152]{1,0:T(8,128)(2,1)S(1)}, u32[]{:S(2)}, u32[]{:S(2)}) collective-permute-start(bf16[144,1152]{1,0:T(8,128)(2,1)S(1)} %maximum_select_fusion.12), channel_id=1, source_target_pairs={{0,4},{4,0},{8,12},{12,8},{16,20},{20,16},{24,28},{28,24},{1,5},{5... | collective-permute-start | bytes 995336 | tf_op jit(solution)/shard_map/ppermute | solution.py:153
  725.2 30.5 %collective-permute-start.44 = (bf16[144,4304]{1,0:T(8,128)(2,1)S(1)}, bf16[144,4304]{1,0:T(8,128)(2,1)S(1)}, u32[]{:S(2)}, u32[]{:S(2)}) collective-permute-start(bf16[144,4304]{1,0:T(8,128)(2,1)S(1)} %constant_dynamic-slice_fusion.1), channel_id=1, source_target_pairs={{0,4},{4,0},{8,12},{12,8},{16,20},{20,16},{24,28},{28,24},{1,5},{5... | collective-permute-start | bytes 3718664 | tf_op jit(solution)/shard_map/ppermute | solution.py:153
  739.3 28.6 %collective-permute-start.40 = (bf16[72,4304]{1,0:T(8,128)(2,1)S(1)}, bf16[72,4304]{1,0:T(8,128)(2,1)S(1)}, u32[]{:S(2)}, u32[]{:S(2)}) collective-permute-start(bf16[72,4304]{1,0:T(8,128)(2,1)S(1)} %constant_dynamic-slice_fusion.2), channel_id=1, source_target_pairs={{0,4},{4,0},{8,12},{12,8},{16,20},{20,16},{24,28},{28,24},{1,5},{5... | collective-permute-start | bytes 1859336 | tf_op jit(solution)/shard_map/ppermute | solution.py:153
  756.0 14.6 %collective-permute-start.45 = (bf16[72,4304]{1,0:T(8,128)(2,1)S(1)}, bf16[72,4304]{1,0:T(8,128)(2,1)S(1)}, u32[]{:S(2)}, u32[]{:S(2)}) collective-permute-start(bf16[72,4304]{1,0:T(8,128)(2,1)S(1)} %constant_dynamic-slice_fusion), channel_id=1, source_target_pairs={{0,8},{4,12},{8,0},{12,4},{16,24},{20,28},{24,16},{28,20},{1,9},{5... | collective-permute-start | bytes 1859336 | tf_op jit(solution)/shard_map/ppermute | solution.py:153
  768.1 44.1 %collective-permute-start.41 = (bf16[72,4304]{1,0:T(8,128)(2,1)S(1)}, bf16[72,4304]{1,0:T(8,128)(2,1)S(1)}, u32[]{:S(2)}, u32[]{:S(2)}) collective-permute-start(bf16[72,4304]{1,0:T(8,128)(2,1)S(1)} %add_convert_fusion.9), channel_id=1, source_target_pairs={{0,16},{4,20},{8,24},{12,28},{16,0},{20,4},{24,8},{28,12},{1,17},{... | collective-permute-start | bytes 1859336 | tf_op jit(solution)/shard_map/ppermute | solution.py:153
  770.7 53.6 %collective-permute-start.46 = (bf16[72,4304]{1,0:T(8,128)(2,1)S(1)}, bf16[72,4304]{1,0:T(8,128)(2,1)S(1)}, u32[]{:S(2)}, u32[]{:S(2)}) collective-permute-start(bf16[72,4304]{1,0:T(8,128)(2,1)S(1)} %add_convert_fusion.7), channel_id=1, source_target_pairs={{0,16},{4,20},{8,24},{12,28},{16,0},{20,4},{24,8},{28,12},{1,17},{... | collective-permute-start | bytes 1859336 | tf_op jit(solution)/shard_map/ppermute | solution.py:153
  812.4 13.6 %collective-permute-start.42 = (bf16[72,4304]{1,0:T(8,128)(2,1)S(1)}, bf16[72,4304]{1,0:T(8,128)(2,1)S(1)}, u32[]{:S(2)}, u32[]{:S(2)}) collective-permute-start(bf16[72,4304]{1,0:T(8,128)(2,1)S(1)} %add_convert_fusion.8), channel_id=1, source_target_pairs={{0,4},{4,0},{8,12},{12,8},{16,20},{20,16},{24,28},{28,24},{1,5},{5... | collective-permute-start | bytes 1859336 | tf_op jit(solution)/shard_map/ppermute | solution.py:153
  824.6 17.1 %collective-permute-start.47 = (bf16[72,4304]{1,0:T(8,128)(2,1)S(1)}, bf16[72,4304]{1,0:T(8,128)(2,1)S(1)}, u32[]{:S(2)}, u32[]{:S(2)}) collective-permute-start(bf16[72,4304]{1,0:T(8,128)(2,1)S(1)} %add_convert_fusion.6), channel_id=1, source_target_pairs={{0,8},{4,12},{8,0},{12,4},{16,24},{20,28},{24,16},{28,20},{1,9},{5... | collective-permute-start | bytes 1859336 | tf_op jit(solution)/shard_map/ppermute | solution.py:153
  826.3 40.1 %collective-permute-start.43 = (bf16[144,4304]{1,0:T(8,128)(2,1)S(1)}, bf16[144,4304]{1,0:T(8,128)(2,1)S(1)}, u32[]{:S(2)}, u32[]{:S(2)}) collective-permute-start(bf16[144,4304]{1,0:T(8,128)(2,1)S(1)} %maximum_select_fusion.3), channel_id=1, source_target_pairs={{0,8},{4,12},{8,0},{12,4},{16,24},{20,28},{24,16},{28,20},{1,9},{5... | collective-permute-start | bytes 3718664 | tf_op jit(solution)/shard_map/ppermute | solution.py:153
  841.9 27.2 %collective-permute-start.48 = (bf16[144,4304]{1,0:T(8,128)(2,1)S(1)}, bf16[144,4304]{1,0:T(8,128)(2,1)S(1)}, u32[]{:S(2)}, u32[]{:S(2)}) collective-permute-start(bf16[144,4304]{1,0:T(8,128)(2,1)S(1)} %maximum_select_fusion.4), channel_id=1, source_target_pairs={{0,4},{4,0},{8,12},{12,8},{16,20},{20,16},{24,28},{28,24},{1,5},{5... | collective-permute-start | bytes 3718664 | tf_op jit(solution)/shard_map/ppermute | solution.py:153
  (48 other events, 1400.8 us)
Sparse Core Ops, SparseCore 0:
  9.6 28.6 all-gather.8
  39.8 25.8 all-gather.6
  67.3 25.7 all-gather.10
  94.5 25.7 all-gather.12
  121.7 67.6 all-gather.14
  190.7 67.5 all-gather.16
  405.8 34.8 reduce-scatter.6
  444.1 34.8 reduce-scatter.8
  481.5 34.8 reduce-scatter.10
  519.0 34.8 reduce-scatter.12
  556.5 82.2 reduce-scatter.14
  641.3 82.2 reduce-scatter.16

commit v2 on v1

--- a/solution.py
+++ b/solution.py
@@ -1,10 +1,10 @@
-import functools
 import math
 
 import jax
 import jax.numpy as jnp
 from jax import lax
 from jax.experimental import pallas as pl
+from jax.experimental.layout import Layout, with_layout_constraint
 from jax.experimental.pallas import tpu as pltpu
 from jax.sharding import PartitionSpec as P
 
@@ -14,6 +14,10 @@
 SCALE = 1.0 / math.sqrt(HD)
 SCALE_LOG2 = SCALE * math.log2(math.e)
 QUERY_BLOCK = 736
+HEAD_GROUPS = ((0, 8), (8, 8))
+
+GELU_A = math.sqrt(2 / math.pi)
+GELU_B = 0.044715 * GELU_A
 
 f32 = jnp.float32
 bf16 = jnp.bfloat16
@@ -62,14 +66,19 @@
         lse_ref[0, 0, :, s : s + n] = top + jnp.log2(total)
 
 
-def attend_forward(queries, keys, values, mask):
-    images, width, length = queries.shape
+def attend_forward(projected, mask):
+    images, features, length = projected.shape
+    width = features // 3
     heads = width // HD
     block = pl.BlockSpec((1, HD, length), lambda i, h: (i, h, 0))
+    sources = [
+        pl.BlockSpec((1, HD, length), lambda i, h, which=which: (i, which * heads + h, 0))
+        for which in range(3)
+    ]
     return pl.pallas_call(
         attend_forward_kernel,
         grid=(images, heads),
-        in_specs=[block, block, block, pl.BlockSpec((1, 1, length), lambda i, h: (i, 0, 0))],
+        in_specs=sources + [pl.BlockSpec((1, 1, length), lambda i, h: (i, 0, 0))],
         out_specs=[block, pl.BlockSpec((1, 1, 1, length), lambda i, h: (i, h, 0, 0))],
         out_shape=[
             jax.ShapeDtypeStruct((images, width, length), bf16),
@@ -82,12 +91,20 @@
             transcendentals=images * heads * length * length,
         ),
         name="attend_forward",
-    )(queries, keys, values, mask)
+    )(projected, projected, projected, mask)
 
 
 def attend_backward_kernel(
-    q_ref, k_ref, v_ref, context_ref, grad_ref, lse_ref, mask_ref, dq_ref, dk_ref, dv_ref
+    q_ref,
+    k_ref,
+    v_ref,
+    context_ref,
+    grad_ref,
+    lse_ref,
+    mask_ref,
+    *rest,
 ):
+    all_ref, out_ref = rest[-2:]
     length = q_ref.shape[-1]
     key_low = k_ref[0]
     keys = key_low.astype(f32)
@@ -119,34 +136,52 @@
         score_grads = (probs * prob_grads).astype(bf16)
         dv += dot2(probs.astype(bf16), grad_rows[s : s + n], 1, 0)
         dk += dot2(score_grads, query_rows[s : s + n], 1, 0)
-        dq_ref[0, :, s : s + n] = (dot2(key_low, score_grads, 1, 0) * SCALE).astype(bf16)
-    dk_ref[0] = (dk * SCALE).T.astype(bf16)
-    dv_ref[0] = dv.T.astype(bf16)
-
-
-def attend_backward(queries, keys, values, context, grads, lse, mask):
-    images, width, length = queries.shape
-    heads = width // HD
-    block = pl.BlockSpec((1, HD, length), lambda i, h: (i, h, 0))
-    out = jax.ShapeDtypeStruct((images, width, length), bf16)
-    return pl.pallas_call(
+        dq = (dot2(key_low, score_grads, 1, 0) * SCALE).astype(bf16)
+        out_ref[0, 0, :, s : s + n] = dq
+        all_ref[0, 0, :, s : s + n] = dq
+    for which, value in ((1, (dk * SCALE).T.astype(bf16)), (2, dv.T.astype(bf16))):
+        out_ref[0, which] = value
+        all_ref[0, which] = value
+
+
+def attend_backward(projected, context, grads, lse, mask, first, count, held=None):
+    images, features, length = projected.shape
+    heads = features // (3 * HD)
+    block = pl.BlockSpec((1, HD, length), lambda i, h: (i, first + h, 0))
+    sources = [
+        pl.BlockSpec((1, HD, length), lambda i, h, which=which: (i, which * heads + first + h, 0))
+        for which in range(3)
+    ]
+    earlier = [] if held is None else [held]
+    whole, part = pl.pallas_call(
         attend_backward_kernel,
-        grid=(images, heads),
-        in_specs=[block] * 5
+        grid=(images, count),
+        in_specs=sources
         + [
-            pl.BlockSpec((1, 1, 1, length), lambda i, h: (i, h, 0, 0)),
+            block,
+            block,
+            pl.BlockSpec((1, 1, 1, length), lambda i, h: (i, first + h, 0, 0)),
             pl.BlockSpec((1, 1, length), lambda i, h: (i, 0, 0)),
+        ]
+        + [pl.BlockSpec(memory_space=pl.ANY)] * len(earlier),
+        out_specs=[
+            pl.BlockSpec((1, 3, HD, length), lambda i, h: (i, 0, first + h, 0)),
+            pl.BlockSpec((1, 3, HD, length), lambda i, h: (i, 0, h, 0)),
         ],
-        out_specs=[block] * 3,
-        out_shape=[out, out, out],
+        out_shape=[
+            jax.ShapeDtypeStruct((images, 3, heads * HD, length), bf16),
+            jax.ShapeDtypeStruct((images, 3, count * HD, length), bf16),
+        ],
+        input_output_aliases={7: 0} if earlier else {},
         compiler_params=pltpu.CompilerParams(vmem_limit_bytes=50 << 20),
         cost_estimate=pl.CostEstimate(
-            flops=images * heads * length * length * 2560,
-            bytes_accessed=images * width * length * 16,
-            transcendentals=images * heads * length * length,
+            flops=images * count * length * length * 2560,
+            bytes_accessed=images * count * HD * length * 16,
+            transcendentals=images * count * length * length,
         ),
         name="attend_backward",
-    )(queries, keys, values, context, grads, lse, mask)
+    )(projected, projected, projected, context, grads, lse, mask, *earlier)
+    return whole, part.reshape(images, 3 * count * HD, length)
 
 
 def swap(values, axis, bits):
@@ -188,11 +223,12 @@
     return jnp.concatenate([take_block(held, me ^ j, 1) for j in range(count)], 0)
 
 
-def sum_everywhere(values):
+def sum_chain(values):
     for axis in ("fsdp", "seq"):
         bit = 1
         while bit < lax.axis_size(axis):
-            values = values + swap(values, axis, bit)
+            values, came = yield (values, swap(values, axis, bit))
+            values = values + came
             bit *= 2
     return values
 
@@ -203,23 +239,66 @@
     )
 
 
-def sum_seq(values, order):
+def rows_first(values):
+    return with_layout_constraint(values, Layout((0, 1)))
+
+
+def reduce_chain(full, *orders):
+    (values,) = yield (lax.psum_scatter(full, "fsdp", scatter_dimension=0, tiled=True),)
     me = lax.axis_index("seq")
+    rows, width = values.shape
+    cut = -(-width // (128 * len(orders))) * 128
+    parts = [values[:, p * cut : min((p + 1) * cut, width)] for p in range(len(orders))]
+    steps = len(orders[0])
     halved = []
-    for step in order:
-        rows = values.shape[0]
-        bit = (me // step) % 2
-        if rows % 16 == 0 and step != order[-1]:
-            half = rows // 2
-            sent = take_block(values, 1 - bit, half)
-            kept = take_block(values, bit, half)
-            halved.append((step, bit))
-        else:
-            sent = kept = values
-        values = (kept.astype(f32) + swap(sent, "seq", step).astype(f32)).astype(bf16)
-    for step, bit in reversed(halved):
-        values = merge(values, swap(values, "seq", step), bit)
-    return values
+    for k in range(steps):
+        halve = rows % 16 == 0 and k < steps - 1
+        flight = []
+        for part, order in zip(parts, orders):
+            sent = kept = part
+            if halve:
+                bit = (me // order[k]) % 2
+                sent, kept = (take_block(part, b, rows // 2) for b in (1 - bit, bit))
+            flight.append((kept, swap(sent, "seq", order[k])))
+        flight = yield flight
+        parts = [(kept.astype(f32) + came.astype(f32)).astype(bf16) for kept, came in flight]
+        if halve:
+            rows //= 2
+            halved.append(k)
+    for k in reversed(halved):
+        flight = yield [
+            (part, swap(part, "seq", order[k])) for part, order in zip(parts, orders)
+        ]
+        parts = [
+            merge(part, came, (me // order[k]) % 2) for (part, came), order in zip(flight, orders)
+        ]
+    return jnp.concatenate(parts, 1)
+
+
+class Flow:
+    def __init__(self):
+        self.chains, self.pending, self.results = {}, {}, {}
+
+    def start(self, name, chain):
+        self.chains[name], self.pending[name] = chain, next(chain)
+
+    def point(self, main, *names):
+        names = [name for name in names if name in self.pending]
+        main, ended = lax.optimization_barrier((main, [self.pending[n] for n in names]))
+        for name, values in zip(names, ended):
+            self.advance(name, values)
+        return main
+
+    def advance(self, name, values):
+        try:
+            self.pending[name] = self.chains[name].send(values)
+        except StopIteration as end:
+            self.results[name] = end.value
+            del self.pending[name]
+
+    def finish(self):
+        while self.pending:
+            self.point((), *self.pending)
 
 
 def seq_bits():
@@ -230,9 +309,14 @@
     return bits
 
 
-def own_grad(full, order):
-    mine = lax.psum_scatter(full.astype(bf16), "fsdp", scatter_dimension=0, tiled=True)
-    return sum_seq(mine, order).astype(f32)
+def ungroup(parts, which):
+    return jnp.concatenate(
+        [
+            part[..., which * heads * HD : (which + 1) * heads * HD]
+            for part, (_, heads) in zip(parts, HEAD_GROUPS)
+        ],
+        -1,
+    )
 
 
 def norm_parts(values):
@@ -319,14 +403,12 @@
     def whole(weight):
         return lax.all_gather(weight, "fsdp", axis=0, tiled=True)
 
-    query_full = whole(query_weight)
-    key_full = whole(key_weight)
-    value_full = whole(value_weight)
+    project_full = whole(jnp.concatenate([query_weight, key_weight, value_weight], 1))
+    project_shift = jnp.concatenate([query_shift, jnp.zeros_like(query_shift), value_shift])
     out_full = whole(out_weight)
     up_full = whole(up_weight)
     down_full = whole(down_weight.T)
 
-    cotangent_low = tokens_to_images(cotangent, member, group)
     image_mask = lax.dynamic_slice(
         key_mask, (member * share, (seq // group) * SEQ), (share, SEQ)
     )
@@ -342,65 +424,81 @@
     inputs = inputs_low.astype(f32)
     hat_one, _ = norm_parts(inputs)
     normed_one = (hat_one * first_gain + first_shift).astype(bf16)
-    queries = (ein("itd,dn->int", normed_one, query_full) + query_shift[:, None]).astype(bf16)
-    keys = ein("itd,dn->int", normed_one, key_full).astype(bf16)
-    values = (ein("itd,dn->int", normed_one, value_full) + value_shift[:, None]).astype(bf16)
-    context, lse = attend_forward(queries, keys, values, key_keep)
+    projected = (ein("itd,dm->imt", normed_one, project_full) + project_shift[:, None]).astype(
+        bf16
+    )
+    projected, cotangent = lax.optimization_barrier((projected, cotangent))
+    cotangent_low = tokens_to_images(cotangent, member, group)
+    context, lse = attend_forward(projected, key_keep)
     hidden = inputs + ein("int,nd->itd", context, out_full) + out_shift
     hat_two, scale_two = norm_parts(hidden)
     normed_two = (hat_two * second_gain + second_shift).astype(bf16)
     pre = ein("itd,df->itf", normed_two, up_full) + up_shift
-    tanh = jnp.tanh(math.sqrt(2 / math.pi) * (pre + 0.044715 * pre * pre * pre))
-    active = (0.5 * pre * (1.0 + tanh)).astype(bf16)
-    slope = (
-        0.5 * (1.0 + tanh)
-        + 0.5
-        * pre
-        * (1.0 - tanh * tanh)
-        * (math.sqrt(2 / math.pi) * (1.0 + 3 * 0.044715 * pre * pre))
-    ).astype(bf16)
+    square = pre * pre
+    tanh = jnp.tanh(pre * (GELU_A + GELU_B * square))
+    half_pre = 0.5 * pre
+    active, slope = lax.optimization_barrier(
+        (
+            (half_pre + half_pre * tanh).astype(bf16),
+            (
+                0.5 + 0.5 * tanh + half_pre * (1.0 - tanh * tanh) * (GELU_A + 3 * GELU_B * square)
+            ).astype(bf16),
+        )
+    )
+    flow = Flow()
+
+    out_grad_low = jnp.where(image_mask[:, :, None] > 0, cotangent_low, 0).astype(bf16)
+    down_grad = rows_first(ein("itd,itf->df", out_grad_low, active).astype(bf16))
+    down_bias_grad = token_sum(out_grad_low)
+    active, slope, out_grad_low, down_grad = flow.point((active, slope, out_grad_low, down_grad))
+    flow.start("down", reduce_chain(down_grad, order_a, order_b))
     output = (hidden + ein("itf,df->itd", active, down_full) + down_shift).astype(bf16)
+    output, slope = flow.point((output, slope))
     output = images_to_tokens(output, member, group)
-
-    out_grad_low = jnp.where(image_mask[:, :, None] > 0, cotangent_low, 0).astype(bf16)
-    down_grad = ein("itd,itf->df", out_grad_low, active)
-    down_bias_grad = token_sum(out_grad_low)
-    down_owned = own_grad(down_grad, order_a).T
     pre_grad = (ein("itd,df->itf", out_grad_low, down_full) * slope.astype(f32)).astype(bf16)
-    up_grad = ein("itd,itf->df", normed_two, pre_grad)
     up_bias_grad = token_sum(pre_grad)
-    up_owned = own_grad(up_grad, order_b)
+    up_grad = rows_first(ein("itd,itf->df", normed_two, pre_grad).astype(bf16))
+    pre_grad, up_grad = flow.point((pre_grad, up_grad))
+    flow.start("up", reduce_chain(up_grad, order_a, order_b))
     normed_two_grad = ein("itf,df->itd", pre_grad, up_full)
     hidden_grad = out_grad_low.astype(f32) + norm_grad(
         normed_two_grad, hat_two, scale_two, second_gain
     )
     second_gain_grad = jnp.sum(normed_two_grad * hat_two, (0, 1))
     second_shift_grad = jnp.sum(normed_two_grad, (0, 1))
+    hidden_grad, output = flow.point((hidden_grad, output), "down")
 
     attn_grad_low = hidden_grad.astype(bf16)
     context_grad = ein("itd,nd->int", attn_grad_low, out_full).astype(bf16)
-    out_grad = ein("int,itd->nd", context, attn_grad_low)
+    out_grad = rows_first(ein("int,itd->nd", context, attn_grad_low).astype(bf16))
     out_bias_grad = token_sum(attn_grad_low)
-    out_owned = own_grad(out_grad, order_a)
-    dq, dk, dv = attend_backward(queries, keys, values, context, context_grad, lse, key_keep)
-    query_owned = own_grad(ein("itd,int->dn", normed_one, dq), order_b)
-    key_owned = own_grad(ein("itd,int->dn", normed_one, dk), order_a)
-    value_owned = own_grad(ein("itd,int->dn", normed_one, dv), order_b)
-    query_bias_grad = jnp.sum(dq.astype(f32), (0, 2))
-    value_bias_grad = jnp.sum(dv.astype(f32), (0, 2))
-    normed_one_grad = (
-        ein("int,dn->itd", dq, query_full)
-        + ein("int,dn->itd", dk, key_full)
-        + ein("int,dn->itd", dv, value_full)
-    )
+    context_grad, out_grad = flow.point((context_grad, out_grad))
+    flow.start("out", reduce_chain(out_grad, order_a))
+    grads, part_a = attend_backward(
+        projected, context, context_grad, lse, key_keep, *HEAD_GROUPS[0]
+    )
+    grads, part_a, context_grad = flow.point((grads, part_a, context_grad), "down", "up")
+    weight_grad = rows_first(ein("itd,imt->dm", normed_one, part_a).astype(bf16))
+    weight_grad, grads, context_grad = flow.point(
+        (weight_grad, grads, context_grad), "down", "up"
+    )
+    flow.start("a", reduce_chain(weight_grad, order_a, order_b))
+    grads, part_b = attend_backward(
+        projected, context, context_grad, lse, key_keep, *HEAD_GROUPS[1], grads
+    )
+    grads, part_b = flow.point((grads, part_b), "down", "up", "out")
+    weight_grad = rows_first(ein("itd,imt->dm", normed_one, part_b).astype(bf16))
+    grads, weight_grad = flow.point((grads, weight_grad), "down", "up", "out", "a")
+    flow.start("b", reduce_chain(weight_grad, order_a, order_b))
+    bias_grads = [jnp.sum(part.astype(f32), (0, 2)) for part in (part_a, part_b)]
+    normed_one_grad = ein("imt,dm->itd", grads.reshape(projected.shape), project_full)
+    query_bias_grad, value_bias_grad = ungroup(bias_grads, 0), ungroup(bias_grads, 2)
     hat_one, scale_one = norm_parts(inputs_low.astype(f32))
     first_gain_grad = jnp.sum(normed_one_grad * hat_one, (0, 1))
     first_shift_grad = jnp.sum(normed_one_grad, (0, 1))
     input_grad = (
         hidden_grad + norm_grad(normed_one_grad, hat_one, scale_one, first_gain)
     ).astype(bf16)
-    input_grad = images_to_tokens(input_grad, member, group)
-
     small_grads = [
         first_gain_grad,
         first_shift_grad,
@@ -412,9 +510,26 @@
         down_bias_grad,
         up_bias_grad,
     ]
+    input_grad, small_grads = flow.point(
+        (input_grad, small_grads), "down", "up", "out", "a", "b"
+    )
+    input_grad = images_to_tokens(input_grad, member, group)
     count = lax.axis_size("fsdp")
     packed = jnp.concatenate([v.reshape(count, -1) for v in small_grads], 1)
-    packed = take_block(sum_everywhere(packed), shard, 1)[0]
+    flow.start("small", sum_chain(packed))
+    flow.point((), *flow.pending)
+    flow.point((), *flow.pending)
+    flow.point((), *flow.pending)
+    input_grad = flow.point(input_grad, *flow.pending)
+    flow.finish()
+    sums = flow.results
+    up_owned, down_owned, out_owned = (sums[name].astype(f32) for name in ("up", "down", "out"))
+    down_owned = down_owned.T
+    query_owned, key_owned, value_owned = (
+        ungroup([sums["a"], sums["b"]], which).astype(f32) for which in range(3)
+    )
+
+    packed = take_block(sums["small"], shard, 1)[0]
     (
         first_gain_owned,
         first_shift_owned,

time: 884 us -> 734 us (0.83)
  waiting for transfers between devices: 326 us -> 154 us
  matrix products: 275 us -> 250 us
  other arithmetic: 51.2 us -> 75.5 us
    ppermute x49 -> x64, waiting for transfers between devices: 224 us -> 116 us  [swap(): lax.ppermute(values, axis, [(i, i ^ bits) for i in range(lax.axis_size(ax...]
    all_gather x6 -> x4, waiting for transfers between devices: 88.2 us -> 36.6 us  [whole(): return lax.all_gather(weight, 'fsdp', axis=0, tiled=True)]
    dot_general x18 -> x13, matrix products: 275 us -> 250 us  [ein(): return jnp.einsum(spec, a, b, preferred_element_type=f32)]
    reduce_scatter x6 -> x5, waiting for transfers between devices: 10.7 us -> 0.06 us  [reduce_chain(): lax.psum_scatter(full, 'fsdp', scatter_dimension=0, tiled=True)]
    add x5 -> x6, other arithmetic: 0.09 us -> 9.52 us  [the longest x1 9.43 us: body(): out_grad_low.astype(f32)]
    ppermute x49 -> x64, starting transfers between devices: 64.3 us -> 70 us  [swap(): lax.ppermute(values, axis, [(i, i ^ bits) for i in range(lax.axis_size(ax...]
    pallas_call x2 -> x3, Pallas kernels: 87.8 us -> 91.7 us  [the longest x2 57.4 us: attend_backward(): pl.pallas_call(attend_backward_kernel, grid=(images, count), in_specs=sou...]
    dynamic_slice x15 -> x21, local copies, waits for them, and re-layouts: 18.3 us -> 20.5 us  [take_block(): return lax.dynamic_slice_in_dim(values, index * size, size, 0)]
  transfers between devices with their start and end apart: 61 -> 73, of which waited for: 32 -> 23; matrix products, arithmetic and copies ran while one was open for 32% -> 51% of each run, Pallas kernels for 4% -> 13%
where the time goes in v2:
time: 734 us; the launch traced here: 723 us
  matrix products  250 us (34%)
  waiting for transfers between devices  154 us (21%)
  Pallas kernels  91.7 us (12%)
  other arithmetic  75.5 us (10%)
  starting transfers between devices  70.3 us (10%)
  local copies, waits for them, and re-layouts  65.3 us (9%)
  between operations  15.7 us (2%)
    dot_general x13, matrix products, ein(): return jnp.einsum(spec, a, b, preferred_element_type=f32)  250 us
    ppermute x64, waiting for transfers between devices, swap(): lax.ppermute(values, axis, [(i, i ^ bits) for i in range(lax.axis_size(ax...  116 us
    ppermute x64, starting transfers between devices, swap(): lax.ppermute(values, axis, [(i, i ^ bits) for i in range(lax.axis_size(ax...  70 us
    pallas_call x2, Pallas kernels, attend_backward(): pl.pallas_call(attend_backward_kernel, grid=(images, count), in_specs=sou...  57.4 us
    all_gather x4, waiting for transfers between devices, whole(): return lax.all_gather(weight, 'fsdp', axis=0, tiled=True)  36.6 us
    pallas_call x1, Pallas kernels, attend_forward(): pl.pallas_call(attend_forward_kernel, grid=(images, heads), in_specs=sour...  34.3 us
    dynamic_slice x21, local copies, waits for them, and re-layouts, take_block(): return lax.dynamic_slice_in_dim(values, index * size, size, 0)  20.5 us
    convert_element_type x27, other arithmetic, reduce_chain(): (kept.astype(f32) + came.astype(f32)).astype(bf16)  19.4 us
  transfers between devices with their start and end apart: 73, of which 23 were waited for; matrix products, arithmetic and copies ran while one was open for 51% of the time, Pallas kernels for 13%

profile of v2, /device:TPU:0, one launch (start us, length us, event | category | flops | bytes accessed | tf_op | source)
XLA Modules:
  0.0 723.0 jit_solution(4960765568194309285)
XLA Ops:
  7.2 2.9 pad_maximum_fusion.1
  11.9 3.5 constant_dynamic-slice_fusion.49
  15.3 3.0 collective-permute-start
  21.3 2.0 collective-permute-start.4
  28.5 8.8 %collective-permute-done = bf16[2,184,1152]{2,1,0:T(8,128)(2,1)S(1)} collective-permute-done((bf16[2,184,1152]{2,1,0:T(8,128)(2,1)}, bf16[2,184,1152]{2,1,0:T(8,128)(2,1)S(1)}, u32[]{:S(2)}, u32[]{:S(2)}) %collective-permute-start) | collective-permute-done | bytes 847904 | tf_op jit(solution)/shard_map/ppermute | solution.py:188
  37.3 2.9 collective-permute-done.1
  40.3 16.5 %collective-permute-done.2 = bf16[2,184,1152]{2,1,0:T(8,128)(2,1)S(1)} collective-permute-done((bf16[2,184,1152]{2,1,0:T(8,128)(2,1)}, bf16[2,184,1152]{2,1,0:T(8,128)(2,1)S(1)}, u32[]{:S(2)}, u32[]{:S(2)}) %collective-permute-start.2) | collective-permute-done | bytes 847904 | tf_op jit(solution)/shard_map/ppermute | solution.py:188
  58.6 10.6 %all-gather.5.cloned.1.call-done = bf16[1152,3456]{1,0:T(8,128)(2,1)} async-done(((bf16[288,3456]{1,0:T(8,128)(2,1)}), bf16[1152,3456]{1,0:T(8,128)(2,1)}) %all-gather.5.cloned.1.call-update) | async-done | bytes 7962640 | tf_op jit(solution)/shard_map/all_gather | solution.py:404
  69.2 22.5 %fusion.19.q_ref.k_ref.v_ref = bf16[2,3456,736]{2,1,0:T(8,128)(2,1)} fusion(f32[3456]{0:T(1024)S(1)} %pad_maximum_fusion.3, bf16[1152,3456]{1,0:T(8,128)(2,1)} %all-gather.5.cloned.1.call-done, f32[1152]{0:T(1024)S(1)} %add.379, f32[1152]{0:T(1024)S(1)} %mul.115, f32[2,736]{1,0:T(2,128)S(1)} %add_rsqrt_fusion.1, f32[2,736]{1,0:T(2,128)S(1)} %broadcast_multiply_fusion.5, ...), kind=kOutput, calls=%fused_computation.35 | convolution fusion | flops 11753201664 | bytes 21563392 | tf_op jit(solution)/shard_map/itd,dm->imt/dot_general | solution.py:337
  97.1 34.3 %attend_forward.1 = (bf16[2,1152,736]{2,1,0:T(8,128)(2,1)S(1)}, f32[2,16,1,736]{3,2,1,0:T(1,128)S(1)}) custom-call(bf16[2,3456,736]{2,1,0:T(8,128)(2,1)} %fusion.19.q_ref.k_ref.v_ref, bf16[2,3456,736]{2,1,0:T(8,128)(2,1)} %fusion.19.q_ref.k_ref.v_ref, bf16[2,3456,736]{2,1,0:T(8,128)(2,1)} %fusion.19.q_ref.k_ref.v_ref, s32[2,1,736]{2,1,0:T(1,128)S(1)} %broadcast_in_dim.20.mask_ref), custom_call_target="tpu_custom_call" | custom-call | flops 17750294528 | bytes 13565952 | tf_op jit(solution)/shard_map/attend_forward/pallas_call | solution.py:78
  132.1 9.5 %fusion.58 = (f32[2,736]{1,0:T(2,128)S(1)}, f32[2,736,1152]{2,1,0:T(8,128)S(1)}) fusion(f32[1152]{0:T(1024)} %add.390, bf16[2,1152,736]{2,1,0:T(8,128)(2,1)S(1)} %get-tuple-element.166.context_ref, bf16[1152,1152]{1,0:T(8,128)(2,1)} %all-gather.7.cloned.1.call-done, bf16[2,184,1152]{2,1,0:T(8,128)(2,1)} %copy-done.15, ...), kind=kOutput, calls=%fused_computation.216 | convolution fusion | flops 3925645824 | bytes 16230656 | tf_op jit(solution)/shard_map/int,nd->itd/dot_general | solution.py:337
  141.6 2.8 copy-done.5
  145.4 3.3 convert_reduce_fusion.4
  148.7 17.0 %all-gather.9.cloned.1.call-done = bf16[1152,4304]{1,0:T(8,128)(2,1)} async-done(((bf16[288,4304]{1,0:T(8,128)(2,1)}), bf16[1152,4304]{1,0:T(8,128)(2,1)}) %all-gather.9.cloned.1.call-update) | async-done | bytes 9916432 | tf_op jit(solution)/shard_map/all_gather | solution.py:404
  165.7 35.0 %add_convert_fusion = (bf16[2,736,4304]{2,1,0:T(8,128)(2,1)}, bf16[2,736,4304]{2,1,0:T(8,128)(2,1)S(1)}) fusion(f32[4304]{0:T(1024)S(1)} %copy-done.59, bf16[1152,4304]{1,0:T(8,128)(2,1)} %all-gather.9.cloned.1.call-done, f32[2,736,1152]{2,1,0:T(8,128)} %copy-done.5, f32[1152]{0:T(1024)S(1)} %copy-done.67, f32[1152]{0:T(1024)S(1)} %mul.248, ...), kind=kOutput, calls=%fused_computation.4 | convolution fusion | flops 14725817344 | bytes 42079552 | tf_op jit(solution)/shard_map/itd,df->itf/dot_general | solution.py:337
  200.8 4.7 copy-done.78
  205.4 19.6 %fusion.1 = bf16[1152,4304]{1,0:T(8,128)(2,1)} fusion(bf16[2,736,1152]{2,1,0:T(8,128)(2,1)S(1)} %get-tuple-element.170, bf16[2,736,4304]{2,1,0:T(8,128)(2,1)S(1)} %get-tuple-element.171), kind=kOutput, calls=%fused_computation.9 | convolution fusion | flops 14601922560 | bytes 25978880 | tf_op jit(solution)/shard_map/itd,itf->df/dot_general | solution.py:337
  225.8 9.0 %all-gather.11.cloned.1.call-done = bf16[1152,4304]{1,0:T(8,128)(2,1)} async-done(((bf16[288,4304]{1,0:T(8,128)(2,1)}), bf16[1152,4304]{1,0:T(8,128)(2,1)}) %all-gather.11.cloned.1.call-update) | async-done | bytes 9916432 | tf_op jit(solution)/shard_map/all_gather | solution.py:404
  234.8 24.0 %add_convert_fusion.2 = bf16[2,736,1152]{2,1,0:T(8,128)(2,1)} fusion(f32[2,736,1152]{2,1,0:T(8,128)} %copy-done.5, bf16[2,736,4304]{2,1,0:T(8,128)(2,1)} %copy-done.78, bf16[1152,4304]{1,0:T(8,128)(2,1)} %all-gather.11.cloned.1.call-done, f32[1152]{0:T(1024)S(1)} %add.406), kind=kOutput, calls=%fused_computation.54 | convolution fusion | flops 14602051584 | bytes 32766464 | tf_op jit(solution)/shard_map/itf,df->itd/dot_general | solution.py:337
  258.8 25.8 %convert_reduce_fusion = (f32[4304]{0:T(1024)}, bf16[2,736,4304]{2,1,0:T(8,128)(2,1)}) fusion(bf16[2,736,4304]{2,1,0:T(8,128)(2,1)} %get-tuple-element.173, bf16[2,736,1152]{2,1,0:T(8,128)(2,1)S(1)} %get-tuple-element.170, bf16[1152,4304]{1,0:T(8,128)(2,1)} %all-gather.11.cloned.1.call-done), kind=kOutput, calls=%fused_computation.2 | convolution fusion | flops 14628637696 | bytes 38667072 | tf_op jit(solution)/shard_map/itd,df->itf/dot_general | solution.py:337
  284.5 23.2 %fusion.2 = bf16[1152,4304]{1,0:T(8,128)(2,1)} fusion(bf16[2,736,4304]{2,1,0:T(8,128)(2,1)} %get-tuple-element.174, f32[2,736,1152]{2,1,0:T(8,128)S(1)} %bitcast.75, f32[1152]{0:T(1024)S(1)} %copy-done.67, f32[1152]{0:T(1024)S(1)} %mul.248, f32[2,736]{1,0:T(2,128)S(1)} %add_rsqrt_fusion, f32[2,736]{1,0:T(2,128)S(1)} %broadcast_multiply_fusion.4), kind=kOutput, calls=%fused_computation.10 | convolution fusion | flops 14610401280 | bytes 29391360 | tf_op jit(solution)/shard_map/itd,itf->df/dot_general | solution.py:337
  307.9 2.0 broadcast.90.clone
  316.4 26.8 %multiply_reduce_fusion = (f32[1152]{0:T(1024)}, f32[2,736]{1,0:T(2,128)S(1)}, f32[2,736]{1,0:T(2,128)S(1)}, f32[1152]{0:T(1024)}, f32[2,736,1152]{2,1,0:T(8,128)}) fusion(f32[2,736,1152]{2,1,0:T(8,128)} %copy-done.5, f32[2,736]{1,0:T(2,128)S(1)} %add_rsqrt_fusion, f32[2,736]{1,0:T(2,128)S(1)} %broadcast_multiply_fusion.4, f32[1152]{0:T(1024)S(1)} %mul.248, ...), kind=kOutput, calls=%fused_computation.50 | convolution fusion | flops 14612221952 | bytes 36190720 | tf_op jit(solution)/shard_map/itf,df->itd/dot_general | solution.py:337
  343.2 9.4 %multiply_add_fusion.1 = f32[2,736,1152]{2,1,0:T(8,128)} fusion(bf16[2,736,1152]{2,1,0:T(8,128)(2,1)S(1)} %get-tuple-element.170, f32[2,736,1152]{2,1,0:T(8,128)} %get-tuple-element.411, f32[2,736,1152]{2,1,0:T(8,128)} %copy-done.5, f32[2,736]{1,0:T(2,128)S(1)} %get-tuple-element.415, f32[2,736]{1,0:T(2,128)S(1)} %get-tuple-element.416, f32[1152]{0:T(1024)S(1)} %mul.248, ...), kind=kLoop, calls=%fused_computation.52 | loop fusion | flops 15261696 | bytes 23768576 | tf_op jit(solution)/shard_map/add | solution.py:464
  352.7 2.3 constant_dynamic-update-slice_fusion.5
  354.9 2.1 constant_dynamic-update-slice_fusion.4
  358.0 2.4 slice.173
  360.5 2.4 slice.172
  362.9 8.7 %convolution_convert_fusion = bf16[2,736,1152]{2,1,0:T(8,128)(2,1)} fusion(bf16[1152,1152]{1,0:T(8,128)(2,1)S(1)} %copy-done.77, f32[2,736,1152]{2,1,0:T(8,128)} %multiply_add_fusion.1), kind=kOutput, calls=%fused_computation.61 | convolution fusion | flops 3910385664 | bytes 12828672 | tf_op jit(solution)/shard_map/itd,nd->int/dot_general | solution.py:337
  371.6 5.9 copy.46
  377.5 9.2 %fusion.22 = bf16[1152,1152]{1,0:T(8,128)(2,1)} fusion(bf16[2,1152,736]{2,1,0:T(8,128)(2,1)S(1)} %copy-done.1, f32[2,736,1152]{2,1,0:T(8,128)} %multiply_add_fusion.1), kind=kOutput, calls=%fused_computation.36 | convolution fusion | flops 3910017024 | bytes 12828672 | tf_op jit(solution)/shard_map/int,itd->nd/dot_general | solution.py:337
  386.7 2.4 constant_dynamic-slice_fusion.34
  389.9 2.5 constant_dynamic-slice_fusion.36
  394.8 28.5 %attend_backward.2 = (bf16[2,3,1152,736]{3,2,1,0:T(8,128)(2,1)}, bf16[2,3,576,736]{3,2,1,0:T(8,128)(2,1)}) custom-call(bf16[2,3456,736]{2,1,0:T(8,128)(2,1)} %fusion.19.q_ref.k_ref.v_ref, bf16[2,3456,736]{2,1,0:T(8,128)(2,1)} %fusion.19.q_ref.k_ref.v_ref, bf16[2,3456,736]{2,1,0:T(8,128)(2,1)} %fusion.19.q_ref.k_ref.v_ref, ...), custom_call_target="tpu_custom_call" | custom-call | flops 22187868160 | bytes 13565952 | tf_op jit(solution)/shard_map/attend_backward/pallas_call | solution.py:156
  426.4 2.3 add_convert_fusion.6
  435.9 9.6 %fusion.23 = bf16[1152,1728]{1,0:T(8,128)(2,1)} fusion(bf16[2,1728,736]{2,1,0:T(8,128)(2,1)S(1)} %bitcast.81, f32[1152]{0:T(1024)S(1)} %copy-done.64, f32[1152]{0:T(1024)S(1)} %copy-done.51, f32[2,736]{1,0:T(2,128)S(1)} %copy-done.55, f32[2,736]{1,0:T(2,128)S(1)} %copy-done.49, bf16[2,184,1152]{2,1,0:T(8,128)(2,1)S(1)} %copy-done.16, ...), kind=kOutput, calls=%fused_computation.37 | convolution fusion | flops 5884526592 | bytes 12481024 | tf_op jit(solution)/shard_map/itd,imt->dm/dot_general | solution.py:337
  445.5 3.5 convert_reduce_fusion.2
  457.6 2.3 collective-permute-start.18
  462.7 28.9 %attend_backward.3 = (bf16[2,3,1152,736]{3,2,1,0:T(8,128)(2,1)}, bf16[2,3,576,736]{3,2,1,0:T(8,128)(2,1)}) custom-call(bf16[2,3456,736]{2,1,0:T(8,128)(2,1)} %fusion.19.q_ref.k_ref.v_ref, bf16[2,3456,736]{2,1,0:T(8,128)(2,1)} %fusion.19.q_ref.k_ref.v_ref, bf16[2,3456,736]{2,1,0:T(8,128)(2,1)} %fusion.19.q_ref.k_ref.v_ref, ...), custom_call_target="tpu_custom_call", output_to_operand_aliasing={{0}: (7, {})} | custom-call | flops 22187868160 | bytes 13565952 | tf_op jit(solution)/shard_map/attend_backward/pallas_call | solution.py:156
  493.5 2.3 collective-permute-start.24
  505.1 13.1 %fusion.24 = bf16[1152,1728]{1,0:T(8,128)(2,1)} fusion(bf16[2,1728,736]{2,1,0:T(8,128)(2,1)} %bitcast.76, f32[1152]{0:T(1024)} %copy-done.63, f32[1152]{0:T(1024)} %copy-done.50, f32[2,736]{1,0:T(2,128)} %copy-done.54, f32[2,736]{1,0:T(2,128)S(1)} %copy-done.49, bf16[2,184,1152]{2,1,0:T(8,128)(2,1)} %copy-done.15, bf16[2,184,1152]{2,1,0:T(8,128)(2,1)} %copy-done.12, ...), kind=kOutput, calls=%fused_computation.38 | convolution fusion | flops 5884526592 | bytes 12481024 | tf_op jit(solution)/shard_map/itd,imt->dm/dot_general | solution.py:337
  518.3 2.3 collective-permute-done.23
  521.7 3.5 convert_reduce_fusion.1
  530.1 2.0 collective-permute-start.28
  533.9 2.0 collective-permute-start.32
  535.9 23.4 %fusion.32 = (f32[1152]{0:T(1024)S(1)}, f32[2,736]{1,0:T(2,128)S(1)}, f32[2,736]{1,0:T(2,128)S(1)}, f32[1152]{0:T(1024)S(1)}, f32[2,736,1152]{2,1,0:T(8,128)}) fusion(f32[2,736]{1,0:T(2,128)S(1)} %copy-done.56, f32[2,736]{1,0:T(2,128)S(1)} %copy-done.49, bf16[2,184,1152]{2,1,0:T(8,128)(2,1)S(1)} %copy-done.17, bf16[2,184,1152]{2,1,0:T(8,128)(2,1)S(1)} %copy-done.14, ...), kind=kOutput, calls=%fused_computation.46 | convolution fusion | flops 11749806080 | bytes 28348928 | tf_op jit(solution)/shard_map/imt,dm->itd/dot_general | solution.py:337
  564.9 9.4 %convert_reduce_fusion.5 = (f32[1152]{0:T(1024)S(1)}, bf16[2,736,1152]{2,1,0:T(8,128)(2,1)S(1)}) fusion(f32[2,736,1152]{2,1,0:T(8,128)} %multiply_add_fusion.1, f32[2,736]{1,0:T(2,128)S(1)} %broadcast_multiply_fusion, f32[2,736]{1,0:T(2,128)S(1)} %copy-done.49, bf16[2,184,1152]{2,1,0:T(8,128)(2,1)} %copy-done.15, bf16[2,184,1152]{2,1,0:T(8,128)(2,1)} %copy-done.12, ...), kind=kLoop, calls=%fused_computation.51 | loop fusion | flops 33913728 | bytes 20381696 | tf_op jit(solution)/shard_map/reduce_sum | solution.py:341
  574.3 7.4 %collective-permute-done.31 = bf16[144,896]{1,0:T(8,128)(2,1)S(1)} collective-permute-done((bf16[144,896]{1,0:T(8,128)(2,1)S(1)}, bf16[144,896]{1,0:T(8,128)(2,1)S(1)}, u32[]{:S(2)}, u32[]{:S(2)}) %collective-permute-start.31) | collective-permute-done | bytes 258080 | tf_op jit(solution)/shard_map/ppermute | solution.py:188
  587.8 3.3 collective-permute-start.38
  594.6 2.1 maximum_select_fusion.4
  596.7 2.6 convert_bitcast_fusion
  605.3 10.6 %collective-permute-done.42 = bf16[144,832]{1,0:T(8,128)(2,1)S(1)} collective-permute-done((bf16[144,832]{1,0:T(8,128)(2,1)S(1)}, bf16[144,832]{1,0:T(8,128)(2,1)S(1)}, u32[]{:S(2)}, u32[]{:S(2)}) %collective-permute-start.42) | collective-permute-done | bytes 239648 | tf_op jit(solution)/shard_map/ppermute | solution.py:188
  615.9 5.9 collective-permute-done.41
  625.7 2.7 collective-permute-start.45
  629.5 2.6 maximum_convert_fusion
  635.0 3.3 collective-permute-start.35
  641.6 8.9 %collective-permute-done.33 = bf16[2,184,1152]{2,1,0:T(8,128)(2,1)S(1)} collective-permute-done((bf16[2,184,1152]{2,1,0:T(8,128)(2,1)S(1)}, bf16[2,184,1152]{2,1,0:T(8,128)(2,1)S(1)}, u32[]{:S(2)}, u32[]{:S(2)}) %collective-permute-start.33) | collective-permute-done | bytes 847904 | tf_op jit(solution)/shard_map/ppermute | solution.py:188
  651.8 11.0 %collective-permute-done.34 = bf16[2,184,1152]{2,1,0:T(8,128)(2,1)S(1)} collective-permute-done((bf16[2,184,1152]{2,1,0:T(8,128)(2,1)S(1)}, bf16[2,184,1152]{2,1,0:T(8,128)(2,1)S(1)}, u32[]{:S(2)}, u32[]{:S(2)}) %collective-permute-start.34) | collective-permute-done | bytes 847904 | tf_op jit(solution)/shard_map/ppermute | solution.py:188
  665.1 15.1 %collective-permute-done.35 = bf16[2,184,1152]{2,1,0:T(8,128)(2,1)S(1)} collective-permute-done((bf16[2,184,1152]{2,1,0:T(8,128)(2,1)S(1)}, bf16[2,184,1152]{2,1,0:T(8,128)(2,1)S(1)}, u32[]{:S(2)}, u32[]{:S(2)}) %collective-permute-start.35) | collective-permute-done | bytes 847904 | tf_op jit(solution)/shard_map/ppermute | solution.py:188
  680.3 9.2 %collective-permute-done.52 = bf16[72,832]{1,0:T(8,128)(2,1)S(1)} collective-permute-done((bf16[72,832]{1,0:T(8,128)(2,1)S(1)}, bf16[72,832]{1,0:T(8,128)(2,1)S(1)}, u32[]{:S(2)}, u32[]{:S(2)}) %collective-permute-start.52) | collective-permute-done | bytes 119840 | tf_op jit(solution)/shard_map/ppermute | solution.py:188
  690.8 2.1 collective-permute-start.58
  697.2 4.4 collective-permute-done.57
  704.4 2.5 collective-permute-done.63
  706.9 4.0 collective-permute-done.62
  (432 shorter events, 119.7 us)
Async XLA Ops:
  7.2 62.0 %all-gather.5.cloned.1.call-start = ((), (), s32[]{:S(2)}) async-start(), calls=%async_computation.5 | async-start | bytes 9953280 | tf_op jit(solution)/shard_map/all_gather | solution.py:404
  10.3 121.8 %all-gather.7.cloned.1.call-start = ((), (), s32[]{:S(2)}) async-start(), calls=%async_computation.6 | async-start | bytes 3317760 | tf_op jit(solution)/shard_map/all_gather | solution.py:404
  11.0 154.7 %all-gather.9.cloned.1.call-start = ((), (), s32[]{:S(2)}) async-start(), calls=%async_computation.7 | async-start | bytes 12533760 | tf_op jit(solution)/shard_map/all_gather | solution.py:404
  11.8 223.0 %all-gather.11.cloned.1.call-start = ((), (), s32[]{:S(2)}) async-start(), calls=%async_computation.8 | async-start | bytes 12533760 | tf_op jit(solution)/shard_map/all_gather | solution.py:404
  15.3 22.0 %collective-permute-start = (bf16[2,184,1152]{2,1,0:T(8,128)(2,1)}, bf16[2,184,1152]{2,1,0:T(8,128)(2,1)S(1)}, u32[]{:S(2)}, u32[]{:S(2)}) collective-permute-start(bf16[2,184,1152]{2,1,0:T(8,128)(2,1)} %get-tuple-element.350), channel_id=1, source_target_pairs={{0,4},{4,0},{8,12},{12,8},{16,20},{20,16},{24,28},{28,24},{1,5},{5... | collective-permute-start | bytes 2543624 | tf_op jit(solution)/shard_map/ppermute | solution.py:188
  18.3 22.0 %collective-permute-start.1 = (bf16[2,184,1152]{2,1,0:T(8,128)(2,1)}, bf16[2,184,1152]{2,1,0:T(8,128)(2,1)S(1)}, u32[]{:S(2)}, u32[]{:S(2)}) collective-permute-start(bf16[2,184,1152]{2,1,0:T(8,128)(2,1)} %get-tuple-element.352), channel_id=1, source_target_pairs={{0,8},{4,12},{8,0},{12,4},{16,24},{20,28},{24,16},{28,20},{1,9},{5... | collective-permute-start | bytes 2543624 | tf_op jit(solution)/shard_map/ppermute | solution.py:188
  19.9 36.9 %collective-permute-start.2 = (bf16[2,184,1152]{2,1,0:T(8,128)(2,1)}, bf16[2,184,1152]{2,1,0:T(8,128)(2,1)S(1)}, u32[]{:S(2)}, u32[]{:S(2)}) collective-permute-start(bf16[2,184,1152]{2,1,0:T(8,128)(2,1)} %get-tuple-element.351), channel_id=1, source_target_pairs={{0,12},{4,8},{8,4},{12,0},{16,28},{20,24},{24,20},{28,16},{1,13},{... | collective-permute-start | bytes 2543624 | tf_op jit(solution)/shard_map/ppermute | solution.py:188
  20.2 337.9 %reduce-scatter.6.cloned.1.call-start = ((), (), s32[]{:S(2)}) async-start(), calls=%async_computation.9 | async-start | bytes 12533760 | tf_op jit(solution)/shard_map/reduce_scatter | solution.py:247
  93.6 51.7 %collective-permute-start.5 = (bf16[2,184,1152]{2,1,0:T(8,128)(2,1)}, bf16[2,184,1152]{2,1,0:T(8,128)(2,1)}, u32[]{:S(2)}, u32[]{:S(2)}) collective-permute-start(bf16[2,184,1152]{2,1,0:T(8,128)(2,1)} %get-tuple-element.348), channel_id=1, source_target_pairs={{0,4},{4,0},{8,12},{12,8},{16,20},{20,16},{24,28},{28,24},{1,5},{5... | collective-permute-start | bytes 2543624 | tf_op jit(solution)/shard_map/ppermute | solution.py:188
  95.0 50.3 %collective-permute-start.6 = (bf16[2,184,1152]{2,1,0:T(8,128)(2,1)}, bf16[2,184,1152]{2,1,0:T(8,128)(2,1)}, u32[]{:S(2)}, u32[]{:S(2)}) collective-permute-start(bf16[2,184,1152]{2,1,0:T(8,128)(2,1)} %get-tuple-element.347), channel_id=1, source_target_pairs={{0,8},{4,12},{8,0},{12,4},{16,24},{20,28},{24,16},{28,20},{1,9},{5... | collective-permute-start | bytes 2543624 | tf_op jit(solution)/shard_map/ppermute | solution.py:188
  96.6 48.8 %collective-permute-start.7 = (bf16[2,184,1152]{2,1,0:T(8,128)(2,1)}, bf16[2,184,1152]{2,1,0:T(8,128)(2,1)}, u32[]{:S(2)}, u32[]{:S(2)}) collective-permute-start(bf16[2,184,1152]{2,1,0:T(8,128)(2,1)} %get-tuple-element.346), channel_id=1, source_target_pairs={{0,12},{4,8},{8,4},{12,0},{16,28},{20,24},{24,20},{28,16},{1,13},{... | collective-permute-start | bytes 2543624 | tf_op jit(solution)/shard_map/ppermute | solution.py:188
  225.0 198.3 %reduce-scatter.8.cloned.1.call-start = ((), (), s32[]{:S(2)}) async-start(), calls=%async_computation.10 | async-start | bytes 12533760 | tf_op jit(solution)/shard_map/reduce_scatter | solution.py:247
  307.8 184.6 %reduce-scatter.10.cloned.1.call-start = ((), (), s32[]{:S(2)}) async-start(), calls=%async_computation.11 | async-start | bytes 3317760 | tf_op jit(solution)/shard_map/reduce_scatter | solution.py:247
  312.9 39.8 %collective-permute-start.8 = (bf16[2,184,1152]{2,1,0:T(8,128)(2,1)}, bf16[2,184,1152]{2,1,0:T(8,128)(2,1)}, u32[]{:S(2)}, u32[]{:S(2)}) collective-permute-start(bf16[2,184,1152]{2,1,0:T(8,128)(2,1)} %get-tuple-element.343), channel_id=1, source_target_pairs={{0,4},{4,0},{8,12},{12,8},{16,20},{20,16},{24,28},{28,24},{1,5},{5... | collective-permute-start | bytes 2543624 | tf_op jit(solution)/shard_map/ppermute | solution.py:188
  314.3 40.6 %collective-permute-start.9 = (bf16[2,184,1152]{2,1,0:T(8,128)(2,1)}, bf16[2,184,1152]{2,1,0:T(8,128)(2,1)}, u32[]{:S(2)}, u32[]{:S(2)}) collective-permute-start(bf16[2,184,1152]{2,1,0:T(8,128)(2,1)} %get-tuple-element.342), channel_id=1, source_target_pairs={{0,8},{4,12},{8,0},{12,4},{16,24},{20,28},{24,16},{28,20},{1,9},{5... | collective-permute-start | bytes 2543624 | tf_op jit(solution)/shard_map/ppermute | solution.py:188
  315.8 41.2 %collective-permute-start.10 = (bf16[2,184,1152]{2,1,0:T(8,128)(2,1)}, bf16[2,184,1152]{2,1,0:T(8,128)(2,1)S(1)}, u32[]{:S(2)}, u32[]{:S(2)}) collective-permute-start(bf16[2,184,1152]{2,1,0:T(8,128)(2,1)} %get-tuple-element.341), channel_id=1, source_target_pairs={{0,12},{4,8},{8,4},{12,0},{16,28},{20,24},{24,20},{28,16},{1,13},{... | collective-permute-start | bytes 2543624 | tf_op jit(solution)/shard_map/ppermute | solution.py:188
  389.1 34.3 %collective-permute-start.12 = (bf16[144,2128]{1,0:T(8,128)(2,1)}, bf16[144,2128]{1,0:T(8,128)(2,1)}, u32[]{:S(2)}, u32[]{:S(2)}) collective-permute-start(bf16[144,2128]{1,0:T(8,128)(2,1)} %get-tuple-element.357), channel_id=1, source_target_pairs={{0,8},{4,12},{8,0},{12,4},{16,24},{20,28},{24,16},{28,20},{1,9},{5... | collective-permute-start | bytes 1838600 | tf_op jit(solution)/shard_map/ppermute | solution.py:188
  392.4 31.0 %collective-permute-start.11 = (bf16[144,2176]{1,0:T(8,128)(2,1)}, bf16[144,2176]{1,0:T(8,128)(2,1)}, u32[]{:S(2)}, u32[]{:S(2)}) collective-permute-start(bf16[144,2176]{1,0:T(8,128)(2,1)} %get-tuple-element.359), channel_id=1, source_target_pairs={{0,4},{4,0},{8,12},{12,8},{16,20},{20,16},{24,28},{28,24},{1,5},{5... | collective-permute-start | bytes 1880072 | tf_op jit(solution)/shard_map/ppermute | solution.py:188
  423.3 97.4 %reduce-scatter.12.cloned.1.call-start = ((), (), s32[]{:S(2)}) async-start(), calls=%async_computation.12 | async-start | bytes 5160960 | tf_op jit(solution)/shard_map/reduce_scatter | solution.py:247
  425.9 23.7 %collective-permute-start.16 = (bf16[144,2128]{1,0:T(8,128)(2,1)}, bf16[144,2128]{1,0:T(8,128)(2,1)}, u32[]{:S(2)}, u32[]{:S(2)}) collective-permute-start(bf16[144,2128]{1,0:T(8,128)(2,1)} %get-tuple-element.353), channel_id=1, source_target_pairs={{0,8},{4,12},{8,0},{12,4},{16,24},{20,28},{24,16},{28,20},{1,9},{5... | collective-permute-start | bytes 1838600 | tf_op jit(solution)/shard_map/ppermute | solution.py:188
  429.6 20.0 %collective-permute-start.14 = (bf16[72,2128]{1,0:T(8,128)(2,1)}, bf16[72,2128]{1,0:T(8,128)(2,1)}, u32[]{:S(2)}, u32[]{:S(2)}) collective-permute-start(bf16[72,2128]{1,0:T(8,128)(2,1)} %get-tuple-element.367), channel_id=1, source_target_pairs={{0,4},{4,0},{8,12},{12,8},{16,20},{20,16},{24,28},{28,24},{1,5},{5... | collective-permute-start | bytes 919304 | tf_op jit(solution)/shard_map/ppermute | solution.py:188
  432.7 16.9 %collective-permute-start.13 = (bf16[72,2176]{1,0:T(8,128)(2,1)}, bf16[72,2176]{1,0:T(8,128)(2,1)}, u32[]{:S(2)}, u32[]{:S(2)}) collective-permute-start(bf16[72,2176]{1,0:T(8,128)(2,1)} %get-tuple-element.369), channel_id=1, source_target_pairs={{0,8},{4,12},{8,0},{12,4},{16,24},{20,28},{24,16},{28,20},{1,9},{5... | collective-permute-start | bytes 940040 | tf_op jit(solution)/shard_map/ppermute | solution.py:188
  434.7 15.6 %collective-permute-start.15 = (bf16[144,2176]{1,0:T(8,128)(2,1)}, bf16[144,2176]{1,0:T(8,128)(2,1)}, u32[]{:S(2)}, u32[]{:S(2)}) collective-permute-start(bf16[144,2176]{1,0:T(8,128)(2,1)} %get-tuple-element.355), channel_id=1, source_target_pairs={{0,4},{4,0},{8,12},{12,8},{16,20},{20,16},{24,28},{28,24},{1,5},{5... | collective-permute-start | bytes 1880072 | tf_op jit(solution)/shard_map/ppermute | solution.py:188
  452.4 39.2 %collective-permute-start.20 = (bf16[72,2128]{1,0:T(8,128)(2,1)}, bf16[72,2128]{1,0:T(8,128)(2,1)}, u32[]{:S(2)}, u32[]{:S(2)}) collective-permute-start(bf16[72,2128]{1,0:T(8,128)(2,1)} %get-tuple-element.363), channel_id=1, source_target_pairs={{0,4},{4,0},{8,12},{12,8},{16,20},{20,16},{24,28},{28,24},{1,5},{5... | collective-permute-start | bytes 919304 | tf_op jit(solution)/shard_map/ppermute | solution.py:188
  455.5 36.9 %collective-permute-start.19 = (bf16[72,2176]{1,0:T(8,128)(2,1)}, bf16[72,2176]{1,0:T(8,128)(2,1)}, u32[]{:S(2)}, u32[]{:S(2)}) collective-permute-start(bf16[72,2176]{1,0:T(8,128)(2,1)} %get-tuple-element.365), channel_id=1, source_target_pairs={{0,8},{4,12},{8,0},{12,4},{16,24},{20,28},{24,16},{28,20},{1,9},{5... | collective-permute-start | bytes 940040 | tf_op jit(solution)/shard_map/ppermute | solution.py:188
  456.4 126.0 %reduce-scatter.14.cloned.1.call-start = ((), (), s32[]{:S(2)}) async-start(), calls=%async_computation.13 | async-start | bytes 5160960 | tf_op jit(solution)/shard_map/reduce_scatter | solution.py:247
  457.6 34.0 %collective-permute-start.18 = (bf16[72,2128]{1,0:T(8,128)(2,1)S(1)}, bf16[72,2128]{1,0:T(8,128)(2,1)S(1)}, u32[]{:S(2)}, u32[]{:S(2)}) collective-permute-start(bf16[72,2128]{1,0:T(8,128)(2,1)S(1)} %add_convert_fusion.15), channel_id=1, source_target_pairs={{0,16},{4,20},{8,24},{12,28},{16,0},{20,4},{24,8},{28,12},{1,17},{... | collective-permute-start | bytes 919304 | tf_op jit(solution)/shard_map/ppermute | solution.py:188
  461.1 31.2 %collective-permute-start.17 = (bf16[72,2176]{1,0:T(8,128)(2,1)S(1)}, bf16[72,2176]{1,0:T(8,128)(2,1)}, u32[]{:S(2)}, u32[]{:S(2)}) collective-permute-start(bf16[72,2176]{1,0:T(8,128)(2,1)S(1)} %add_convert_fusion.16), channel_id=1, source_target_pairs={{0,16},{4,20},{8,24},{12,28},{16,0},{20,4},{24,8},{28,12},{1,17},{... | collective-permute-start | bytes 940040 | tf_op jit(solution)/shard_map/ppermute | solution.py:188
  493.5 24.8 %collective-permute-start.24 = (bf16[72,2128]{1,0:T(8,128)(2,1)S(1)}, bf16[72,2128]{1,0:T(8,128)(2,1)S(1)}, u32[]{:S(2)}, u32[]{:S(2)}) collective-permute-start(bf16[72,2128]{1,0:T(8,128)(2,1)S(1)} %add_convert_fusion.11), channel_id=1, source_target_pairs={{0,16},{4,20},{8,24},{12,28},{16,0},{20,4},{24,8},{28,12},{1,17},{... | collective-permute-start | bytes 919304 | tf_op jit(solution)/shard_map/ppermute | solution.py:188
  497.0 23.6 %collective-permute-start.23 = (bf16[72,2176]{1,0:T(8,128)(2,1)S(1)}, bf16[72,2176]{1,0:T(8,128)(2,1)S(1)}, u32[]{:S(2)}, u32[]{:S(2)}) collective-permute-start(bf16[72,2176]{1,0:T(8,128)(2,1)S(1)} %add_convert_fusion.12), channel_id=1, source_target_pairs={{0,16},{4,20},{8,24},{12,28},{16,0},{20,4},{24,8},{28,12},{1,17},{... | collective-permute-start | bytes 940040 | tf_op jit(solution)/shard_map/ppermute | solution.py:188
  498.9 19.4 %collective-permute-start.22 = (bf16[72,2128]{1,0:T(8,128)(2,1)S(1)}, bf16[72,2128]{1,0:T(8,128)(2,1)S(1)}, u32[]{:S(2)}, u32[]{:S(2)}) collective-permute-start(bf16[72,2128]{1,0:T(8,128)(2,1)S(1)} %add_convert_fusion.13), channel_id=1, source_target_pairs={{0,4},{4,0},{8,12},{12,8},{16,20},{20,16},{24,28},{28,24},{1,5},{5... | collective-permute-start | bytes 919304 | tf_op jit(solution)/shard_map/ppermute | solution.py:188
  501.4 19.2 %collective-permute-start.21 = (bf16[72,2176]{1,0:T(8,128)(2,1)S(1)}, bf16[72,2176]{1,0:T(8,128)(2,1)S(1)}, u32[]{:S(2)}, u32[]{:S(2)}) collective-permute-start(bf16[72,2176]{1,0:T(8,128)(2,1)S(1)} %add_convert_fusion.14), channel_id=1, source_target_pairs={{0,8},{4,12},{8,0},{12,4},{16,24},{20,28},{24,16},{28,20},{1,9},{5... | collective-permute-start | bytes 940040 | tf_op jit(solution)/shard_map/ppermute | solution.py:188
  504.2 16.4 %collective-permute-start.25 = (bf16[144,1152]{1,0:T(8,128)(2,1)S(1)}, bf16[144,1152]{1,0:T(8,128)(2,1)S(1)}, u32[]{:S(2)}, u32[]{:S(2)}) collective-permute-start(bf16[144,1152]{1,0:T(8,128)(2,1)S(1)} %get-tuple-element.361), channel_id=1, source_target_pairs={{0,4},{4,0},{8,12},{12,8},{16,20},{20,16},{24,28},{28,24},{1,5},{5... | collective-permute-start | bytes 995336 | tf_op jit(solution)/shard_map/ppermute | solution.py:188
  527.3 35.6 %collective-permute-start.30 = (bf16[72,1152]{1,0:T(8,128)(2,1)}, bf16[72,1152]{1,0:T(8,128)(2,1)}, u32[]{:S(2)}, u32[]{:S(2)}) collective-permute-start(bf16[72,1152]{1,0:T(8,128)(2,1)} %get-tuple-element.379), channel_id=1, source_target_pairs={{0,8},{4,12},{8,0},{12,4},{16,24},{20,28},{24,16},{28,20},{1,9},{5... | collective-permute-start | bytes 497672 | tf_op jit(solution)/shard_map/ppermute | solution.py:188
  528.1 54.3 %collective-permute-start.29 = (bf16[72,2128]{1,0:T(8,128)(2,1)}, bf16[72,2128]{1,0:T(8,128)(2,1)}, u32[]{:S(2)}, u32[]{:S(2)}) collective-permute-start(bf16[72,2128]{1,0:T(8,128)(2,1)} %add_convert_fusion.9), channel_id=1, source_target_pairs={{0,4},{4,0},{8,12},{12,8},{16,20},{20,16},{24,28},{28,24},{1,5},{5... | collective-permute-start | bytes 919304 | tf_op jit(solution)/shard_map/ppermute | solution.py:188
  530.1 52.4 %collective-permute-start.28 = (bf16[72,2176]{1,0:T(8,128)(2,1)}, bf16[72,2176]{1,0:T(8,128)(2,1)}, u32[]{:S(2)}, u32[]{:S(2)}) collective-permute-start(bf16[72,2176]{1,0:T(8,128)(2,1)} %add_convert_fusion.10), channel_id=1, source_target_pairs={{0,8},{4,12},{8,0},{12,4},{16,24},{20,28},{24,16},{28,20},{1,9},{5... | collective-permute-start | bytes 940040 | tf_op jit(solution)/shard_map/ppermute | solution.py:188
  533.0 49.4 %collective-permute-start.27 = (bf16[144,2128]{1,0:T(8,128)(2,1)}, bf16[144,2128]{1,0:T(8,128)(2,1)}, u32[]{:S(2)}, u32[]{:S(2)}) collective-permute-start(bf16[144,2128]{1,0:T(8,128)(2,1)} %maximum_select_fusion.7), channel_id=1, source_target_pairs={{0,8},{4,12},{8,0},{12,4},{16,24},{20,28},{24,16},{28,20},{1,9},{5... | collective-permute-start | bytes 1838600 | tf_op jit(solution)/shard_map/ppermute | solution.py:188
  533.9 29.8 %collective-permute-start.32 = (bf16[144,832]{1,0:T(8,128)(2,1)}, bf16[144,832]{1,0:T(8,128)(2,1)}, u32[]{:S(2)}, u32[]{:S(2)}) collective-permute-start(bf16[144,832]{1,0:T(8,128)(2,1)} %get-tuple-element.375), channel_id=1, source_target_pairs={{0,8},{4,12},{8,0},{12,4},{16,24},{20,28},{24,16},{28,20},{1,9},{5... | collective-permute-start | bytes 718856 | tf_op jit(solution)/shard_map/ppermute | solution.py:188
  562.9 19.6 %collective-permute-start.26 = (bf16[144,2176]{1,0:T(8,128)(2,1)S(1)}, bf16[144,2176]{1,0:T(8,128)(2,1)}, u32[]{:S(2)}, u32[]{:S(2)}) collective-permute-start(bf16[144,2176]{1,0:T(8,128)(2,1)S(1)} %maximum_select_fusion.6), channel_id=1, source_target_pairs={{0,4},{4,0},{8,12},{12,8},{16,20},{20,16},{24,28},{28,24},{1,5},{5... | collective-permute-start | bytes 1880072 | tf_op jit(solution)/shard_map/ppermute | solution.py:188
  563.6 18.1 %collective-permute-start.31 = (bf16[144,896]{1,0:T(8,128)(2,1)S(1)}, bf16[144,896]{1,0:T(8,128)(2,1)S(1)}, u32[]{:S(2)}, u32[]{:S(2)}) collective-permute-start(bf16[144,896]{1,0:T(8,128)(2,1)S(1)} %get-tuple-element.377), channel_id=1, source_target_pairs={{0,4},{4,0},{8,12},{12,8},{16,20},{20,16},{24,28},{28,24},{1,5},{5... | collective-permute-start | bytes 774152 | tf_op jit(solution)/shard_map/ppermute | solution.py:188
  583.4 17.5 %collective-permute-start.43 = (f32[4,3380]{1,0:T(4,128)S(1)}, f32[4,3380]{1,0:T(4,128)S(1)}, u32[]{:S(2)}, u32[]{:S(2)}) collective-permute-start(f32[4,3380]{1,0:T(4,128)S(1)} %concatenate.189), channel_id=1, source_target_pairs={{0,1},{1,0},{2,3},{3,2},{4,5},{5,4},{6,7},{7,6},{8,9},{9,8},{10,11... | collective-permute-start | bytes 162248 | tf_op jit(solution)/shard_map/ppermute | solution.py:188
  584.7 17.6 %collective-permute-start.40 = (bf16[72,832]{1,0:T(8,128)(2,1)S(1)}, bf16[72,832]{1,0:T(8,128)(2,1)S(1)}, u32[]{:S(2)}, u32[]{:S(2)}) collective-permute-start(bf16[72,832]{1,0:T(8,128)(2,1)S(1)} %get-tuple-element.385), channel_id=1, source_target_pairs={{0,4},{4,0},{8,12},{12,8},{16,20},{20,16},{24,28},{28,24},{1,5},{5... | collective-permute-start | bytes 359432 | tf_op jit(solution)/shard_map/ppermute | solution.py:188
  586.4 17.6 %collective-permute-start.39 = (bf16[72,896]{1,0:T(8,128)(2,1)S(1)}, bf16[72,896]{1,0:T(8,128)(2,1)S(1)}, u32[]{:S(2)}, u32[]{:S(2)}) collective-permute-start(bf16[72,896]{1,0:T(8,128)(2,1)S(1)} %get-tuple-element.387), channel_id=1, source_target_pairs={{0,8},{4,12},{8,0},{12,4},{16,24},{20,28},{24,16},{28,20},{1,9},{5... | collective-permute-start | bytes 387080 | tf_op jit(solution)/shard_map/ppermute | solution.py:188
  587.8 17.4 %collective-permute-start.38 = (bf16[72,1152]{1,0:T(8,128)(2,1)S(1)}, bf16[72,1152]{1,0:T(8,128)(2,1)S(1)}, u32[]{:S(2)}, u32[]{:S(2)}) collective-permute-start(bf16[72,1152]{1,0:T(8,128)(2,1)S(1)} %add_convert_fusion.22), channel_id=1, source_target_pairs={{0,16},{4,20},{8,24},{12,28},{16,0},{20,4},{24,8},{28,12},{1,17},{... | collective-permute-start | bytes 497672 | tf_op jit(solution)/shard_map/ppermute | solution.py:188
  592.6 29.2 %collective-permute-start.37 = (bf16[144,2128]{1,0:T(8,128)(2,1)S(1)}, bf16[144,2128]{1,0:T(8,128)(2,1)S(1)}, u32[]{:S(2)}, u32[]{:S(2)}) collective-permute-start(bf16[144,2128]{1,0:T(8,128)(2,1)S(1)} %maximum_select_fusion.9), channel_id=1, source_target_pairs={{0,8},{4,12},{8,0},{12,4},{16,24},{20,28},{24,16},{28,20},{1,9},{5... | collective-permute-start | bytes 1838600 | tf_op jit(solution)/shard_map/ppermute | solution.py:188
  600.8 21.0 %collective-permute-start.36 = (bf16[144,2176]{1,0:T(8,128)(2,1)S(1)}, bf16[144,2176]{1,0:T(8,128)(2,1)S(1)}, u32[]{:S(2)}, u32[]{:S(2)}) collective-permute-start(bf16[144,2176]{1,0:T(8,128)(2,1)S(1)} %maximum_select_fusion.8), channel_id=1, source_target_pairs={{0,4},{4,0},{8,12},{12,8},{16,20},{20,16},{24,28},{28,24},{1,5},{5... | collective-permute-start | bytes 1880072 | tf_op jit(solution)/shard_map/ppermute | solution.py:188
  602.2 13.6 %collective-permute-start.42 = (bf16[144,832]{1,0:T(8,128)(2,1)S(1)}, bf16[144,832]{1,0:T(8,128)(2,1)S(1)}, u32[]{:S(2)}, u32[]{:S(2)}) collective-permute-start(bf16[144,832]{1,0:T(8,128)(2,1)S(1)} %get-tuple-element.371), channel_id=1, source_target_pairs={{0,8},{4,12},{8,0},{12,4},{16,24},{20,28},{24,16},{28,20},{1,9},{5... | collective-permute-start | bytes 718856 | tf_op jit(solution)/shard_map/ppermute | solution.py:188
  604.0 17.8 %collective-permute-start.41 = (bf16[144,896]{1,0:T(8,128)(2,1)S(1)}, bf16[144,896]{1,0:T(8,128)(2,1)S(1)}, u32[]{:S(2)}, u32[]{:S(2)}) collective-permute-start(bf16[144,896]{1,0:T(8,128)(2,1)S(1)} %get-tuple-element.373), channel_id=1, source_target_pairs={{0,4},{4,0},{8,12},{12,8},{16,20},{20,16},{24,28},{28,24},{1,5},{5... | collective-permute-start | bytes 774152 | tf_op jit(solution)/shard_map/ppermute | solution.py:188
  622.5 9.5 %collective-permute-start.48 = (bf16[72,832]{1,0:T(8,128)(2,1)S(1)}, bf16[72,832]{1,0:T(8,128)(2,1)S(1)}, u32[]{:S(2)}, u32[]{:S(2)}) collective-permute-start(bf16[72,832]{1,0:T(8,128)(2,1)S(1)} %get-tuple-element.381), channel_id=1, source_target_pairs={{0,4},{4,0},{8,12},{12,8},{16,20},{20,16},{24,28},{28,24},{1,5},{5... | collective-permute-start | bytes 359432 | tf_op jit(solution)/shard_map/ppermute | solution.py:188
  623.5 11.5 %collective-permute-start.47 = (bf16[72,896]{1,0:T(8,128)(2,1)S(1)}, bf16[72,896]{1,0:T(8,128)(2,1)S(1)}, u32[]{:S(2)}, u32[]{:S(2)}) collective-permute-start(bf16[72,896]{1,0:T(8,128)(2,1)S(1)} %get-tuple-element.383), channel_id=1, source_target_pairs={{0,8},{4,12},{8,0},{12,4},{16,24},{20,28},{24,16},{28,20},{1,9},{5... | collective-permute-start | bytes 387080 | tf_op jit(solution)/shard_map/ppermute | solution.py:188
  625.3 9.5 %collective-permute-start.46 = (bf16[72,832]{1,0:T(8,128)(2,1)S(1)}, bf16[72,832]{1,0:T(8,128)(2,1)S(1)}, u32[]{:S(2)}, u32[]{:S(2)}) collective-permute-start(bf16[72,832]{1,0:T(8,128)(2,1)S(1)} %add_convert_fusion.29), channel_id=1, source_target_pairs={{0,16},{4,20},{8,24},{12,28},{16,0},{20,4},{24,8},{28,12},{1,17},{... | collective-permute-start | bytes 359432 | tf_op jit(solution)/shard_map/ppermute | solution.py:188
  625.7 12.5 %collective-permute-start.45 = (bf16[72,896]{1,0:T(8,128)(2,1)S(1)}, bf16[72,896]{1,0:T(8,128)(2,1)S(1)}, u32[]{:S(2)}, u32[]{:S(2)}) collective-permute-start(bf16[72,896]{1,0:T(8,128)(2,1)S(1)} %add_convert_fusion.30), channel_id=1, source_target_pairs={{0,16},{4,20},{8,24},{12,28},{16,0},{20,4},{24,8},{28,12},{1,17},{... | collective-permute-start | bytes 387080 | tf_op jit(solution)/shard_map/ppermute | solution.py:188
  629.1 10.0 %collective-permute-start.44 = (bf16[72,1152]{1,0:T(8,128)(2,1)S(1)}, bf16[72,1152]{1,0:T(8,128)(2,1)S(1)}, u32[]{:S(2)}, u32[]{:S(2)}) collective-permute-start(bf16[72,1152]{1,0:T(8,128)(2,1)S(1)} %add_convert_fusion.21), channel_id=1, source_target_pairs={{0,8},{4,12},{8,0},{12,4},{16,24},{20,28},{24,16},{28,20},{1,9},{5... | collective-permute-start | bytes 497672 | tf_op jit(solution)/shard_map/ppermute | solution.py:188
  632.1 18.4 %collective-permute-start.33 = (bf16[2,184,1152]{2,1,0:T(8,128)(2,1)S(1)}, bf16[2,184,1152]{2,1,0:T(8,128)(2,1)S(1)}, u32[]{:S(2)}, u32[]{:S(2)}) collective-permute-start(bf16[2,184,1152]{2,1,0:T(8,128)(2,1)S(1)} %get-tuple-element.339), channel_id=1, source_target_pairs={{0,4},{4,0},{8,12},{12,8},{16,20},{20,16},{24,28},{28,24},{1,5},{5... | collective-permute-start | bytes 2543624 | tf_op jit(solution)/shard_map/ppermute | solution.py:188
  634.8 28.0 %collective-permute-start.34 = (bf16[2,184,1152]{2,1,0:T(8,128)(2,1)S(1)}, bf16[2,184,1152]{2,1,0:T(8,128)(2,1)S(1)}, u32[]{:S(2)}, u32[]{:S(2)}) collective-permute-start(bf16[2,184,1152]{2,1,0:T(8,128)(2,1)S(1)} %get-tuple-element.338), channel_id=1, source_target_pairs={{0,8},{4,12},{8,0},{12,4},{16,24},{20,28},{24,16},{28,20},{1,9},{5... | collective-permute-start | bytes 2543624 | tf_op jit(solution)/shard_map/ppermute | solution.py:188
  635.0 45.2 %collective-permute-start.35 = (bf16[2,184,1152]{2,1,0:T(8,128)(2,1)S(1)}, bf16[2,184,1152]{2,1,0:T(8,128)(2,1)S(1)}, u32[]{:S(2)}, u32[]{:S(2)}) collective-permute-start(bf16[2,184,1152]{2,1,0:T(8,128)(2,1)S(1)} %get-tuple-element.337), channel_id=1, source_target_pairs={{0,12},{4,8},{8,4},{12,0},{16,28},{20,24},{24,20},{28,16},{1,13},{... | collective-permute-start | bytes 2543624 | tf_op jit(solution)/shard_map/ppermute | solution.py:188
  639.2 25.1 %collective-permute-start.55 = (f32[4,3380]{1,0:T(4,128)S(1)}, f32[4,3380]{1,0:T(4,128)S(1)}, u32[]{:S(2)}, u32[]{:S(2)}) collective-permute-start(f32[4,3380]{1,0:T(4,128)S(1)} %add.447), channel_id=1, source_target_pairs={{0,4},{4,0},{8,12},{12,8},{16,20},{20,16},{24,28},{28,24},{1,5},{5... | collective-permute-start | bytes 162248 | tf_op jit(solution)/shard_map/ppermute | solution.py:188
  640.4 39.9 %collective-permute-start.54 = (bf16[72,832]{1,0:T(8,128)(2,1)S(1)}, bf16[72,832]{1,0:T(8,128)(2,1)S(1)}, u32[]{:S(2)}, u32[]{:S(2)}) collective-permute-start(bf16[72,832]{1,0:T(8,128)(2,1)S(1)} %add_convert_fusion.25), channel_id=1, source_target_pairs={{0,16},{4,20},{8,24},{12,28},{16,0},{20,4},{24,8},{28,12},{1,17},{... | collective-permute-start | bytes 359432 | tf_op jit(solution)/shard_map/ppermute | solution.py:188
  650.4 39.1 %collective-permute-start.53 = (bf16[72,896]{1,0:T(8,128)(2,1)S(1)}, bf16[72,896]{1,0:T(8,128)(2,1)S(1)}, u32[]{:S(2)}, u32[]{:S(2)}) collective-permute-start(bf16[72,896]{1,0:T(8,128)(2,1)S(1)} %add_convert_fusion.26), channel_id=1, source_target_pairs={{0,16},{4,20},{8,24},{12,28},{16,0},{20,4},{24,8},{28,12},{1,17},{... | collective-permute-start | bytes 387080 | tf_op jit(solution)/shard_map/ppermute | solution.py:188
  662.8 26.7 %collective-permute-start.50 = (bf16[144,1152]{1,0:T(8,128)(2,1)S(1)}, bf16[144,1152]{1,0:T(8,128)(2,1)S(1)}, u32[]{:S(2)}, u32[]{:S(2)}) collective-permute-start(bf16[144,1152]{1,0:T(8,128)(2,1)S(1)} %maximum_select_fusion.14), channel_id=1, source_target_pairs={{0,4},{4,0},{8,12},{12,8},{16,20},{20,16},{24,28},{28,24},{1,5},{5... | collective-permute-start | bytes 995336 | tf_op jit(solution)/shard_map/ppermute | solution.py:188
  664.3 25.3 %collective-permute-start.52 = (bf16[72,832]{1,0:T(8,128)(2,1)S(1)}, bf16[72,832]{1,0:T(8,128)(2,1)S(1)}, u32[]{:S(2)}, u32[]{:S(2)}) collective-permute-start(bf16[72,832]{1,0:T(8,128)(2,1)S(1)} %add_convert_fusion.27), channel_id=1, source_target_pairs={{0,4},{4,0},{8,12},{12,8},{16,20},{20,16},{24,28},{28,24},{1,5},{5... | collective-permute-start | bytes 359432 | tf_op jit(solution)/shard_map/ppermute | solution.py:188
  680.2 9.3 %collective-permute-start.51 = (bf16[72,896]{1,0:T(8,128)(2,1)S(1)}, bf16[72,896]{1,0:T(8,128)(2,1)S(1)}, u32[]{:S(2)}, u32[]{:S(2)}) collective-permute-start(bf16[72,896]{1,0:T(8,128)(2,1)S(1)} %add_convert_fusion.28), channel_id=1, source_target_pairs={{0,8},{4,12},{8,0},{12,4},{16,24},{20,28},{24,16},{28,20},{1,9},{5... | collective-permute-start | bytes 387080 | tf_op jit(solution)/shard_map/ppermute | solution.py:188
  692.9 8.7 %collective-permute-start.57 = (bf16[144,832]{1,0:T(8,128)(2,1)S(1)}, bf16[144,832]{1,0:T(8,128)(2,1)S(1)}, u32[]{:S(2)}, u32[]{:S(2)}) collective-permute-start(bf16[144,832]{1,0:T(8,128)(2,1)S(1)} %maximum_select_fusion.16), channel_id=1, source_target_pairs={{0,8},{4,12},{8,0},{12,4},{16,24},{20,28},{24,16},{28,20},{1,9},{5... | collective-permute-start | bytes 718856 | tf_op jit(solution)/shard_map/ppermute | solution.py:188
  701.8 9.1 %collective-permute-start.61 = (bf16[144,896]{1,0:T(8,128)(2,1)S(1)}, bf16[144,896]{1,0:T(8,128)(2,1)S(1)}, u32[]{:S(2)}, u32[]{:S(2)}) collective-permute-start(bf16[144,896]{1,0:T(8,128)(2,1)S(1)} %maximum_select_fusion.17), channel_id=1, source_target_pairs={{0,4},{4,0},{8,12},{12,8},{16,20},{20,16},{24,28},{28,24},{1,5},{5... | collective-permute-start | bytes 774152 | tf_op jit(solution)/shard_map/ppermute | solution.py:188
  (97 other events, 1341.2 us)
Sparse Core Ops, SparseCore 0:
  10.3 58.8 all-gather.4
  70.7 25.7 all-gather.6
  98.1 67.6 all-gather.8
  167.2 67.6 all-gather.10
  237.2 82.2 reduce-scatter.5
  322.0 82.2 reduce-scatter.7
  423.4 33.0 reduce-scatter.9
  459.9 44.1 reduce-scatter.11
  521.7 43.2 reduce-scatter.13

commit v3 on v2

v3 whole, which is shorter than its diff:
```python
import math

import jax
import jax.numpy as jnp
from jax import lax
from jax.experimental import pallas as pl
from jax.experimental.layout import Layout, with_layout_constraint
from jax.experimental.pallas import tpu as pltpu
from jax.sharding import PartitionSpec as P

HD = 72
SEQ = 736
EPS = 1e-06
SCALE = 1.0 / math.sqrt(HD)
SCALE_LOG2 = SCALE * math.log2(math.e)
HEAD_GROUPS = ((0, 8), (8, 8))
STEP_HEADS = 4

GELU_A = math.sqrt(2 / math.pi)
GELU_B = 0.044715 * GELU_A

f32 = jnp.float32
bf16 = jnp.bfloat16


def dot2(a, b, ca, cb):
    return lax.dot_general(a, b, (((ca,), (cb,)), ((), ())), preferred_element_type=f32)


def split3(v):
    high = v.astype(bf16).astype(f32)
    mid = (v - high).astype(bf16).astype(f32)
    return [high, mid, v - high - mid]


def rows8(rows, length):
    row = lax.broadcasted_iota(jnp.int32, (8, length), 0)
    out = jnp.zeros((8, length), f32)
    for j, value in enumerate(rows):
        out = jnp.where(row == j, value, out)
    return out


def attend_forward_kernel(q_ref, k_ref, v_ref, mask_ref, context_ref, lse_ref):
    length = q_ref.shape[-1]
    bias = jnp.where(mask_ref[0] > 0, 0.0, -1e30).astype(f32)
    key_rows = rows8([bias], length)
    query_rows = rows8([jnp.ones((1, length), f32)], length)
    zeros = jnp.zeros((8, length), f32)
    ones = jnp.ones((8, length), f32)
    for h in range(STEP_HEADS):
        rows = slice(h * HD, (h + 1) * HD)
        keys = k_ref[0, rows].astype(f32)
        key_side = jnp.concatenate([keys, key_rows, keys, zeros], 0).T.astype(bf16)
        scaled = q_ref[0, rows].astype(f32) * SCALE_LOG2
        high = scaled.astype(bf16).astype(f32)
        query_side = jnp.concatenate([high, query_rows, scaled - high, zeros], 0).astype(bf16)
        value_side = jnp.concatenate([v_ref[0, rows].astype(f32), ones], 0).astype(bf16)
        scores = dot2(key_side, query_side, 1, 0)
        top = jnp.max(scores, 0, keepdims=True)
        probs = jnp.exp2(scores - top).astype(bf16)
        summed = dot2(value_side, probs, 1, 0)
        total = summed[HD : HD + 1]
        context_ref[0, rows] = (summed[:HD] * (1.0 / total)).astype(bf16)
        lse_ref[0, h] = top + jnp.log2(total)


def attend_forward(projected, mask):
    images, features, length = projected.shape
    width = features // 3
    heads = width // HD
    steps = heads // STEP_HEADS
    rows = STEP_HEADS * HD
    sources = [
        pl.BlockSpec((1, rows, length), lambda i, h, which=which: (i, which * steps + h, 0))
        for which in range(3)
    ]
    return pl.pallas_call(
        attend_forward_kernel,
        grid=(images, steps),
        in_specs=sources + [pl.BlockSpec((1, 1, length), lambda i, h: (i, 0, 0))],
        out_specs=[
            pl.BlockSpec((1, rows, length), lambda i, h: (i, h, 0)),
            pl.BlockSpec((1, STEP_HEADS, 1, length), lambda i, h: (i, h, 0, 0)),
        ],
        out_shape=[
            jax.ShapeDtypeStruct((images, width, length), bf16),
            jax.ShapeDtypeStruct((images, heads, 1, length), f32),
        ],
        compiler_params=pltpu.CompilerParams(vmem_limit_bytes=50 << 20),
        cost_estimate=pl.CostEstimate(
            flops=images * heads * length * length * 1024,
            bytes_accessed=images * width * length * 8,
            transcendentals=images * heads * length * length,
        ),
        name="attend_forward",
    )(projected, projected, projected, mask)


def attend_backward_kernel(
    q_ref, k_ref, v_ref, context_ref, grad_ref, lse_ref, mask_ref, *rest
):
    all_ref, out_ref = rest[-2:]
    length = q_ref.shape[-1]
    bias = jnp.where(mask_ref[0] > 0, 0.0, -1e30).astype(f32)
    one = jnp.ones((1, length), f32)
    key_rows = rows8([bias, one, one, one], length)
    value_rows = rows8([one, one, one], length)
    zeros = jnp.zeros((8, length), f32)
    for h in range(STEP_HEADS):
        rows = slice(h * HD, (h + 1) * HD)
        key_low = k_ref[0, rows]
        keys = key_low.astype(f32)
        key_side = jnp.concatenate([keys, key_rows, keys, zeros], 0).T.astype(bf16)
        queries = q_ref[0, rows].astype(f32)
        scaled = queries * SCALE_LOG2
        high = scaled.astype(bf16).astype(f32)
        query_side = jnp.concatenate(
            [high, rows8([one] + split3(-lse_ref[0, h]), length), scaled - high, zeros], 0
        ).astype(bf16)
        grads = grad_ref[0, rows].astype(f32)
        row_dot = jnp.sum(grads * context_ref[0, rows].astype(f32), 0, keepdims=True)
        grad_side = jnp.concatenate([grads, rows8(split3(-row_dot), length)], 0).astype(bf16)
        value_side = jnp.concatenate([v_ref[0, rows].astype(f32), value_rows], 0).T.astype(bf16)
        probs = jnp.exp2(dot2(key_side, query_side, 1, 0))
        score_grads = (probs * dot2(value_side, grad_side, 1, 0)).astype(bf16)
        dq = dot2(key_low, score_grads, 1, 0) * SCALE
        dk = (dot2(score_grads, queries.T.astype(bf16), 1, 0) * SCALE).T
        dv = dot2(probs.astype(bf16), grads.T.astype(bf16), 1, 0).T
        for which, value in enumerate((dq, dk, dv)):
            out_ref[0, which, rows] = value.astype(bf16)
            all_ref[0, which, rows] = value.astype(bf16)


def attend_backward(projected, context, grads, lse, mask, step, group, held_all, held_part):
    images, features, length = projected.shape
    heads = features // (3 * HD)
    steps = heads // STEP_HEADS
    rows = STEP_HEADS * HD
    first, count = (v // STEP_HEADS for v in group)
    block = pl.BlockSpec((1, rows, length), lambda i: (i, step, 0))
    sources = [
        pl.BlockSpec((1, rows, length), lambda i, which=which: (i, which * steps + step, 0))
        for which in range(3)
    ]
    held = [v for v in (held_all, held_part) if v is not None]
    aliases = {7 + k: k for k in range(len(held))}
    return pl.pallas_call(
        attend_backward_kernel,
        grid=(images,),
        in_specs=sources
        + [
            block,
            block,
            pl.BlockSpec((1, STEP_HEADS, 1, length), lambda i: (i, step, 0, 0)),
            pl.BlockSpec((1, 1, length), lambda i: (i, 0, 0)),
        ]
        + [pl.BlockSpec(memory_space=pl.ANY)] * len(held),
        out_specs=[
            pl.BlockSpec((1, 3, rows, length), lambda i: (i, 0, step, 0)),
            pl.BlockSpec((1, 3, rows, length), lambda i: (i, 0, step - first, 0)),
        ],
        out_shape=[
            jax.ShapeDtypeStruct((images, 3, n * rows, length), bf16) for n in (steps, count)
        ],
        input_output_aliases=aliases,
        compiler_params=pltpu.CompilerParams(vmem_limit_bytes=50 << 20),
        cost_estimate=pl.CostEstimate(
            flops=images * STEP_HEADS * length * length * 25600,
            bytes_accessed=images * rows * length * 22,
            transcendentals=images * STEP_HEADS * length * length,
        ),
        name="attend_backward",
    )(projected, projected, projected, context, grads, lse, mask, *held)


def swap(values, axis, bits):
    return lax.ppermute(values, axis, [(i, i ^ bits) for i in range(lax.axis_size(axis))])


def take_block(values, index, size):
    return lax.dynamic_slice_in_dim(values, index * size, size, 0)


def exchange(blocks):
    group, count = blocks.shape[0], lax.axis_size("seq")
    groups = [list(range(k, k + group)) for k in range(0, count, group)]
    return lax.all_to_all(blocks, "seq", 0, 0, axis_index_groups=groups)


def tokens_to_images(tokens, group):
    rows, local, width = tokens.shape
    blocks = exchange(tokens.reshape(group, rows // group, local, width))
    return jnp.swapaxes(blocks, 0, 1).reshape(rows // group, group * local, width)


def images_to_tokens(images, group):
    share, length, width = images.shape
    blocks = jnp.swapaxes(images.reshape(share, group, length // group, width), 0, 1)
    return exchange(blocks).reshape(share * group, length // group, width)


def gather_small(local):
    me = lax.axis_index("fsdp")
    count = lax.axis_size("fsdp")
    held = local[None]
    bit = 1
    while bit < count:
        held = jnp.concatenate([held, swap(held, "fsdp", bit)], 0)
        bit *= 2
    return jnp.concatenate([take_block(held, me ^ j, 1) for j in range(count)], 0)


def sum_chain(values, group):
    for axis, step in (("fsdp", 1), ("seq", 1), ("seq", group)):
        count = lax.axis_size(axis)
        reach = count if axis == "fsdp" else group if step == 1 else count // group
        if reach > 1:
            flight = yield [values] + [swap(values, axis, step * j) for j in range(1, reach)]
            values = sum(flight[1:], flight[0])
    return values


def in_order(pieces, member):
    bit = 1
    while bit < len(pieces):
        here = (member // bit) % 2
        pieces = [
            jnp.where(here == 0, piece, pieces[k ^ bit]) for k, piece in enumerate(pieces)
        ]
        bit *= 2
    return jnp.concatenate(pieces, 0)


def rows_first(values):
    return with_layout_constraint(values, Layout((0, 1)))


def sum_pieces(wholes, group, member, piece):
    flight = yield [
        [swap(take_block(whole, member ^ j, piece), "seq", j) if j else whole for j in range(group)]
        for whole in wholes
    ]
    return [
        sum((v.astype(f32) for v in came), take_block(whole, member, piece).astype(f32)).astype(bf16)
        for whole, *came in flight
    ]


def reduce_chain(fulls, group, calls=()):
    wholes = yield [
        lax.psum_scatter(full, "fsdp", scatter_dimension=0, tiled=True) for full in fulls
    ]
    member = lax.axis_index("seq") % group
    piece = wholes[0].shape[0] // group
    if 1 in calls:
        flight = yield [exchange(whole.reshape(group, piece, -1)) for whole in wholes]
        parts = [jnp.sum(came.astype(f32), 0).astype(bf16) for came in flight]
    else:
        parts = yield from sum_pieces(wholes, group, member, piece)
    bit = group
    while bit < lax.axis_size("seq"):
        if 2 in calls:
            pairs = [[i, i ^ bit] for i in range(lax.axis_size("seq")) if not i & bit]
            flight = yield [
                lax.all_to_all(
                    jnp.broadcast_to(part, (2, *part.shape)), "seq", 0, 0, axis_index_groups=pairs
                )
                for part in parts
            ]
        else:
            flight = yield [(part, swap(part, "seq", bit)) for part in parts]
        parts = [(came[0].astype(f32) + came[1].astype(f32)).astype(bf16) for came in flight]
        bit *= 2
    if 3 in calls:
        flight = yield [exchange(jnp.broadcast_to(part, (group, *part.shape))) for part in parts]
        return [came.reshape(group * piece, -1).astype(f32) for came in flight]
    flight = yield [
        [swap(part, "seq", j) if j else part for j in range(group)] for part in parts
    ]
    return [in_order(pieces, member).astype(f32) for pieces in flight]


def gather_chain(weight):
    if lax.axis_size("fsdp") != 4:
        return (yield lax.all_gather(weight, "fsdp", axis=0, tiled=True))
    sibling, far = yield (swap(weight, "fsdp", 1), swap(weight, "fsdp", 2))
    (far_sibling,) = yield (swap(far, "fsdp", 1),)
    return rows_first(in_order([weight, sibling, far, far_sibling], lax.axis_index("fsdp")))


class Flow:
    def __init__(self):
        self.chains, self.pending, self.results = {}, {}, {}

    def start(self, name, chain):
        self.chains[name], self.pending[name] = chain, next(chain)

    def point(self, main, *names):
        names = [name for name in names if name in self.pending]
        main, ended = lax.optimization_barrier((main, [self.pending[n] for n in names]))
        for name, values in zip(names, ended):
            self.advance(name, values)
        return main

    def hold(self, main, *names):
        main, ended = lax.optimization_barrier((main, [self.pending[n] for n in names]))
        self.pending.update(zip(names, ended))
        return main

    def advance(self, name, values):
        try:
            self.pending[name] = self.chains[name].send(values)
        except StopIteration as end:
            self.results[name] = end.value
            del self.pending[name]

    def finish(self):
        while self.pending:
            self.point((), *self.pending)


def ungroup(parts, which):
    return jnp.concatenate(
        [
            part[..., which * heads * HD : (which + 1) * heads * HD]
            for part, (_, heads) in zip(parts, HEAD_GROUPS)
        ],
        -1,
    )


def norm_parts(values):
    center = values - jnp.mean(values, -1, keepdims=True)
    spread = jnp.mean(center * center, -1, keepdims=True)
    scale = lax.rsqrt(spread + EPS)
    return center * scale, scale


def norm_grad(grad, hat, scale, gain):
    e = grad * gain
    return scale * (
        e - jnp.mean(e, -1, keepdims=True) - hat * jnp.mean(e * hat, -1, keepdims=True)
    )


def ein(spec, a, b):
    return jnp.einsum(spec, a, b, preferred_element_type=f32)


def token_sum(values):
    return jnp.sum(values.astype(f32), (0, 1))


def body(
    patches,
    key_mask,
    attn_norm_gain,
    attn_norm_bias,
    query_weight,
    query_bias,
    key_weight,
    value_weight,
    value_bias,
    out_weight,
    out_bias,
    mlp_norm_gain,
    mlp_norm_bias,
    up_weight,
    up_bias,
    down_weight,
    down_bias,
    cotangent,
):
    rows, local, width = patches.shape
    group = SEQ // local
    share = rows // group
    shard = lax.axis_index("fsdp")
    seq = lax.axis_index("seq")
    member = seq % group

    flow = Flow()
    inputs_low = tokens_to_images(patches, group)

    small = [
        attn_norm_gain,
        attn_norm_bias,
        query_bias,
        value_bias,
        out_bias,
        mlp_norm_gain,
        mlp_norm_bias,
        down_bias,
        up_bias,
    ]
    gathered = gather_small(jnp.concatenate(small)).astype(f32)
    starts = [0]
    for v in small:
        starts.append(starts[-1] + v.shape[0])
    (
        first_gain,
        first_shift,
        query_shift,
        value_shift,
        out_shift,
        second_gain,
        second_shift,
        down_shift,
        up_shift,
    ) = (gathered[:, a:b].reshape(-1) for a, b in zip(starts[:-1], starts[1:]))

    def whole(weight):
        return lax.all_gather(weight, "fsdp", axis=0, tiled=True)

    project_full = whole(jnp.concatenate([query_weight, key_weight, value_weight], 1))
    project_shift = jnp.concatenate([query_shift, jnp.zeros_like(query_shift), value_shift])
    inputs_low, out_local = lax.optimization_barrier((inputs_low, out_weight))
    flow.start("out_weight", gather_chain(out_local))
    up_full = whole(up_weight)
    down_full = whole(down_weight.T)

    image_mask = lax.dynamic_slice(
        key_mask, (member * share, (seq // group) * SEQ), (share, SEQ)
    )
    key_keep = image_mask[:, None, :]

    inputs = inputs_low.astype(f32)
    hat_one, _ = norm_parts(inputs)
    normed_one = (hat_one * first_gain + first_shift).astype(bf16)
    projected = (ein("itd,dm->imt", normed_one, project_full) + project_shift[:, None]).astype(
        bf16
    )
    projected, cotangent = flow.point((projected, cotangent), "out_weight")
    cotangent_low = tokens_to_images(cotangent, group)
    context, lse = attend_forward(projected, key_keep)
    if "out_weight" in flow.pending:
        context, lse = flow.point((context, lse), "out_weight")
    out_full = flow.results["out_weight"]
    hidden = inputs + ein("int,nd->itd", context, out_full) + out_shift
    hat_two, scale_two = norm_parts(hidden)
    normed_two = (hat_two * second_gain + second_shift).astype(bf16)
    pre = ein("itd,df->itf", normed_two, up_full) + up_shift
    square = pre * pre
    tanh = jnp.tanh(pre * (GELU_A + GELU_B * square))
    half_pre = 0.5 * pre
    active, slope = lax.optimization_barrier(
        (
            (half_pre + half_pre * tanh).astype(bf16),
            (
                0.5 + 0.5 * tanh + half_pre * (1.0 - tanh * tanh) * (GELU_A + 3 * GELU_B * square)
            ).astype(bf16),
        )
    )
    out_grad_low = jnp.where(image_mask[:, :, None] > 0, cotangent_low, 0).astype(bf16)
    down_grad = rows_first(ein("itd,itf->df", out_grad_low, active).astype(bf16))
    down_bias_grad = token_sum(out_grad_low)
    active, slope, out_grad_low, down_grad = flow.point((active, slope, out_grad_low, down_grad))
    flow.start("down", reduce_chain([down_grad], group, (1,)))
    output = (hidden + ein("itf,df->itd", active, down_full) + down_shift).astype(bf16)
    output, slope = flow.point((output, slope))
    output = images_to_tokens(output, group)
    pre_grad = (ein("itd,df->itf", out_grad_low, down_full) * slope.astype(f32)).astype(bf16)
    up_bias_grad = token_sum(pre_grad)
    up_grad = rows_first(ein("itd,itf->df", normed_two, pre_grad).astype(bf16))
    pre_grad, up_grad, output = flow.point((pre_grad, up_grad, output))
    flow.start("up", reduce_chain([up_grad], group, (1, 2, 3)))
    normed_two_grad = ein("itf,df->itd", pre_grad, up_full)
    hidden_grad = out_grad_low.astype(f32) + norm_grad(
        normed_two_grad, hat_two, scale_two, second_gain
    )
    second_gain_grad = jnp.sum(normed_two_grad * hat_two, (0, 1))
    second_shift_grad = jnp.sum(normed_two_grad, (0, 1))
    hidden_grad, output = flow.point((hidden_grad, output), "down")

    attn_grad_low = hidden_grad.astype(bf16)
    context_grad = ein("nd,itd->int", out_full, attn_grad_low).astype(bf16)
    out_grad = rows_first(ein("int,itd->nd", context, attn_grad_low).astype(bf16))
    out_bias_grad = token_sum(attn_grad_low)
    context_grad, out_grad = flow.point((context_grad, out_grad), "down")
    grads, parts = None, []
    per_group = HEAD_GROUPS[0][1] // STEP_HEADS
    points = ((), ("down", "up"), ("up",), ("up",))
    for step in range(len(HEAD_GROUPS) * per_group):
        number, inside = divmod(step, per_group)
        grads, part = attend_backward(
            projected,
            context,
            context_grad,
            lse,
            key_keep,
            step,
            HEAD_GROUPS[number],
            grads,
            part if inside else None,
        )
        grads, part, context_grad = flow.point((grads, part, context_grad), *points[step])
        if inside == per_group - 1:
            part = part.reshape(part.shape[0], -1, SEQ)
            parts.append(part)
            weight_grad = rows_first(ein("itd,imt->dm", normed_one, part).astype(bf16))
            grads, weight_grad, context_grad = flow.point(
                (grads, weight_grad, context_grad), *(["out_a"] if number else [])
            )
            if number:
                flow.start("b", reduce_chain([weight_grad], group))
            else:
                flow.start("out_a", reduce_chain([out_grad, weight_grad], group))
    bias_grads = [jnp.sum(part.astype(f32), (0, 2)) for part in parts]
    normed_one_grad = ein("imt,dm->itd", grads.reshape(projected.shape), project_full)
    query_bias_grad, value_bias_grad = ungroup(bias_grads, 0), ungroup(bias_grads, 2)
    hat_one, scale_one = norm_parts(inputs_low.astype(f32))
    first_gain_grad = jnp.sum(normed_one_grad * hat_one, (0, 1))
    first_shift_grad = jnp.sum(normed_one_grad, (0, 1))
    input_grad = (
        hidden_grad + norm_grad(normed_one_grad, hat_one, scale_one, first_gain)
    ).astype(bf16)
    small_grads = [
        first_gain_grad,
        first_shift_grad,
        query_bias_grad,
        value_bias_grad,
        out_bias_grad,
        second_gain_grad,
        second_shift_grad,
        down_bias_grad,
        up_bias_grad,
    ]
    input_grad, small_grads = flow.point(
        (input_grad, small_grads), "down", "up", "out_a", "b"
    )
    input_grad = images_to_tokens(input_grad, group)
    count = lax.axis_size("fsdp")
    packed = jnp.concatenate([v.reshape(count, -1) for v in small_grads], 1)
    flow.start("small", sum_chain(packed, group))
    flow.point((), "out_a", "b", "small")
    input_grad = flow.point(input_grad, *flow.pending)
    flow.finish()
    sums = flow.results
    (up_owned,), (down_owned,), (out_owned, part_a), (part_b,) = (
        sums[name] for name in ("up", "down", "out_a", "b")
    )
    down_owned = down_owned.T
    query_owned, key_owned, value_owned = (
        ungroup([part_a, part_b], which) for which in range(3)
    )

    packed = take_block(sums["small"], shard, 1)[0]
    (
        first_gain_owned,
        first_shift_owned,
        query_bias_owned,
        value_bias_owned,
        out_bias_owned,
        second_gain_owned,
        second_shift_owned,
        down_bias_owned,
        up_bias_owned,
    ) = (packed[a:b] for a, b in zip(starts[:-1], starts[1:]))
    return (
        output,
        input_grad,
        first_gain_owned,
        first_shift_owned,
        query_owned,
        query_bias_owned,
        key_owned,
        value_owned,
        value_bias_owned,
        out_owned,
        out_bias_owned,
        second_gain_owned,
        second_shift_owned,
        up_owned,
        up_bias_owned,
        down_owned,
        down_bias_owned,
    )


def solution(mesh):
    tokens, vector, matrix = P("fsdp", "seq", None), P("fsdp"), P("fsdp", None)
    in_specs = (
        tokens,
        matrix,
        vector,
        vector,
        matrix,
        vector,
        matrix,
        matrix,
        vector,
        matrix,
        vector,
        vector,
        vector,
        matrix,
        vector,
        P(None, "fsdp"),
        vector,
        tokens,
    )
    out_specs = (
        tokens,
        tokens,
        vector,
        vector,
        matrix,
        vector,
        matrix,
        matrix,
        vector,
        matrix,
        vector,
        vector,
        vector,
        matrix,
        vector,
        P(None, "fsdp"),
        vector,
    )
    return jax.shard_map(body, mesh=mesh, in_specs=in_specs, out_specs=out_specs, check_vma=False)
```

time: 734 us -> 704 us (0.959)
  local copies, waits for them, and re-layouts: 65.3 us -> 45.2 us
  starting transfers between devices: 70.3 us -> 79.9 us
    all_to_all x0 -> x8, waiting for transfers between devices: none -> 48.7 us  [the longest x7 35.2 us: exchange(): return lax.all_to_all(blocks, 'seq', 0, 0, axis_index_groups=groups)]
    ppermute x64 -> x37, waiting for transfers between devices: 116 us -> 75.8 us  [swap(): lax.ppermute(values, axis, [(i, i ^ bits) for i in range(lax.axis_size(ax...]
    all_to_all x0 -> x8, starting transfers between devices: none -> 36.8 us  [the longest x7 32.2 us: exchange(): return lax.all_to_all(blocks, 'seq', 0, 0, axis_index_groups=groups)]
    ppermute x64 -> x37, starting transfers between devices: 70 us -> 42.7 us  [swap(): lax.ppermute(values, axis, [(i, i ^ bits) for i in range(lax.axis_size(ax...]
    dynamic_slice x21 -> x4, local copies, waits for them, and re-layouts: 20.5 us -> 1.3 us  [take_block(): return lax.dynamic_slice_in_dim(values, index * size, size, 0)]
    all_gather x4 -> x3, waiting for transfers between devices: 36.6 us -> 22 us  [whole(): return lax.all_gather(weight, 'fsdp', axis=0, tiled=True)]
    convert_element_type x32 -> x12, other arithmetic: 27 us -> 13.4 us  [the longest x5 4.78 us: reduce_chain(): (came[0].astype(f32) + came[1].astype(f32)).astype(bf16)]
    slice x15 -> x0, local copies, waits for them, and re-layouts: 9.55 us -> none  [the longest x13 7.42 us: reduce_chain(): values[:, p * cut:min((p + 1) * cut, width)]]
  transfers between devices with their start and end apart: 73 -> 53, of which waited for: 23 -> 23; matrix products, arithmetic and copies ran while one was open for 51% -> 48% of each run, Pallas kernels for 13% -> 12%
where the time goes in v3:
time: 704 us; the launch traced here: 696 us
  matrix products  248 us (35%)
  waiting for transfers between devices  148 us (21%)
  Pallas kernels  85.8 us (12%)
  starting transfers between devices  79.9 us (11%)
  other arithmetic  73.3 us (10%)
  local copies, waits for them, and re-layouts  45.2 us (6%)
  between operations  15.5 us (2%)
    dot_general x13, matrix products, ein(): return jnp.einsum(spec, a, b, preferred_element_type=f32)  248 us
    ppermute x37, waiting for transfers between devices, swap(): lax.ppermute(values, axis, [(i, i ^ bits) for i in range(lax.axis_size(ax...  75.8 us
    pallas_call x4, Pallas kernels, attend_backward(): pl.pallas_call(attend_backward_kernel, grid=(images,), in_specs=sources +...  59.1 us
    ppermute x37, starting transfers between devices, swap(): lax.ppermute(values, axis, [(i, i ^ bits) for i in range(lax.axis_size(ax...  42.7 us
    all_to_all x7, waiting for transfers between devices, exchange(): return lax.all_to_all(blocks, 'seq', 0, 0, axis_index_groups=groups)  35.2 us
    all_to_all x7, starting transfers between devices, exchange(): return lax.all_to_all(blocks, 'seq', 0, 0, axis_index_groups=groups)  32.2 us
    pallas_call x1, Pallas kernels, attend_forward(): pl.pallas_call(attend_forward_kernel, grid=(images, steps), in_specs=sour...  26.8 us
    all_gather x3, waiting for transfers between devices, whole(): return lax.all_gather(weight, 'fsdp', axis=0, tiled=True)  22 us
  transfers between devices with their start and end apart: 53, of which 23 were waited for; matrix products, arithmetic and copies ran while one was open for 48% of the time, Pallas kernels for 12%

profile of v3, /device:TPU:0, one launch (start us, length us, event | category | flops | bytes accessed | tf_op | source)
XLA Modules:
  0.0 695.6 jit_solution(16241086916927869773)
XLA Ops:
  7.3 2.9 pad_maximum_fusion
  11.0 5.3 all-to-all-start
  23.1 31.9 %all-to-all-done = bf16[4,2,184,1152]{3,2,1,0:T(8,128)(2,1)S(1)} async-done(((bf16[4,2,184,1152]{3,2,1,0:T(8,128)(2,1)}), bf16[4,2,184,1152]{3,2,1,0:T(8,128)(2,1)S(1)}, u32[]{:S(2)}, u32[]{:S(2)}) %all-to-all-start) | async-done | bytes 3391520 | tf_op jit(solution)/shard_map/all_to_all | solution.py:188
  56.8 2.3 copy.63
  62.3 12.6 %all-gather.4.cloned.1.call-done = bf16[1152,3456]{1,0:T(8,128)(2,1)} async-done(((bf16[288,3456]{1,0:T(8,128)(2,1)}), bf16[1152,3456]{1,0:T(8,128)(2,1)}) %all-gather.4.cloned.1.call-update) | async-done | bytes 7962640 | tf_op jit(solution)/shard_map/all_gather | solution.py:413
  74.9 21.1 %fusion.19.q_ref.k_ref.v_ref = bf16[2,3456,736]{2,1,0:T(8,128)(2,1)} fusion(f32[3456]{0:T(1024)S(1)} %pad_maximum_fusion.5, bf16[1152,3456]{1,0:T(8,128)(2,1)} %all-gather.4.cloned.1.call-done, bf16[2,736,1152]{2,1,0:T(8,128)(2,1)S(1)} %bitcast.100, f32[1152]{0:T(1024)S(1)} %add.251, f32[1152]{0:T(1024)S(1)} %mul.167, f32[2,736]{1,0:T(2,128)S(1)} %add_rsqrt_fusion.1, ...), kind=kOutput, calls=%fused_computation.35 | convolution fusion | flops 11741331456 | bytes 21563392 | tf_op jit(solution)/shard_map/itd,dm->imt/dot_general | solution.py:348
  96.1 4.7 all-to-all-start.1
  101.4 26.8 %attend_forward.1 = (bf16[2,1152,736]{2,1,0:T(8,128)(2,1)S(1)}, f32[2,16,1,736]{3,2,1,0:T(1,128)S(1)}) custom-call(bf16[2,3456,736]{2,1,0:T(8,128)(2,1)} %fusion.19.q_ref.k_ref.v_ref, bf16[2,3456,736]{2,1,0:T(8,128)(2,1)} %fusion.19.q_ref.k_ref.v_ref, bf16[2,3456,736]{2,1,0:T(8,128)(2,1)} %fusion.19.q_ref.k_ref.v_ref, s32[2,1,736]{2,1,0:T(1,128)S(1)} %broadcast_in_dim.46.mask_ref), custom_call_target="tpu_custom_call" | custom-call | flops 17750294528 | bytes 13565952 | tf_op jit(solution)/shard_map/attend_forward/pallas_call | solution.py:78
  128.2 3.1 broadcast_select_fusion.7
  131.4 5.7 fusion.48
  137.2 2.9 copy-done.9
  140.9 3.2 all-gather.6.cloned.1.call-done
  144.1 36.4 %add_convert_fusion = (bf16[2,736,4304]{2,1,0:T(8,128)(2,1)}, bf16[2,736,4304]{2,1,0:T(8,128)(2,1)}) fusion(f32[4304]{0:T(1024)S(1)} %add.269, bf16[1152,4304]{1,0:T(8,128)(2,1)} %all-gather.6.cloned.1.call-done, f32[2,736,1152]{2,1,0:T(8,128)} %copy-done.9, f32[1152]{0:T(1024)S(1)} %add.266, f32[1152]{0:T(1024)S(1)} %mul.175, ...), kind=kOutput, calls=%fused_computation.4 | convolution fusion | flops 14725817344 | bytes 42079552 | tf_op jit(solution)/shard_map/itd,df->itf/dot_general | solution.py:348
  180.6 2.4 copy.67
  185.4 2.1 copy-done.69
  187.5 18.8 %fusion.1 = bf16[1152,4304]{1,0:T(8,128)(2,1)} fusion(bf16[2,736,1152]{2,1,0:T(8,128)(2,1)S(1)} %bitcast_select_fusion, bf16[2,736,4304]{2,1,0:T(8,128)(2,1)S(1)} %copy-done.69), kind=kOutput, calls=%fused_computation.9 | convolution fusion | flops 14601922560 | bytes 25978880 | tf_op jit(solution)/shard_map/itd,itf->df/dot_general | solution.py:348
  207.1 6.2 all-gather.8.cloned.1.call-done
  213.3 22.9 %add_convert_fusion.2 = bf16[2,736,1152]{2,1,0:T(8,128)(2,1)S(1)} fusion(f32[2,736,1152]{2,1,0:T(8,128)} %copy-done.9, bf16[2,736,4304]{2,1,0:T(8,128)(2,1)} %get-tuple-element.146, bf16[1152,4304]{1,0:T(8,128)(2,1)} %all-gather.8.cloned.1.call-done, f32[1152]{0:T(1024)S(1)} %add.278), kind=kOutput, calls=%fused_computation.54 | convolution fusion | flops 14602051584 | bytes 32766464 | tf_op jit(solution)/shard_map/itf,df->itd/dot_general | solution.py:348
  238.3 4.0 all-to-all-start.2
  242.3 25.6 %convert_reduce_fusion = (f32[4304]{0:T(1024)}, bf16[2,736,4304]{2,1,0:T(8,128)(2,1)}) fusion(bf16[2,736,4304]{2,1,0:T(8,128)(2,1)} %get-tuple-element.148, bf16[2,736,1152]{2,1,0:T(8,128)(2,1)} %copy-done.13, bf16[1152,4304]{1,0:T(8,128)(2,1)} %all-gather.8.cloned.1.call-done), kind=kOutput, calls=%fused_computation.2 | convolution fusion | flops 14628637696 | bytes 38667072 | tf_op jit(solution)/shard_map/itd,df->itf/dot_general | solution.py:348
  267.9 24.1 %fusion.2 = bf16[1152,4304]{1,0:T(8,128)(2,1)} fusion(bf16[2,736,4304]{2,1,0:T(8,128)(2,1)} %get-tuple-element.150, f32[2,736,1152]{2,1,0:T(8,128)} %copy-done.9, f32[1152]{0:T(1024)S(1)} %add.266, f32[1152]{0:T(1024)S(1)} %mul.175, f32[2,736]{1,0:T(2,128)S(1)} %add_rsqrt_fusion, f32[2,736]{1,0:T(2,128)S(1)} %broadcast_multiply_fusion.4), kind=kOutput, calls=%fused_computation.10 | convolution fusion | flops 14610401280 | bytes 29391360 | tf_op jit(solution)/shard_map/itd,itf->df/dot_general | solution.py:348
  292.0 27.5 %multiply_reduce_fusion = (f32[1152]{0:T(1024)}, f32[2,736]{1,0:T(2,128)S(1)}, f32[2,736]{1,0:T(2,128)S(1)}, f32[1152]{0:T(1024)}, f32[2,736,1152]{2,1,0:T(8,128)}) fusion(f32[2,736,1152]{2,1,0:T(8,128)} %copy-done.9, f32[2,736]{1,0:T(2,128)S(1)} %add_rsqrt_fusion, f32[2,736]{1,0:T(2,128)S(1)} %broadcast_multiply_fusion.4, f32[1152]{0:T(1024)S(1)} %mul.175, ...), kind=kOutput, calls=%fused_computation.50 | convolution fusion | flops 14612221952 | bytes 36190720 | tf_op jit(solution)/shard_map/itf,df->itd/dot_general | solution.py:348
  319.6 9.5 %multiply_add_fusion.1 = f32[2,736,1152]{2,1,0:T(8,128)} fusion(bf16[2,736,1152]{2,1,0:T(8,128)(2,1)} %copy-done.13, f32[2,736,1152]{2,1,0:T(8,128)} %get-tuple-element.324, f32[2,736,1152]{2,1,0:T(8,128)} %copy-done.9, f32[2,736]{1,0:T(2,128)S(1)} %get-tuple-element.328, f32[2,736]{1,0:T(2,128)S(1)} %get-tuple-element.329, f32[1152]{0:T(1024)S(1)} %mul.175, ...), kind=kLoop, calls=%fused_computation.52 | loop fusion | flops 15261696 | bytes 23768576 | tf_op jit(solution)/shard_map/add | solution.py:468
  329.1 4.7 all-to-all-start.3
  334.0 3.5 convert_reduce_fusion.4
  337.6 8.4 %convolution_convert_fusion = bf16[2,736,1152]{2,1,0:T(8,128)(2,1)} fusion(bf16[288,1152]{1,0:T(8,128)(2,1)S(1)} %copy-done.28, bf16[288,1152]{1,0:T(8,128)(2,1)S(1)} %copy-done.26, bf16[288,1152]{1,0:T(8,128)(2,1)S(1)} %copy-done.24, bf16[288,1152]{1,0:T(8,128)(2,1)S(1)} %copy-done.22, f32[2,736,1152]{2,1,0:T(8,128)} %multiply_add_fusion.1), kind=kOutput, calls=%fused_computation.61 | convolution fusion | flops 3921002496 | bytes 12828672 | tf_op jit(solution)/shard_map/nd,itd->int/dot_general | solution.py:348
  346.0 5.9 copy.69
  351.9 9.1 %fusion.22 = bf16[1152,1152]{1,0:T(8,128)(2,1)} fusion(bf16[2,1152,736]{2,1,0:T(8,128)(2,1)S(1)} %copy-done.1, f32[2,736,1152]{2,1,0:T(8,128)} %multiply_add_fusion.1), kind=kOutput, calls=%fused_computation.36 | convolution fusion | flops 3910017024 | bytes 12828672 | tf_op jit(solution)/shard_map/int,itd->nd/dot_general | solution.py:348
  361.0 2.8 all-to-all-done.3
  363.8 3.1 reduce_sum.191
  366.9 2.3 collective-permute-start.5
  370.1 14.7 %attend_backward.4 = (bf16[2,3,1152,736]{3,2,1,0:T(8,128)(2,1)}, bf16[2,3,576,736]{3,2,1,0:T(8,128)(2,1)}) custom-call(bf16[2,3456,736]{2,1,0:T(8,128)(2,1)} %fusion.19.q_ref.k_ref.v_ref, bf16[2,3456,736]{2,1,0:T(8,128)(2,1)} %fusion.19.q_ref.k_ref.v_ref, bf16[2,3456,736]{2,1,0:T(8,128)(2,1)} %fusion.19.q_ref.k_ref.v_ref, ...), custom_call_target="tpu_custom_call" | custom-call | flops 110939340800 | bytes 9326592 | tf_op jit(solution)/shard_map/attend_backward/pallas_call | solution.py:148
  385.7 14.8 %attend_backward.5 = (bf16[2,3,1152,736]{3,2,1,0:T(8,128)(2,1)}, bf16[2,3,576,736]{3,2,1,0:T(8,128)(2,1)}) custom-call(bf16[2,3456,736]{2,1,0:T(8,128)(2,1)} %fusion.19.q_ref.k_ref.v_ref, bf16[2,3456,736]{2,1,0:T(8,128)(2,1)} %fusion.19.q_ref.k_ref.v_ref, ...), custom_call_target="tpu_custom_call", output_to_operand_aliasing={{0}: (7, {}), {1}: (8, {})} | custom-call | flops 110939340800 | bytes 9326592 | tf_op jit(solution)/shard_map/attend_backward/pallas_call | solution.py:148
  400.5 4.7 all-to-all-start.4
  405.2 13.0 %fusion.23 = bf16[1152,1728]{1,0:T(8,128)(2,1)} fusion(bf16[2,1728,736]{2,1,0:T(8,128)(2,1)} %bitcast.113, bf16[2,736,1152]{2,1,0:T(8,128)(2,1)} %bitcast.102, f32[1152]{0:T(1024)} %copy-done.59, f32[1152]{0:T(1024)} %copy-done.48, f32[2,736]{1,0:T(2,128)} %copy-done.53, f32[2,736]{1,0:T(2,128)S(1)} %copy-done.44), kind=kOutput, calls=%fused_computation.37 | convolution fusion | flops 5872656384 | bytes 12481024 | tf_op jit(solution)/shard_map/itd,imt->dm/dot_general | solution.py:348
  419.2 14.6 %attend_backward.6 = (bf16[2,3,1152,736]{3,2,1,0:T(8,128)(2,1)}, bf16[2,3,576,736]{3,2,1,0:T(8,128)(2,1)}) custom-call(bf16[2,3456,736]{2,1,0:T(8,128)(2,1)} %fusion.19.q_ref.k_ref.v_ref, bf16[2,3456,736]{2,1,0:T(8,128)(2,1)} %fusion.19.q_ref.k_ref.v_ref, bf16[2,3456,736]{2,1,0:T(8,128)(2,1)} %fusion.19.q_ref.k_ref.v_ref, ...), custom_call_target="tpu_custom_call", output_to_operand_aliasing={{0}: (7, {})} | custom-call | flops 110939340800 | bytes 9326592 | tf_op jit(solution)/shard_map/attend_backward/pallas_call | solution.py:148
  434.3 3.2 reduce_sum.192
  437.5 2.2 broadcast_in_dim.49
  439.7 4.6 all-to-all-start.5
  445.2 15.0 %attend_backward.7 = (bf16[2,3,1152,736]{3,2,1,0:T(8,128)(2,1)}, bf16[2,3,576,736]{3,2,1,0:T(8,128)(2,1)}) custom-call(bf16[2,3456,736]{2,1,0:T(8,128)(2,1)} %fusion.19.q_ref.k_ref.v_ref, bf16[2,3456,736]{2,1,0:T(8,128)(2,1)} %fusion.19.q_ref.k_ref.v_ref, ...), custom_call_target="tpu_custom_call", output_to_operand_aliasing={{0}: (7, {}), {1}: (8, {})} | custom-call | flops 110939340800 | bytes 9326592 | tf_op jit(solution)/shard_map/attend_backward/pallas_call | solution.py:148
  460.3 13.5 %all-to-all-done.5 = bf16[2,72,4304]{2,1,0:T(8,128)(2,1)} async-done(((bf16[2,72,4304]{2,1,0:T(8,128)(2,1)}), bf16[2,72,4304]{2,1,0:T(8,128)(2,1)}, u32[]{:S(2)}, u32[]{:S(2)}) %all-to-all-start.5) | async-done | bytes 1239584 | tf_op jit(solution)/shard_map/all_to_all | solution.py:266
  473.8 13.1 %fusion.24 = bf16[1152,1728]{1,0:T(8,128)(2,1)} fusion(bf16[2,1728,736]{2,1,0:T(8,128)(2,1)} %bitcast.112, bf16[2,736,1152]{2,1,0:T(8,128)(2,1)} %bitcast.103, f32[1152]{0:T(1024)} %copy-done.59, f32[1152]{0:T(1024)} %copy-done.48, f32[2,736]{1,0:T(2,128)} %copy-done.53, f32[2,736]{1,0:T(2,128)S(1)} %copy-done.45), kind=kOutput, calls=%fused_computation.38 | convolution fusion | flops 5872656384 | bytes 12481024 | tf_op jit(solution)/shard_map/itd,imt->dm/dot_general | solution.py:348
  489.0 3.2 collective-permute-start.7
  492.4 4.4 convert_reduce_fusion.2
  499.9 4.9 all-to-all-start.6
  504.8 3.4 convert_reduce_fusion.1
  509.5 3.0 collective-permute-start.11
  513.0 22.3 %fusion.32 = (f32[1152]{0:T(1024)S(1)}, f32[2,736]{1,0:T(2,128)S(1)}, f32[2,736]{1,0:T(2,128)S(1)}, f32[1152]{0:T(1024)S(1)}, f32[2,736,1152]{2,1,0:T(8,128)}) fusion(bf16[2,736,1152]{2,1,0:T(8,128)(2,1)S(1)} %bitcast.104, f32[2,736]{1,0:T(2,128)S(1)} %copy-done.54, f32[2,736]{1,0:T(2,128)S(1)} %copy-done.45, f32[1152]{0:T(1024)S(1)} %copy-done.49, ...), kind=kOutput, calls=%fused_computation.46 | convolution fusion | flops 11737935872 | bytes 28348928 | tf_op jit(solution)/shard_map/imt,dm->itd/dot_general | solution.py:348
  535.6 2.8 collective-permute-start.14
  539.0 12.2 %collective-permute-done.11 = bf16[72,1152]{1,0:T(8,128)(2,1)S(1)} collective-permute-done((bf16[72,1152]{1,0:T(8,128)(2,1)S(1)}, bf16[72,1152]{1,0:T(8,128)(2,1)S(1)}, u32[]{:S(2)}, u32[]{:S(2)}) %collective-permute-start.11) | collective-permute-done | bytes 165920 | tf_op jit(solution)/shard_map/ppermute | solution.py:178
  552.9 10.1 %convert_reduce_fusion.5 = (f32[1152]{0:T(1024)S(1)}, bf16[2,736,1152]{2,1,0:T(8,128)(2,1)}) fusion(f32[2,736,1152]{2,1,0:T(8,128)} %multiply_add_fusion.1, f32[2,736]{1,0:T(2,128)S(1)} %broadcast_multiply_fusion, f32[2,736]{1,0:T(2,128)S(1)} %copy-done.45, bf16[2,736,1152]{2,1,0:T(8,128)(2,1)S(1)} %bitcast.105, f32[2,736]{1,0:T(2,128)S(1)} %broadcast_multiply_fusion.1, ...), kind=kLoop, calls=%fused_computation.51 | loop fusion | flops 22043520 | bytes 20381696 | tf_op jit(solution)/shard_map/reduce_sum | solution.py:352
  567.5 3.9 copy.84
  571.4 3.9 all-to-all-start.7
  578.7 2.5 collective-permute-start.16
  581.2 4.3 bitcast_convert_fusion
  585.6 3.0 collective-permute-start.19
  591.1 25.4 %collective-permute-done.15 = bf16[72,1152]{1,0:T(8,128)(2,1)S(1)} collective-permute-done((bf16[72,1152]{1,0:T(8,128)(2,1)S(1)}, bf16[72,1152]{1,0:T(8,128)(2,1)S(1)}, u32[]{:S(2)}, u32[]{:S(2)}) %collective-permute-start.15) | collective-permute-done | bytes 165920 | tf_op jit(solution)/shard_map/ppermute | solution.py:178
  616.5 5.5 collective-permute-done.16
  622.0 9.0 %collective-permute-done.19 = bf16[72,1728]{1,0:T(8,128)(2,1)S(1)} collective-permute-done((bf16[72,1728]{1,0:T(8,128)(2,1)S(1)}, bf16[72,1728]{1,0:T(8,128)(2,1)S(1)}, u32[]{:S(2)}, u32[]{:S(2)}) %collective-permute-start.19) | collective-permute-done | bytes 248864 | tf_op jit(solution)/shard_map/ppermute | solution.py:178
  631.0 3.7 collective-permute-done.18
  648.9 4.8 collective-permute-done.24
  654.4 2.6 convert_bitcast_fusion
  657.0 3.3 collective-permute-done.28
  660.3 4.0 collective-permute-done.27
  (304 shorter events, 82.7 us)
Async XLA Ops:
  7.3 67.6 %all-gather.4.cloned.1.call-start = ((), (), s32[]{:S(2)}) async-start(), calls=%async_computation.13 | async-start | bytes 9953280 | tf_op jit(solution)/shard_map/all_gather | solution.py:413
  10.3 133.9 %all-gather.6.cloned.1.call-start = ((), (), s32[]{:S(2)}) async-start(), calls=%async_computation.14 | async-start | bytes 12533760 | tf_op jit(solution)/shard_map/all_gather | solution.py:413
  11.0 44.0 %all-to-all-start = ((bf16[4,2,184,1152]{3,2,1,0:T(8,128)(2,1)}), bf16[4,2,184,1152]{3,2,1,0:T(8,128)(2,1)S(1)}, u32[]{:S(2)}, u32[]{:S(2)}) async-start(bf16[4,2,184,1152]{3,2,1,0:T(8,128)(2,1)} %bitcast.118), calls=%async_computation | async-start | bytes 6782976 | tf_op jit(solution)/shard_map/all_to_all | solution.py:188
  16.3 197.0 %all-gather.8.cloned.1.call-start = ((), (), s32[]{:S(2)}) async-start(), calls=%async_computation.15 | async-start | bytes 12533760 | tf_op jit(solution)/shard_map/all_gather | solution.py:413
  16.5 1.2 collective-permute-start
  17.8 3.8 collective-permute-start.1
  22.6 52.3 %copy-start.48 = (f32[1152]{0:T(1024)}, f32[1152]{0:T(1024)S(1)}, u32[]{:S(2)}) copy-start(f32[1152]{0:T(1024)S(1)} %mul.167) | copy-start | bytes 13828
  22.8 52.1 %copy-start.59 = (f32[1152]{0:T(1024)}, f32[1152]{0:T(1024)S(1)}, u32[]{:S(2)}) copy-start(f32[1152]{0:T(1024)S(1)} %add.251) | copy-start | bytes 13828
  59.1 72.3 %copy-start.7 = (bf16[2,4,184,1152]{3,2,1,0:T(8,128)(2,1)}, bf16[2,4,184,1152]{3,2,1,0:T(8,128)(2,1)S(1)}, u32[]{:S(2)}) copy-start(bf16[2,4,184,1152]{3,2,1,0:T(8,128)(2,1)S(1)} %copy.63) | copy-start | bytes 10174468
  59.1 37.0 %collective-permute-start.3 = (bf16[288,1152]{1,0:T(8,128)(2,1)}, bf16[288,1152]{1,0:T(8,128)(2,1)}, u32[]{:S(2)}, u32[]{:S(2)}) collective-permute-start(bf16[288,1152]{1,0:T(8,128)(2,1)} %param.27), channel_id=1, source_target_pairs={{0,2},{1,3},{2,0},{3,1},{4,6},{5,7},{6,4},{7,5},{8,10},{9,11},{10,... | collective-permute-start | bytes 1990664 | tf_op jit(solution)/shard_map/ppermute | solution.py:178
  60.7 35.3 %collective-permute-start.2 = (bf16[288,1152]{1,0:T(8,128)(2,1)}, bf16[288,1152]{1,0:T(8,128)(2,1)}, u32[]{:S(2)}, u32[]{:S(2)}) collective-permute-start(bf16[288,1152]{1,0:T(8,128)(2,1)} %param.27), channel_id=1, source_target_pairs={{0,1},{1,0},{2,3},{3,2},{4,5},{5,4},{6,7},{7,6},{8,9},{9,8},{10,11... | collective-permute-start | bytes 1990664 | tf_op jit(solution)/shard_map/ppermute | solution.py:178
  61.3 34.8 %copy-start.43 = (f32[2,736]{1,0:T(2,128)}, f32[2,736]{1,0:T(2,128)S(1)}, u32[]{:S(2)}) copy-start(f32[2,736]{1,0:T(2,128)S(1)} %broadcast_multiply_fusion.5) | copy-start | bytes 17668
  62.3 33.7 %copy-start.53 = (f32[2,736]{1,0:T(2,128)}, f32[2,736]{1,0:T(2,128)S(1)}, u32[]{:S(2)}) copy-start(f32[2,736]{1,0:T(2,128)S(1)} %add_rsqrt_fusion.1) | copy-start | bytes 17668
  96.1 84.5 %all-to-all-start.1 = ((bf16[4,2,184,1152]{3,2,1,0:T(8,128)(2,1)}), bf16[4,2,184,1152]{3,2,1,0:T(8,128)(2,1)}, u32[]{:S(2)}, u32[]{:S(2)}) async-start(bf16[4,2,184,1152]{3,2,1,0:T(8,128)(2,1)} %bitcast.119), calls=%async_computation.1 | async-start | bytes 6782976 | tf_op jit(solution)/shard_map/all_to_all | solution.py:188
  100.8 228.3 %reduce-scatter.6.cloned.1.call-start = ((), (), s32[]{:S(2)}) async-start(), calls=%async_computation.16 | async-start | bytes 12533760 | tf_op jit(solution)/shard_map/reduce_scatter | solution.py:252
  101.1 27.1 %collective-permute-start.4 = (bf16[288,1152]{1,0:T(8,128)(2,1)}, bf16[288,1152]{1,0:T(8,128)(2,1)S(1)}, u32[]{:S(2)}, u32[]{:S(2)}) collective-permute-start(bf16[288,1152]{1,0:T(8,128)(2,1)} %collective-permute-done.3), channel_id=1, source_target_pairs={{0,1},{1,0},{2,3},{3,2},{4,5},{5,4},{6,7},{7,6},{8,9},{9,8},{10,11... | collective-permute-start | bytes 1990664 | tf_op jit(solution)/shard_map/ppermute | solution.py:178
  238.3 53.7 %all-to-all-start.2 = ((bf16[4,2,184,1152]{3,2,1,0:T(8,128)(2,1)}), bf16[4,2,184,1152]{3,2,1,0:T(8,128)(2,1)S(1)}, u32[]{:S(2)}, u32[]{:S(2)}) async-start(bf16[4,2,184,1152]{3,2,1,0:T(8,128)(2,1)} %bitcast.110), calls=%async_computation.2 | async-start | bytes 6782976 | tf_op jit(solution)/shard_map/all_to_all | solution.py:188
  242.2 158.2 %reduce-scatter.8.cloned.1.call-start = ((), (), s32[]{:S(2)}) async-start(), calls=%async_computation.17 | async-start | bytes 12533760 | tf_op jit(solution)/shard_map/reduce_scatter | solution.py:252
  292.0 27.5 %copy-start.10 = (bf16[4,2,184,1152]{3,2,1,0:T(8,128)(2,1)}, bf16[4,2,184,1152]{3,2,1,0:T(8,128)(2,1)S(1)}, u32[]{:S(2)}) copy-start(bf16[4,2,184,1152]{3,2,1,0:T(8,128)(2,1)S(1)} %all-to-all-done.2) | copy-start | bytes 10174468
  329.1 34.7 %all-to-all-start.3 = ((bf16[4,72,4304]{2,1,0:T(8,128)(2,1)}), bf16[4,72,4304]{2,1,0:T(8,128)(2,1)}, u32[]{:S(2)}, u32[]{:S(2)}) async-start(bf16[4,72,4304]{2,1,0:T(8,128)(2,1)} %bitcast.123), calls=%async_computation.4 | async-start | bytes 5013504 | tf_op jit(solution)/shard_map/all_to_all | solution.py:188
  333.8 153.1 %reduce-scatter.10.cloned.1.call-start = ((), (), s32[]{:S(2)}) async-start(), calls=%async_computation.18 | async-start | bytes 3317760 | tf_op jit(solution)/shard_map/reduce_scatter | solution.py:252
  366.9 33.6 %collective-permute-start.5 = (bf16[72,4304]{1,0:T(8,128)(2,1)}, bf16[72,4304]{1,0:T(8,128)(2,1)}, u32[]{:S(2)}, u32[]{:S(2)}) collective-permute-start(bf16[72,4304]{1,0:T(8,128)(2,1)} %reduce_sum.191), channel_id=1, source_target_pairs={{0,16},{4,20},{8,24},{12,28},{16,0},{20,4},{24,8},{28,12},{1,17},{... | collective-permute-start | bytes 1859336 | tf_op jit(solution)/shard_map/ppermute | solution.py:178
  400.5 33.8 %all-to-all-start.4 = ((bf16[4,72,4304]{2,1,0:T(8,128)(2,1)}), bf16[4,72,4304]{2,1,0:T(8,128)(2,1)}, u32[]{:S(2)}, u32[]{:S(2)}) async-start(bf16[4,72,4304]{2,1,0:T(8,128)(2,1)} %bitcast.122), calls=%async_computation.6 | async-start | bytes 5013504 | tf_op jit(solution)/shard_map/all_to_all | solution.py:188
  405.2 81.7 %reduce-scatter.12.cloned.1.call-start = ((), (), s32[]{:S(2)}) async-start(), calls=%async_computation.19 | async-start | bytes 5160960 | tf_op jit(solution)/shard_map/reduce_scatter | solution.py:252
  439.7 34.1 %all-to-all-start.5 = ((bf16[2,72,4304]{2,1,0:T(8,128)(2,1)}), bf16[2,72,4304]{2,1,0:T(8,128)(2,1)}, u32[]{:S(2)}, u32[]{:S(2)}) async-start(bf16[2,72,4304]{2,1,0:T(8,128)(2,1)} %broadcast_in_dim.49), calls=%async_computation.7 | async-start | bytes 2506752 | tf_op jit(solution)/shard_map/all_to_all | solution.py:266
  444.3 120.4 %reduce-scatter.14.cloned.1.call-start = ((), (), s32[]{:S(2)}) async-start(), calls=%async_computation.20 | async-start | bytes 5160960 | tf_op jit(solution)/shard_map/reduce_scatter | solution.py:252
  445.2 28.6 %copy-start.45 = (f32[2,736]{1,0:T(2,128)S(1)}, f32[2,736]{1,0:T(2,128)}, u32[]{:S(2)}) copy-start(f32[2,736]{1,0:T(2,128)} %copy-done.43) | copy-start | bytes 17668
  489.0 46.4 %collective-permute-start.8 = (bf16[72,4304]{1,0:T(8,128)(2,1)}, bf16[72,4304]{1,0:T(8,128)(2,1)}, u32[]{:S(2)}, u32[]{:S(2)}) collective-permute-start(bf16[72,4304]{1,0:T(8,128)(2,1)} %add_convert_fusion.5), channel_id=1, source_target_pairs={{0,12},{4,8},{8,4},{12,0},{16,28},{20,24},{24,20},{28,16},{1,13},{... | collective-permute-start | bytes 1859336 | tf_op jit(solution)/shard_map/ppermute | solution.py:178
  489.0 46.7 %collective-permute-start.7 = (bf16[72,4304]{1,0:T(8,128)(2,1)}, bf16[72,4304]{1,0:T(8,128)(2,1)}, u32[]{:S(2)}, u32[]{:S(2)}) collective-permute-start(bf16[72,4304]{1,0:T(8,128)(2,1)} %add_convert_fusion.5), channel_id=1, source_target_pairs={{0,8},{4,12},{8,0},{12,4},{16,24},{20,28},{24,16},{28,20},{1,9},{5... | collective-permute-start | bytes 1859336 | tf_op jit(solution)/shard_map/ppermute | solution.py:178
  492.2 46.3 %collective-permute-start.6 = (bf16[72,4304]{1,0:T(8,128)(2,1)}, bf16[72,4304]{1,0:T(8,128)(2,1)}, u32[]{:S(2)}, u32[]{:S(2)}) collective-permute-start(bf16[72,4304]{1,0:T(8,128)(2,1)} %add_convert_fusion.5), channel_id=1, source_target_pairs={{0,4},{4,0},{8,12},{12,8},{16,20},{20,16},{24,28},{28,24},{1,5},{5... | collective-permute-start | bytes 1859336 | tf_op jit(solution)/shard_map/ppermute | solution.py:178
  499.9 64.7 %all-to-all-start.6 = ((bf16[4,72,4304]{2,1,0:T(8,128)(2,1)}), bf16[4,72,4304]{2,1,0:T(8,128)(2,1)}, u32[]{:S(2)}, u32[]{:S(2)}) async-start(bf16[4,72,4304]{2,1,0:T(8,128)(2,1)} %broadcast_in_dim.53), calls=%async_computation.10 | async-start | bytes 5013504 | tf_op jit(solution)/shard_map/all_to_all | solution.py:188
  509.5 41.7 %collective-permute-start.11 = (bf16[72,1152]{1,0:T(8,128)(2,1)S(1)}, bf16[72,1152]{1,0:T(8,128)(2,1)S(1)}, u32[]{:S(2)}, u32[]{:S(2)}) collective-permute-start(bf16[72,1152]{1,0:T(8,128)(2,1)S(1)} %get-tuple-element.307), channel_id=1, source_target_pairs={{0,12},{4,8},{8,4},{12,0},{16,28},{20,24},{24,20},{28,16},{1,13},{... | collective-permute-start | bytes 497672 | tf_op jit(solution)/shard_map/ppermute | solution.py:178
  512.4 50.5 %collective-permute-start.10 = (bf16[72,1152]{1,0:T(8,128)(2,1)S(1)}, bf16[72,1152]{1,0:T(8,128)(2,1)S(1)}, u32[]{:S(2)}, u32[]{:S(2)}) collective-permute-start(bf16[72,1152]{1,0:T(8,128)(2,1)S(1)} %get-tuple-element.308), channel_id=1, source_target_pairs={{0,8},{4,12},{8,0},{12,4},{16,24},{20,28},{24,16},{28,20},{1,9},{5... | collective-permute-start | bytes 497672 | tf_op jit(solution)/shard_map/ppermute | solution.py:178
  513.0 22.3 %copy-start.17 = (bf16[288,1728]{1,0:T(8,128)(2,1)S(1)}, bf16[288,1728]{1,0:T(8,128)(2,1)}, u32[]{:S(2)}) copy-start(bf16[288,1728]{1,0:T(8,128)(2,1)} %reduce-scatter.12.cloned.1.call-done) | copy-start | bytes 2985988
  535.4 27.6 %collective-permute-start.9 = (bf16[72,1152]{1,0:T(8,128)(2,1)S(1)}, bf16[72,1152]{1,0:T(8,128)(2,1)S(1)}, u32[]{:S(2)}, u32[]{:S(2)}) collective-permute-start(bf16[72,1152]{1,0:T(8,128)(2,1)S(1)} %get-tuple-element.309), channel_id=1, source_target_pairs={{0,4},{4,0},{8,12},{12,8},{16,20},{20,16},{24,28},{28,24},{1,5},{5... | collective-permute-start | bytes 497672 | tf_op jit(solution)/shard_map/ppermute | solution.py:178
  535.6 27.4 %collective-permute-start.14 = (bf16[72,1728]{1,0:T(8,128)(2,1)S(1)}, bf16[72,1728]{1,0:T(8,128)(2,1)S(1)}, u32[]{:S(2)}, u32[]{:S(2)}) collective-permute-start(bf16[72,1728]{1,0:T(8,128)(2,1)S(1)} %get-tuple-element.300), channel_id=1, source_target_pairs={{0,12},{4,8},{8,4},{12,0},{16,28},{20,24},{24,20},{28,16},{1,13},{... | collective-permute-start | bytes 746504 | tf_op jit(solution)/shard_map/ppermute | solution.py:178
  538.4 25.6 %collective-permute-start.13 = (bf16[72,1728]{1,0:T(8,128)(2,1)S(1)}, bf16[72,1728]{1,0:T(8,128)(2,1)S(1)}, u32[]{:S(2)}, u32[]{:S(2)}) collective-permute-start(bf16[72,1728]{1,0:T(8,128)(2,1)S(1)} %get-tuple-element.301), channel_id=1, source_target_pairs={{0,8},{4,12},{8,0},{12,4},{16,24},{20,28},{24,16},{28,20},{1,9},{5... | collective-permute-start | bytes 746504 | tf_op jit(solution)/shard_map/ppermute | solution.py:178
  551.2 13.5 %collective-permute-start.12 = (bf16[72,1728]{1,0:T(8,128)(2,1)S(1)}, bf16[72,1728]{1,0:T(8,128)(2,1)}, u32[]{:S(2)}, u32[]{:S(2)}) collective-permute-start(bf16[72,1728]{1,0:T(8,128)(2,1)S(1)} %get-tuple-element.302), channel_id=1, source_target_pairs={{0,4},{4,0},{8,12},{12,8},{16,20},{20,16},{24,28},{28,24},{1,5},{5... | collective-permute-start | bytes 746504 | tf_op jit(solution)/shard_map/ppermute | solution.py:178
  565.5 20.0 %collective-permute-start.22 = (f32[4,3380]{1,0:T(4,128)S(1)}, f32[4,3380]{1,0:T(4,128)S(1)}, u32[]{:S(2)}, u32[]{:S(2)}) collective-permute-start(f32[4,3380]{1,0:T(4,128)S(1)} %concatenate.61), channel_id=1, source_target_pairs={{0,3},{1,2},{2,1},{3,0},{4,7},{5,6},{6,5},{7,4},{8,11},{9,10},{10,... | collective-permute-start | bytes 162248 | tf_op jit(solution)/shard_map/ppermute | solution.py:178
  565.6 22.9 %collective-permute-start.21 = (f32[4,3380]{1,0:T(4,128)S(1)}, f32[4,3380]{1,0:T(4,128)}, u32[]{:S(2)}, u32[]{:S(2)}) collective-permute-start(f32[4,3380]{1,0:T(4,128)S(1)} %concatenate.61), channel_id=1, source_target_pairs={{0,2},{1,3},{2,0},{3,1},{4,6},{5,7},{6,4},{7,5},{8,10},{9,11},{10,... | collective-permute-start | bytes 162248 | tf_op jit(solution)/shard_map/ppermute | solution.py:178
  566.5 22.6 %collective-permute-start.20 = (f32[4,3380]{1,0:T(4,128)S(1)}, f32[4,3380]{1,0:T(4,128)}, u32[]{:S(2)}, u32[]{:S(2)}) collective-permute-start(f32[4,3380]{1,0:T(4,128)S(1)} %concatenate.61), channel_id=1, source_target_pairs={{0,1},{1,0},{2,3},{3,2},{4,5},{5,4},{6,7},{7,6},{8,9},{9,8},{10,11... | collective-permute-start | bytes 162248 | tf_op jit(solution)/shard_map/ppermute | solution.py:178
  571.4 94.5 %all-to-all-start.7 = ((bf16[4,2,184,1152]{3,2,1,0:T(8,128)(2,1)}), bf16[4,2,184,1152]{3,2,1,0:T(8,128)(2,1)S(1)}, u32[]{:S(2)}, u32[]{:S(2)}) async-start(bf16[4,2,184,1152]{3,2,1,0:T(8,128)(2,1)} %bitcast.109), calls=%async_computation.12 | async-start | bytes 6782976 | tf_op jit(solution)/shard_map/all_to_all | solution.py:188
  576.7 39.8 %collective-permute-start.15 = (bf16[72,1152]{1,0:T(8,128)(2,1)S(1)}, bf16[72,1152]{1,0:T(8,128)(2,1)S(1)}, u32[]{:S(2)}, u32[]{:S(2)}) collective-permute-start(bf16[72,1152]{1,0:T(8,128)(2,1)S(1)} %add_convert_fusion.11), channel_id=1, source_target_pairs={{0,16},{4,20},{8,24},{12,28},{16,0},{20,4},{24,8},{28,12},{1,17},{... | collective-permute-start | bytes 497672 | tf_op jit(solution)/shard_map/ppermute | solution.py:178
  578.7 43.4 %collective-permute-start.16 = (bf16[72,1728]{1,0:T(8,128)(2,1)S(1)}, bf16[72,1728]{1,0:T(8,128)(2,1)S(1)}, u32[]{:S(2)}, u32[]{:S(2)}) collective-permute-start(bf16[72,1728]{1,0:T(8,128)(2,1)S(1)} %add_convert_fusion.9), channel_id=1, source_target_pairs={{0,16},{4,20},{8,24},{12,28},{16,0},{20,4},{24,8},{28,12},{1,17},{... | collective-permute-start | bytes 746504 | tf_op jit(solution)/shard_map/ppermute | solution.py:178
  585.6 49.1 %copy-start.47 = (f32[4,3380]{1,0:T(4,128)}, f32[4,3380]{1,0:T(4,128)S(1)}, u32[]{:S(2)}) copy-start(f32[4,3380]{1,0:T(4,128)S(1)} %collective-permute-done.22) | copy-start | bytes 162244
  585.6 45.4 %collective-permute-start.19 = (bf16[72,1728]{1,0:T(8,128)(2,1)S(1)}, bf16[72,1728]{1,0:T(8,128)(2,1)S(1)}, u32[]{:S(2)}, u32[]{:S(2)}) collective-permute-start(bf16[72,1728]{1,0:T(8,128)(2,1)S(1)} %get-tuple-element.297), channel_id=1, source_target_pairs={{0,12},{4,8},{8,4},{12,0},{16,28},{20,24},{24,20},{28,16},{1,13},{... | collective-permute-start | bytes 746504 | tf_op jit(solution)/shard_map/ppermute | solution.py:178
  588.6 46.1 %collective-permute-start.18 = (bf16[72,1728]{1,0:T(8,128)(2,1)S(1)}, bf16[72,1728]{1,0:T(8,128)(2,1)S(1)}, u32[]{:S(2)}, u32[]{:S(2)}) collective-permute-start(bf16[72,1728]{1,0:T(8,128)(2,1)S(1)} %get-tuple-element.298), channel_id=1, source_target_pairs={{0,8},{4,12},{8,0},{12,4},{16,24},{20,28},{24,16},{28,20},{1,9},{5... | collective-permute-start | bytes 746504 | tf_op jit(solution)/shard_map/ppermute | solution.py:178
  589.1 45.6 %collective-permute-start.17 = (bf16[72,1728]{1,0:T(8,128)(2,1)S(1)}, bf16[72,1728]{1,0:T(8,128)(2,1)S(1)}, u32[]{:S(2)}, u32[]{:S(2)}) collective-permute-start(bf16[72,1728]{1,0:T(8,128)(2,1)S(1)} %get-tuple-element.299), channel_id=1, source_target_pairs={{0,4},{4,0},{8,12},{12,8},{16,20},{20,16},{24,28},{28,24},{1,5},{5... | collective-permute-start | bytes 746504 | tf_op jit(solution)/shard_map/ppermute | solution.py:178
  635.6 6.8 collective-permute-start.32
  637.1 6.0 collective-permute-start.31
  638.6 6.1 collective-permute-start.30
  639.2 25.1 %copy-start.19 = (bf16[72,1152]{1,0:T(8,128)(2,1)}, bf16[72,1152]{1,0:T(8,128)(2,1)S(1)}, u32[]{:S(2)}) copy-start(bf16[72,1152]{1,0:T(8,128)(2,1)S(1)} %add_convert_fusion.10) | copy-start | bytes 497668
  639.2 8.2 %collective-permute-start.25 = (bf16[72,1152]{1,0:T(8,128)(2,1)S(1)}, bf16[72,1152]{1,0:T(8,128)(2,1)S(1)}, u32[]{:S(2)}, u32[]{:S(2)}) collective-permute-start(bf16[72,1152]{1,0:T(8,128)(2,1)S(1)} %add_convert_fusion.10), channel_id=1, source_target_pairs={{0,12},{4,8},{8,4},{12,0},{16,28},{20,24},{24,20},{28,16},{1,13},{... | collective-permute-start | bytes 497672 | tf_op jit(solution)/shard_map/ppermute | solution.py:178
  640.7 13.0 %collective-permute-start.24 = (bf16[72,1152]{1,0:T(8,128)(2,1)S(1)}, bf16[72,1152]{1,0:T(8,128)(2,1)S(1)}, u32[]{:S(2)}, u32[]{:S(2)}) collective-permute-start(bf16[72,1152]{1,0:T(8,128)(2,1)S(1)} %add_convert_fusion.10), channel_id=1, source_target_pairs={{0,8},{4,12},{8,0},{12,4},{16,24},{20,28},{24,16},{28,20},{1,9},{5... | collective-permute-start | bytes 497672 | tf_op jit(solution)/shard_map/ppermute | solution.py:178
  642.4 27.2 %copy-start.46 = (f32[4,3380]{1,0:T(4,128)}, f32[4,3380]{1,0:T(4,128)S(1)}, u32[]{:S(2)}) copy-start(f32[4,3380]{1,0:T(4,128)S(1)} %collective-permute-done.32) | copy-start | bytes 162244
  642.4 14.6 %collective-permute-start.23 = (bf16[72,1152]{1,0:T(8,128)(2,1)S(1)}, bf16[72,1152]{1,0:T(8,128)(2,1)S(1)}, u32[]{:S(2)}, u32[]{:S(2)}) collective-permute-start(bf16[72,1152]{1,0:T(8,128)(2,1)S(1)} %add_convert_fusion.10), channel_id=1, source_target_pairs={{0,4},{4,0},{8,12},{12,8},{16,20},{20,16},{24,28},{28,24},{1,5},{5... | collective-permute-start | bytes 497672 | tf_op jit(solution)/shard_map/ppermute | solution.py:178
  643.1 17.2 %collective-permute-start.28 = (bf16[72,1728]{1,0:T(8,128)(2,1)S(1)}, bf16[72,1728]{1,0:T(8,128)(2,1)S(1)}, u32[]{:S(2)}, u32[]{:S(2)}) collective-permute-start(bf16[72,1728]{1,0:T(8,128)(2,1)S(1)} %add_convert_fusion.8), channel_id=1, source_target_pairs={{0,12},{4,8},{8,4},{12,0},{16,28},{20,24},{24,20},{28,16},{1,13},{... | collective-permute-start | bytes 746504 | tf_op jit(solution)/shard_map/ppermute | solution.py:178
  644.7 19.5 %collective-permute-start.27 = (bf16[72,1728]{1,0:T(8,128)(2,1)S(1)}, bf16[72,1728]{1,0:T(8,128)(2,1)S(1)}, u32[]{:S(2)}, u32[]{:S(2)}) collective-permute-start(bf16[72,1728]{1,0:T(8,128)(2,1)S(1)} %add_convert_fusion.8), channel_id=1, source_target_pairs={{0,8},{4,12},{8,0},{12,4},{16,24},{20,28},{24,16},{28,20},{1,9},{5... | collective-permute-start | bytes 746504 | tf_op jit(solution)/shard_map/ppermute | solution.py:178
  647.4 16.8 %collective-permute-start.26 = (bf16[72,1728]{1,0:T(8,128)(2,1)S(1)}, bf16[72,1728]{1,0:T(8,128)(2,1)S(1)}, u32[]{:S(2)}, u32[]{:S(2)}) collective-permute-start(bf16[72,1728]{1,0:T(8,128)(2,1)S(1)} %add_convert_fusion.8), channel_id=1, source_target_pairs={{0,4},{4,0},{8,12},{12,8},{16,20},{20,16},{24,28},{28,24},{1,5},{5... | collective-permute-start | bytes 746504 | tf_op jit(solution)/shard_map/ppermute | solution.py:178
  653.7 12.2 %collective-permute-start.29 = (bf16[72,1728]{1,0:T(8,128)(2,1)S(1)}, bf16[72,1728]{1,0:T(8,128)(2,1)}, u32[]{:S(2)}, u32[]{:S(2)}) collective-permute-start(bf16[72,1728]{1,0:T(8,128)(2,1)S(1)} %add_convert_fusion.7), channel_id=1, source_target_pairs={{0,16},{4,20},{8,24},{12,28},{16,0},{20,4},{24,8},{28,12},{1,17},{... | collective-permute-start | bytes 746504 | tf_op jit(solution)/shard_map/ppermute | solution.py:178
  667.2 10.5 %collective-permute-start.35 = (bf16[72,1728]{1,0:T(8,128)(2,1)S(1)}, bf16[72,1728]{1,0:T(8,128)(2,1)S(1)}, u32[]{:S(2)}, u32[]{:S(2)}) collective-permute-start(bf16[72,1728]{1,0:T(8,128)(2,1)S(1)} %add_convert_fusion.6), channel_id=1, source_target_pairs={{0,12},{4,8},{8,4},{12,0},{16,28},{20,24},{24,20},{28,16},{1,13},{... | collective-permute-start | bytes 746504 | tf_op jit(solution)/shard_map/ppermute | solution.py:178
  667.7 11.5 %collective-permute-start.34 = (bf16[72,1728]{1,0:T(8,128)(2,1)S(1)}, bf16[72,1728]{1,0:T(8,128)(2,1)S(1)}, u32[]{:S(2)}, u32[]{:S(2)}) collective-permute-start(bf16[72,1728]{1,0:T(8,128)(2,1)S(1)} %add_convert_fusion.6), channel_id=1, source_target_pairs={{0,8},{4,12},{8,0},{12,4},{16,24},{20,28},{24,16},{28,20},{1,9},{5... | collective-permute-start | bytes 746504 | tf_op jit(solution)/shard_map/ppermute | solution.py:178
  669.7 9.5 %collective-permute-start.33 = (bf16[72,1728]{1,0:T(8,128)(2,1)S(1)}, bf16[72,1728]{1,0:T(8,128)(2,1)S(1)}, u32[]{:S(2)}, u32[]{:S(2)}) collective-permute-start(bf16[72,1728]{1,0:T(8,128)(2,1)S(1)} %add_convert_fusion.6), channel_id=1, source_target_pairs={{0,4},{4,0},{8,12},{12,8},{16,20},{20,16},{24,28},{28,24},{1,5},{5... | collective-permute-start | bytes 746504 | tf_op jit(solution)/shard_map/ppermute | solution.py:178
  671.6 6.1 collective-permute-start.36
  (59 other events, 450.5 us)
Sparse Core Ops, SparseCore 0:
  10.4 64.4 all-gather.3
  76.5 67.6 all-gather.5
  145.7 67.5 all-gather.7
  215.8 82.2 reduce-scatter.5
  300.6 82.2 reduce-scatter.7
  385.9 34.8 reduce-scatter.9
  424.1 44.0 reduce-scatter.11
  487.0 42.5 reduce-scatter.13

commit v4 on v3

--- a/solution.py
+++ b/solution.py
@@ -166,9 +166,9 @@
         input_output_aliases=aliases,
         compiler_params=pltpu.CompilerParams(vmem_limit_bytes=50 << 20),
         cost_estimate=pl.CostEstimate(
-            flops=images * STEP_HEADS * length * length * 25600,
-            bytes_accessed=images * rows * length * 22,
-            transcendentals=images * STEP_HEADS * length * length,
+            flops=images * STEP_HEADS * length * length * (256 if step == steps - 1 else 25600),
+            bytes_accessed=images * rows * length * (1 if step == steps - 1 else 22),
+            transcendentals=images * length,
         ),
         name="attend_backward",
     )(projected, projected, projected, context, grads, lse, mask, *held)
@@ -236,6 +236,11 @@
     return with_layout_constraint(values, Layout((0, 1)))
 
 
+def split_columns(total, widths):
+    ends = [sum(widths[:k]) for k in range(len(widths) + 1)]
+    return [total[:, a:b].astype(f32) for a, b in zip(ends[:-1], ends[1:])]
+
+
 def sum_pieces(wholes, group, member, piece):
     flight = yield [
         [swap(take_block(whole, member ^ j, piece), "seq", j) if j else whole for j in range(group)]
@@ -251,6 +256,8 @@
     wholes = yield [
         lax.psum_scatter(full, "fsdp", scatter_dimension=0, tiled=True) for full in fulls
     ]
+    widths = [whole.shape[1] for whole in wholes]
+    wholes = [jnp.concatenate(wholes, 1)]
     member = lax.axis_index("seq") % group
     piece = wholes[0].shape[0] // group
     if 1 in calls:
@@ -274,11 +281,13 @@
         bit *= 2
     if 3 in calls:
         flight = yield [exchange(jnp.broadcast_to(part, (group, *part.shape))) for part in parts]
-        return [came.reshape(group * piece, -1).astype(f32) for came in flight]
+        (total,) = [came.reshape(group * piece, -1) for came in flight]
+        return split_columns(total, widths)
     flight = yield [
         [swap(part, "seq", j) if j else part for j in range(group)] for part in parts
     ]
-    return [in_order(pieces, member).astype(f32) for pieces in flight]
+    (total,) = [in_order(pieces, member) for pieces in flight]
+    return split_columns(total, widths)
 
 
 def gather_chain(weight):
@@ -462,8 +471,8 @@
     pre_grad = (ein("itd,df->itf", out_grad_low, down_full) * slope.astype(f32)).astype(bf16)
     up_bias_grad = token_sum(pre_grad)
     up_grad = rows_first(ein("itd,itf->df", normed_two, pre_grad).astype(bf16))
-    pre_grad, up_grad, output = flow.point((pre_grad, up_grad, output))
-    flow.start("up", reduce_chain([up_grad], group, (1, 2, 3)))
+    pre_grad, up_grad, output = flow.point((pre_grad, up_grad, output), "down")
+    flow.start("up", reduce_chain([up_grad], group, (1, 2)))
     normed_two_grad = ein("itf,df->itd", pre_grad, up_full)
     hidden_grad = out_grad_low.astype(f32) + norm_grad(
         normed_two_grad, hat_two, scale_two, second_gain
@@ -475,11 +484,10 @@
     attn_grad_low = hidden_grad.astype(bf16)
     context_grad = ein("nd,itd->int", out_full, attn_grad_low).astype(bf16)
     out_grad = rows_first(ein("int,itd->nd", context, attn_grad_low).astype(bf16))
-    out_bias_grad = token_sum(attn_grad_low)
     context_grad, out_grad = flow.point((context_grad, out_grad), "down")
     grads, parts = None, []
     per_group = HEAD_GROUPS[0][1] // STEP_HEADS
-    points = ((), ("down", "up"), ("up",), ("up",))
+    points = (("up",), (), ("down",), ("up",))
     for step in range(len(HEAD_GROUPS) * per_group):
         number, inside = divmod(step, per_group)
         grads, part = attend_backward(
@@ -493,19 +501,27 @@
             grads,
             part if inside else None,
         )
-        grads, part, context_grad = flow.point((grads, part, context_grad), *points[step])
+        if step == 3:
+            out_bias_grad = token_sum(attn_grad_low)
+            bias_grads = [jnp.sum(parts[0].astype(f32), (0, 2))]
+            part, out_bias_grad, bias_grads = lax.optimization_barrier(
+                (part, out_bias_grad, bias_grads)
+            )
+        grads, part, context_grad, attn_grad_low, parts = flow.point(
+            (grads, part, context_grad, attn_grad_low, parts), *points[step]
+        )
         if inside == per_group - 1:
             part = part.reshape(part.shape[0], -1, SEQ)
             parts.append(part)
             weight_grad = rows_first(ein("itd,imt->dm", normed_one, part).astype(bf16))
             grads, weight_grad, context_grad = flow.point(
-                (grads, weight_grad, context_grad), *(["out_a"] if number else [])
+                (grads, weight_grad, context_grad), *(["out_a"] if number else ["up"])
             )
             if number:
                 flow.start("b", reduce_chain([weight_grad], group))
             else:
-                flow.start("out_a", reduce_chain([out_grad, weight_grad], group))
-    bias_grads = [jnp.sum(part.astype(f32), (0, 2)) for part in parts]
+                flow.start("out_a", reduce_chain([out_grad, weight_grad], group, (1,)))
+    bias_grads.append(jnp.sum(parts[1].astype(f32), (0, 2)))
     normed_one_grad = ein("imt,dm->itd", grads.reshape(projected.shape), project_full)
     query_bias_grad, value_bias_grad = ungroup(bias_grads, 0), ungroup(bias_grads, 2)
     hat_one, scale_one = norm_parts(inputs_low.astype(f32))

time: 704 us -> 682 us (0.969)
  waiting for transfers between devices: 148 us -> 138 us
    all_to_all x1, waiting for transfers between devices: 13.5 us -> 0.01 us  [reduce_chain(): lax.all_to_all(jnp.broadcast_to(part, (2, *part.shape)), 'seq', 0, 0, axi...]
    ppermute x37 -> x30, waiting for transfers between devices: 75.8 us -> 63.6 us  [swap(): lax.ppermute(values, axis, [(i, i ^ bits) for i in range(lax.axis_size(ax...]
    reduce_sum x2, other arithmetic: 13.6 us -> 3.04 us  [token_sum(): return jnp.sum(values.astype(f32), (0, 1))]
    reduce_scatter x5, waiting for transfers between devices: 0.04 us -> 8.91 us  [reduce_chain(): lax.psum_scatter(full, 'fsdp', scatter_dimension=0, tiled=True)]
    convert_element_type x4 -> x6, other arithmetic: 5.74 us -> 13.7 us  [the longest x1 6.4 us: body(): input_grad = (hidden_grad + norm_grad(normed_one_grad, hat_one, scale_one...]
    ppermute x37 -> x30, starting transfers between devices: 42.7 us -> 36.3 us  [swap(): lax.ppermute(values, axis, [(i, i ^ bits) for i in range(lax.axis_size(ax...]
  transfers between devices with their start and end apart: 53 -> 46, of which waited for: 23 -> 17; matrix products, arithmetic and copies ran while one was open for 48% -> 49% of each run, Pallas kernels for 12% -> 13%
where the time goes in v4:
time: 682 us; the launch traced here: 673 us
  matrix products  246 us (36%)
  waiting for transfers between devices  138 us (20%)
  Pallas kernels  86.5 us (13%)
  starting transfers between devices  73 us (11%)
  other arithmetic  70.4 us (10%)
  local copies, waits for them, and re-layouts  43.7 us (6%)
  between operations  15.5 us (2%)
    dot_general x13, matrix products, ein(): return jnp.einsum(spec, a, b, preferred_element_type=f32)  246 us
    ppermute x30, waiting for transfers between devices, swap(): lax.ppermute(values, axis, [(i, i ^ bits) for i in range(lax.axis_size(ax...  63.6 us
    pallas_call x4, Pallas kernels, attend_backward(): pl.pallas_call(attend_backward_kernel, grid=(images,), in_specs=sources +...  59.7 us
    all_to_all x7, waiting for transfers between devices, exchange(): return lax.all_to_all(blocks, 'seq', 0, 0, axis_index_groups=groups)  41.8 us
    ppermute x30, starting transfers between devices, swap(): lax.ppermute(values, axis, [(i, i ^ bits) for i in range(lax.axis_size(ax...  36.3 us
    all_to_all x7, starting transfers between devices, exchange(): return lax.all_to_all(blocks, 'seq', 0, 0, axis_index_groups=groups)  31.8 us
    pallas_call x1, Pallas kernels, attend_forward(): pl.pallas_call(attend_forward_kernel, grid=(images, steps), in_specs=sour...  26.8 us
    all_gather x3, waiting for transfers between devices, whole(): return lax.all_gather(weight, 'fsdp', axis=0, tiled=True)  22.1 us
  transfers between devices with their start and end apart: 46, of which 17 were waited for; matrix products, arithmetic and copies ran while one was open for 49% of the time, Pallas kernels for 13%

profile of v4, /device:TPU:0, one launch (start us, length us, event | category | flops | bytes accessed | tf_op | source)
XLA Modules:
  0.0 673.2 jit_solution(15033823036710770250)
XLA Ops:
  7.2 2.9 pad_maximum_fusion
  11.0 5.3 all-to-all-start
  23.1 31.9 %all-to-all-done = bf16[4,2,184,1152]{3,2,1,0:T(8,128)(2,1)S(1)} async-done(((bf16[4,2,184,1152]{3,2,1,0:T(8,128)(2,1)}), bf16[4,2,184,1152]{3,2,1,0:T(8,128)(2,1)S(1)}, u32[]{:S(2)}, u32[]{:S(2)}) %all-to-all-start) | async-done | bytes 3391520 | tf_op jit(solution)/shard_map/all_to_all | solution.py:188
  56.8 2.3 copy.63
  62.3 12.6 %all-gather.4.cloned.1.call-done = bf16[1152,3456]{1,0:T(8,128)(2,1)} async-done(((bf16[288,3456]{1,0:T(8,128)(2,1)}), bf16[1152,3456]{1,0:T(8,128)(2,1)}) %all-gather.4.cloned.1.call-update) | async-done | bytes 7962640 | tf_op jit(solution)/shard_map/all_gather | solution.py:422
  74.9 21.1 %fusion.19.q_ref.k_ref.v_ref = bf16[2,3456,736]{2,1,0:T(8,128)(2,1)} fusion(f32[3456]{0:T(1024)S(1)} %pad_maximum_fusion.7, bf16[1152,3456]{1,0:T(8,128)(2,1)} %all-gather.4.cloned.1.call-done, bf16[2,736,1152]{2,1,0:T(8,128)(2,1)S(1)} %bitcast.102, f32[1152]{0:T(1024)S(1)} %add.223, f32[1152]{0:T(1024)S(1)} %mul.159, f32[2,736]{1,0:T(2,128)S(1)} %add_rsqrt_fusion.1, ...), kind=kOutput, calls=%fused_computation.35 | convolution fusion | flops 11741331456 | bytes 21563392 | tf_op jit(solution)/shard_map/itd,dm->imt/dot_general | solution.py:357
  96.0 4.7 all-to-all-start.1
  101.3 26.8 %attend_forward.1 = (bf16[2,1152,736]{2,1,0:T(8,128)(2,1)S(1)}, f32[2,16,1,736]{3,2,1,0:T(1,128)S(1)}) custom-call(bf16[2,3456,736]{2,1,0:T(8,128)(2,1)} %fusion.19.q_ref.k_ref.v_ref, bf16[2,3456,736]{2,1,0:T(8,128)(2,1)} %fusion.19.q_ref.k_ref.v_ref, bf16[2,3456,736]{2,1,0:T(8,128)(2,1)} %fusion.19.q_ref.k_ref.v_ref, s32[2,1,736]{2,1,0:T(1,128)S(1)} %broadcast_in_dim.43.mask_ref), custom_call_target="tpu_custom_call" | custom-call | flops 17750294528 | bytes 13565952 | tf_op jit(solution)/shard_map/attend_forward/pallas_call | solution.py:78
  128.1 3.1 broadcast_select_fusion.7
  131.3 5.7 fusion.47
  137.1 2.9 copy-done.11
  140.8 3.3 all-gather.6.cloned.1.call-done
  144.1 36.4 %add_convert_fusion = (bf16[2,736,4304]{2,1,0:T(8,128)(2,1)}, bf16[2,736,4304]{2,1,0:T(8,128)(2,1)}) fusion(f32[4304]{0:T(1024)S(1)} %add.241, bf16[1152,4304]{1,0:T(8,128)(2,1)} %all-gather.6.cloned.1.call-done, f32[2,736,1152]{2,1,0:T(8,128)} %copy-done.11, f32[1152]{0:T(1024)S(1)} %add.238, f32[1152]{0:T(1024)S(1)} %mul.167, ...), kind=kOutput, calls=%fused_computation.4 | convolution fusion | flops 14725817344 | bytes 42079552 | tf_op jit(solution)/shard_map/itd,df->itf/dot_general | solution.py:357
  180.6 2.4 copy.67
  185.4 2.1 copy-done.67
  187.5 18.8 %fusion.1 = bf16[1152,4304]{1,0:T(8,128)(2,1)} fusion(bf16[2,736,1152]{2,1,0:T(8,128)(2,1)S(1)} %bitcast_select_fusion, bf16[2,736,4304]{2,1,0:T(8,128)(2,1)S(1)} %copy-done.67), kind=kOutput, calls=%fused_computation.9 | convolution fusion | flops 14601922560 | bytes 25978880 | tf_op jit(solution)/shard_map/itd,itf->df/dot_general | solution.py:357
  207.1 6.2 all-gather.8.cloned.1.call-done
  213.3 22.9 %add_convert_fusion.2 = bf16[2,736,1152]{2,1,0:T(8,128)(2,1)S(1)} fusion(f32[2,736,1152]{2,1,0:T(8,128)} %copy-done.11, bf16[2,736,4304]{2,1,0:T(8,128)(2,1)} %get-tuple-element.143, bf16[1152,4304]{1,0:T(8,128)(2,1)} %all-gather.8.cloned.1.call-done, f32[1152]{0:T(1024)S(1)} %add.250), kind=kOutput, calls=%fused_computation.54 | convolution fusion | flops 14602051584 | bytes 32766464 | tf_op jit(solution)/shard_map/itf,df->itd/dot_general | solution.py:357
  238.2 4.0 all-to-all-start.2
  242.3 25.5 %convert_reduce_fusion = (f32[4304]{0:T(1024)}, bf16[2,736,4304]{2,1,0:T(8,128)(2,1)}) fusion(bf16[2,736,4304]{2,1,0:T(8,128)(2,1)} %get-tuple-element.145, bf16[2,736,1152]{2,1,0:T(8,128)(2,1)} %copy-done.17, bf16[1152,4304]{1,0:T(8,128)(2,1)} %all-gather.8.cloned.1.call-done), kind=kOutput, calls=%fused_computation.2 | convolution fusion | flops 14628637696 | bytes 38667072 | tf_op jit(solution)/shard_map/itd,df->itf/dot_general | solution.py:357
  267.8 24.1 %fusion.2 = bf16[1152,4304]{1,0:T(8,128)(2,1)} fusion(bf16[2,736,4304]{2,1,0:T(8,128)(2,1)} %get-tuple-element.148, f32[2,736,1152]{2,1,0:T(8,128)} %copy-done.11, f32[1152]{0:T(1024)S(1)} %add.238, f32[1152]{0:T(1024)S(1)} %mul.167, f32[2,736]{1,0:T(2,128)S(1)} %add_rsqrt_fusion, f32[2,736]{1,0:T(2,128)S(1)} %broadcast_multiply_fusion.4), kind=kOutput, calls=%fused_computation.10 | convolution fusion | flops 14610401280 | bytes 29391360 | tf_op jit(solution)/shard_map/itd,itf->df/dot_general | solution.py:357
  292.0 6.1 reduce-scatter.6.cloned.1.call-done
  298.1 4.6 all-to-all-start.3
  302.7 28.8 %multiply_reduce_fusion = (f32[1152]{0:T(1024)}, f32[2,736]{1,0:T(2,128)S(1)}, f32[2,736]{1,0:T(2,128)S(1)}, f32[1152]{0:T(1024)}, f32[2,736,1152]{2,1,0:T(8,128)}) fusion(f32[2,736,1152]{2,1,0:T(8,128)} %copy-done.11, f32[2,736]{1,0:T(2,128)S(1)} %add_rsqrt_fusion, f32[2,736]{1,0:T(2,128)S(1)} %broadcast_multiply_fusion.4, f32[1152]{0:T(1024)S(1)} %mul.167, ...), kind=kOutput, calls=%fused_computation.50 | convolution fusion | flops 14612221952 | bytes 36190720 | tf_op jit(solution)/shard_map/itf,df->itd/dot_general | solution.py:357
  331.5 8.1 %multiply_add_fusion.1 = f32[2,736,1152]{2,1,0:T(8,128)} fusion(bf16[2,736,1152]{2,1,0:T(8,128)(2,1)S(1)} %copy-done.18, f32[2,736,1152]{2,1,0:T(8,128)} %get-tuple-element.310, f32[2,736,1152]{2,1,0:T(8,128)} %copy-done.11, f32[2,736]{1,0:T(2,128)S(1)} %get-tuple-element.314, f32[2,736]{1,0:T(2,128)S(1)} %get-tuple-element.315, f32[1152]{0:T(1024)S(1)} %mul.167, ...), kind=kLoop, calls=%fused_computation.52 | loop fusion | flops 15261696 | bytes 23768576 | tf_op jit(solution)/shard_map/add | solution.py:477
  339.7 3.1 reduce_sum.203
  344.8 3.3 convert_element_type.172
  349.9 6.4 convolution_convert_fusion
  356.3 5.9 copy.69
  362.2 8.1 %fusion.22 = bf16[1152,1152]{1,0:T(8,128)(2,1)} fusion(bf16[2,1152,736]{2,1,0:T(8,128)(2,1)S(1)} %copy-done.1, bf16[2,736,1152]{2,1,0:T(8,128)(2,1)} %copy-done.15), kind=kOutput, calls=%fused_computation.36 | convolution fusion | flops 3908321280 | bytes 9437184 | tf_op jit(solution)/shard_map/int,itd->nd/dot_general | solution.py:357
  370.3 2.7 collective-permute-done.5
  373.0 2.2 add_convert_fusion.5
  379.6 14.8 %attend_backward.4 = (bf16[2,3,1152,736]{3,2,1,0:T(8,128)(2,1)}, bf16[2,3,576,736]{3,2,1,0:T(8,128)(2,1)}) custom-call(bf16[2,3456,736]{2,1,0:T(8,128)(2,1)} %fusion.19.q_ref.k_ref.v_ref, bf16[2,3456,736]{2,1,0:T(8,128)(2,1)} %fusion.19.q_ref.k_ref.v_ref, bf16[2,3456,736]{2,1,0:T(8,128)(2,1)} %fusion.19.q_ref.k_ref.v_ref, ...), custom_call_target="tpu_custom_call" | custom-call | flops 110939340800 | bytes 9326592 | tf_op jit(solution)/shard_map/attend_backward/pallas_call | solution.py:148
  394.5 4.5 all-to-all-start.4
  399.9 14.8 %attend_backward.5 = (bf16[2,3,1152,736]{3,2,1,0:T(8,128)(2,1)}, bf16[2,3,576,736]{3,2,1,0:T(8,128)(2,1)}) custom-call(bf16[2,3456,736]{2,1,0:T(8,128)(2,1)} %fusion.19.q_ref.k_ref.v_ref, bf16[2,3456,736]{2,1,0:T(8,128)(2,1)} %fusion.19.q_ref.k_ref.v_ref, ...), custom_call_target="tpu_custom_call", output_to_operand_aliasing={{0}: (7, {}), {1}: (8, {})} | custom-call | flops 110939340800 | bytes 9326592 | tf_op jit(solution)/shard_map/attend_backward/pallas_call | solution.py:148
  414.7 12.2 %fusion.23 = bf16[1152,1728]{1,0:T(8,128)(2,1)} fusion(bf16[2,1728,736]{2,1,0:T(8,128)(2,1)} %bitcast.121, bf16[2,736,1152]{2,1,0:T(8,128)(2,1)S(1)} %bitcast.106, f32[1152]{0:T(1024)S(1)} %copy-done.56, f32[1152]{0:T(1024)S(1)} %copy-done.44, f32[2,736]{1,0:T(2,128)S(1)} %copy-done.49, f32[2,736]{1,0:T(2,128)S(1)} %copy-done.38), kind=kOutput, calls=%fused_computation.37 | convolution fusion | flops 5872656384 | bytes 12481024 | tf_op jit(solution)/shard_map/itd,imt->dm/dot_general | solution.py:357
  426.9 5.0 all-to-all-done.4
  431.9 3.1 reduce_sum.206
  435.0 2.2 broadcast_in_dim.46
  437.2 4.5 all-to-all-start.5
  443.4 14.9 %attend_backward.6 = (bf16[2,3,1152,736]{3,2,1,0:T(8,128)(2,1)}, bf16[2,3,576,736]{3,2,1,0:T(8,128)(2,1)}) custom-call(bf16[2,3456,736]{2,1,0:T(8,128)(2,1)} %fusion.19.q_ref.k_ref.v_ref, bf16[2,3456,736]{2,1,0:T(8,128)(2,1)} %fusion.19.q_ref.k_ref.v_ref, bf16[2,3456,736]{2,1,0:T(8,128)(2,1)} %fusion.19.q_ref.k_ref.v_ref, ...), custom_call_target="tpu_custom_call", output_to_operand_aliasing={{0}: (7, {})} | custom-call | flops 110939340800 | bytes 9326592 | tf_op jit(solution)/shard_map/attend_backward/pallas_call | solution.py:148
  458.3 15.2 %attend_backward.7 = (bf16[2,3,1152,736]{3,2,1,0:T(8,128)(2,1)}, bf16[2,3,576,736]{3,2,1,0:T(8,128)(2,1)}) custom-call(bf16[2,3456,736]{2,1,0:T(8,128)(2,1)} %fusion.19.q_ref.k_ref.v_ref, bf16[2,3456,736]{2,1,0:T(8,128)(2,1)} %fusion.19.q_ref.k_ref.v_ref, ...), custom_call_target="tpu_custom_call", output_to_operand_aliasing={{0}: (7, {}), {1}: (8, {})} | custom-call | flops 1109393408 | bytes 423936 | tf_op jit(solution)/shard_map/attend_backward/pallas_call | solution.py:148
  475.6 12.2 %fusion.24 = bf16[1152,1728]{1,0:T(8,128)(2,1)} fusion(bf16[2,1728,736]{2,1,0:T(8,128)(2,1)} %bitcast.108, bf16[2,736,1152]{2,1,0:T(8,128)(2,1)S(1)} %bitcast.107, f32[1152]{0:T(1024)S(1)} %copy-done.57, f32[1152]{0:T(1024)S(1)} %copy-done.45, f32[2,736]{1,0:T(2,128)S(1)} %copy-done.50, f32[2,736]{1,0:T(2,128)S(1)} %copy-done.38), kind=kOutput, calls=%fused_computation.38 | convolution fusion | flops 5872656384 | bytes 12481024 | tf_op jit(solution)/shard_map/itd,imt->dm/dot_general | solution.py:357
  487.8 2.8 reduce-scatter.12.cloned.1.call-done
  490.8 2.5 convert_reduce_fusion.4
  494.8 2.5 collective-permute-start.11
  498.3 4.0 convert_reduce_fusion.1
  503.8 4.8 all-to-all-start.6
  508.6 23.4 %fusion.32 = (f32[1152]{0:T(1024)S(1)}, f32[2,736]{1,0:T(2,128)S(1)}, f32[2,736]{1,0:T(2,128)S(1)}, f32[1152]{0:T(1024)S(1)}, f32[2,736,1152]{2,1,0:T(8,128)}) fusion(bf16[2,736,1152]{2,1,0:T(8,128)(2,1)} %bitcast.104, f32[2,736]{1,0:T(2,128)S(1)} %copy-done.50, f32[2,736]{1,0:T(2,128)S(1)} %copy-done.38, f32[1152]{0:T(1024)S(1)} %copy-done.45, ...), kind=kOutput, calls=%fused_computation.46 | convolution fusion | flops 11737935872 | bytes 28348928 | tf_op jit(solution)/shard_map/imt,dm->itd/dot_general | solution.py:357
  532.1 6.4 fusion.31
  538.5 4.9 all-to-all-done.6
  543.4 3.9 copy.84
  547.3 3.9 all-to-all-start.7
  553.2 2.6 convert_bitcast_fusion
  558.6 2.6 reduce_sum.216
  561.1 2.4 collective-permute-start.12
  564.8 3.0 collective-permute-start.15
  570.3 36.6 %collective-permute-done.15 = bf16[72,1728]{1,0:T(8,128)(2,1)S(1)} collective-permute-done((bf16[72,1728]{1,0:T(8,128)(2,1)S(1)}, bf16[72,1728]{1,0:T(8,128)(2,1)S(1)}, u32[]{:S(2)}, u32[]{:S(2)}) %collective-permute-start.15) | collective-permute-done | bytes 248864 | tf_op jit(solution)/shard_map/ppermute | solution.py:178
  606.9 3.6 collective-permute-done.14
  620.5 2.4 collective-permute-start.22
  622.8 2.6 maximum_convert_fusion
  625.4 13.8 %collective-permute-done.22 = bf16[72,1728]{1,0:T(8,128)(2,1)S(1)} collective-permute-done((bf16[72,1728]{1,0:T(8,128)(2,1)S(1)}, bf16[72,1728]{1,0:T(8,128)(2,1)S(1)}, u32[]{:S(2)}, u32[]{:S(2)}) %collective-permute-start.22) | collective-permute-done | bytes 248864 | tf_op jit(solution)/shard_map/ppermute | solution.py:178
  642.9 3.2 collective-permute-start.28
  653.1 2.9 collective-permute-done.29
  (290 shorter events, 75.3 us)
Async XLA Ops:
  7.2 67.7 %all-gather.4.cloned.1.call-start = ((), (), s32[]{:S(2)}) async-start(), calls=%async_computation.13 | async-start | bytes 9953280 | tf_op jit(solution)/shard_map/all_gather | solution.py:422
  10.2 133.9 %all-gather.6.cloned.1.call-start = ((), (), s32[]{:S(2)}) async-start(), calls=%async_computation.14 | async-start | bytes 12533760 | tf_op jit(solution)/shard_map/all_gather | solution.py:422
  11.0 44.0 %all-to-all-start = ((bf16[4,2,184,1152]{3,2,1,0:T(8,128)(2,1)}), bf16[4,2,184,1152]{3,2,1,0:T(8,128)(2,1)S(1)}, u32[]{:S(2)}, u32[]{:S(2)}) async-start(bf16[4,2,184,1152]{3,2,1,0:T(8,128)(2,1)} %bitcast.123), calls=%async_computation | async-start | bytes 6782976 | tf_op jit(solution)/shard_map/all_to_all | solution.py:188
  16.3 197.0 %all-gather.8.cloned.1.call-start = ((), (), s32[]{:S(2)}) async-start(), calls=%async_computation.15 | async-start | bytes 12533760 | tf_op jit(solution)/shard_map/all_gather | solution.py:422
  16.5 1.2 collective-permute-start
  17.7 3.8 collective-permute-start.1
  20.7 80.6 %copy-start.6 = (s32[2,1,736]{2,1,0:T(1,128)}, s32[2,1,736]{2,1,0:T(1,128)S(1)}, u32[]{:S(2)}) copy-start(s32[2,1,736]{2,1,0:T(1,128)S(1)} %broadcast_in_dim.43.mask_ref) | copy-start | bytes 17668
  22.6 52.3 %copy-start.43 = (f32[1152]{0:T(1024)}, f32[1152]{0:T(1024)S(1)}, u32[]{:S(2)}) copy-start(f32[1152]{0:T(1024)S(1)} %mul.159) | copy-start | bytes 13828
  22.8 52.1 %copy-start.55 = (f32[1152]{0:T(1024)}, f32[1152]{0:T(1024)S(1)}, u32[]{:S(2)}) copy-start(f32[1152]{0:T(1024)S(1)} %add.223) | copy-start | bytes 13828
  59.1 72.3 %copy-start.8 = (bf16[2,4,184,1152]{3,2,1,0:T(8,128)(2,1)}, bf16[2,4,184,1152]{3,2,1,0:T(8,128)(2,1)S(1)}, u32[]{:S(2)}) copy-start(bf16[2,4,184,1152]{3,2,1,0:T(8,128)(2,1)S(1)} %copy.63) | copy-start | bytes 10174468
  59.1 36.9 %collective-permute-start.3 = (bf16[288,1152]{1,0:T(8,128)(2,1)}, bf16[288,1152]{1,0:T(8,128)(2,1)}, u32[]{:S(2)}, u32[]{:S(2)}) collective-permute-start(bf16[288,1152]{1,0:T(8,128)(2,1)} %param.27), channel_id=1, source_target_pairs={{0,2},{1,3},{2,0},{3,1},{4,6},{5,7},{6,4},{7,5},{8,10},{9,11},{10,... | collective-permute-start | bytes 1990664 | tf_op jit(solution)/shard_map/ppermute | solution.py:178
  60.7 35.3 %collective-permute-start.2 = (bf16[288,1152]{1,0:T(8,128)(2,1)}, bf16[288,1152]{1,0:T(8,128)(2,1)}, u32[]{:S(2)}, u32[]{:S(2)}) collective-permute-start(bf16[288,1152]{1,0:T(8,128)(2,1)} %param.27), channel_id=1, source_target_pairs={{0,1},{1,0},{2,3},{3,2},{4,5},{5,4},{6,7},{7,6},{8,9},{9,8},{10,11... | collective-permute-start | bytes 1990664 | tf_op jit(solution)/shard_map/ppermute | solution.py:178
  61.2 34.7 %copy-start.37 = (f32[2,736]{1,0:T(2,128)}, f32[2,736]{1,0:T(2,128)S(1)}, u32[]{:S(2)}) copy-start(f32[2,736]{1,0:T(2,128)S(1)} %broadcast_multiply_fusion.5) | copy-start | bytes 17668
  62.3 33.7 %copy-start.48 = (f32[2,736]{1,0:T(2,128)}, f32[2,736]{1,0:T(2,128)S(1)}, u32[]{:S(2)}) copy-start(f32[2,736]{1,0:T(2,128)S(1)} %add_rsqrt_fusion.1) | copy-start | bytes 17668
  96.0 84.5 %all-to-all-start.1 = ((bf16[4,2,184,1152]{3,2,1,0:T(8,128)(2,1)}), bf16[4,2,184,1152]{3,2,1,0:T(8,128)(2,1)}, u32[]{:S(2)}, u32[]{:S(2)}) async-start(bf16[4,2,184,1152]{3,2,1,0:T(8,128)(2,1)} %bitcast.124), calls=%async_computation.1 | async-start | bytes 6782976 | tf_op jit(solution)/shard_map/all_to_all | solution.py:188
  100.7 197.3 %reduce-scatter.6.cloned.1.call-start = ((), (), s32[]{:S(2)}) async-start(), calls=%async_computation.16 | async-start | bytes 12533760 | tf_op jit(solution)/shard_map/reduce_scatter | solution.py:257
  101.0 27.1 %collective-permute-start.4 = (bf16[288,1152]{1,0:T(8,128)(2,1)}, bf16[288,1152]{1,0:T(8,128)(2,1)S(1)}, u32[]{:S(2)}, u32[]{:S(2)}) collective-permute-start(bf16[288,1152]{1,0:T(8,128)(2,1)} %collective-permute-done.3), channel_id=1, source_target_pairs={{0,1},{1,0},{2,3},{3,2},{4,5},{5,4},{6,7},{7,6},{8,9},{9,8},{10,11... | collective-permute-start | bytes 1990664 | tf_op jit(solution)/shard_map/ppermute | solution.py:178
  238.2 53.7 %all-to-all-start.2 = ((bf16[4,2,184,1152]{3,2,1,0:T(8,128)(2,1)}), bf16[4,2,184,1152]{3,2,1,0:T(8,128)(2,1)S(1)}, u32[]{:S(2)}, u32[]{:S(2)}) async-start(bf16[4,2,184,1152]{3,2,1,0:T(8,128)(2,1)} %bitcast.117), calls=%async_computation.2 | async-start | bytes 6782976 | tf_op jit(solution)/shard_map/all_to_all | solution.py:188
  242.2 152.2 %reduce-scatter.8.cloned.1.call-start = ((), (), s32[]{:S(2)}) async-start(), calls=%async_computation.17 | async-start | bytes 12533760 | tf_op jit(solution)/shard_map/reduce_scatter | solution.py:257
  298.1 41.5 %all-to-all-start.3 = ((bf16[4,72,4304]{2,1,0:T(8,128)(2,1)}), bf16[4,72,4304]{2,1,0:T(8,128)(2,1)}, u32[]{:S(2)}, u32[]{:S(2)}) async-start(bf16[4,72,4304]{2,1,0:T(8,128)(2,1)} %bitcast.128), calls=%async_computation.4 | async-start | bytes 5013504 | tf_op jit(solution)/shard_map/all_to_all | solution.py:188
  302.7 28.9 %copy-start.18 = (bf16[2,736,1152]{2,1,0:T(8,128)(2,1)S(1)}, bf16[2,736,1152]{2,1,0:T(8,128)(2,1)}, u32[]{:S(2)}) copy-start(bf16[2,736,1152]{2,1,0:T(8,128)(2,1)} %copy-done.17) | copy-start | bytes 10174468
  302.7 185.1 %reduce-scatter.10.cloned.1.call-start = ((), (), s32[]{:S(2)}) async-start(), calls=%async_computation.18 | async-start | bytes 3317760 | tf_op jit(solution)/shard_map/reduce_scatter | solution.py:257
  342.8 30.2 %collective-permute-start.5 = (bf16[72,4304]{1,0:T(8,128)(2,1)}, bf16[72,4304]{1,0:T(8,128)(2,1)}, u32[]{:S(2)}, u32[]{:S(2)}) collective-permute-start(bf16[72,4304]{1,0:T(8,128)(2,1)} %reduce_sum.203), channel_id=1, source_target_pairs={{0,16},{4,20},{8,24},{12,28},{16,0},{20,4},{24,8},{28,12},{1,17},{... | collective-permute-start | bytes 1859336 | tf_op jit(solution)/shard_map/ppermute | solution.py:178
  362.2 16.5 %copy-start.7 = (s32[2,1,736]{2,1,0:T(1,128)S(1)}, s32[2,1,736]{2,1,0:T(1,128)}, u32[]{:S(2)}) copy-start(s32[2,1,736]{2,1,0:T(1,128)} %copy-done.6) | copy-start | bytes 17668
  375.2 83.1 %collective-permute-start.8 = (bf16[72,4304]{1,0:T(8,128)(2,1)}, bf16[72,4304]{1,0:T(8,128)(2,1)}, u32[]{:S(2)}, u32[]{:S(2)}) collective-permute-start(bf16[72,4304]{1,0:T(8,128)(2,1)} %add_convert_fusion.5), channel_id=1, source_target_pairs={{0,12},{4,8},{8,4},{12,0},{16,28},{20,24},{24,20},{28,16},{1,13},{... | collective-permute-start | bytes 1859336 | tf_op jit(solution)/shard_map/ppermute | solution.py:178
  376.4 81.9 %collective-permute-start.7 = (bf16[72,4304]{1,0:T(8,128)(2,1)}, bf16[72,4304]{1,0:T(8,128)(2,1)}, u32[]{:S(2)}, u32[]{:S(2)}) collective-permute-start(bf16[72,4304]{1,0:T(8,128)(2,1)} %add_convert_fusion.5), channel_id=1, source_target_pairs={{0,8},{4,12},{8,0},{12,4},{16,24},{20,28},{24,16},{28,20},{1,9},{5... | collective-permute-start | bytes 1859336 | tf_op jit(solution)/shard_map/ppermute | solution.py:178
  378.0 80.3 %collective-permute-start.6 = (bf16[72,4304]{1,0:T(8,128)(2,1)}, bf16[72,4304]{1,0:T(8,128)(2,1)}, u32[]{:S(2)}, u32[]{:S(2)}) collective-permute-start(bf16[72,4304]{1,0:T(8,128)(2,1)} %add_convert_fusion.5), channel_id=1, source_target_pairs={{0,4},{4,0},{8,12},{12,8},{16,20},{20,16},{24,28},{28,24},{1,5},{5... | collective-permute-start | bytes 1859336 | tf_op jit(solution)/shard_map/ppermute | solution.py:178
  394.5 37.5 %all-to-all-start.4 = ((bf16[4,72,4304]{2,1,0:T(8,128)(2,1)}), bf16[4,72,4304]{2,1,0:T(8,128)(2,1)}, u32[]{:S(2)}, u32[]{:S(2)}) async-start(bf16[4,72,4304]{2,1,0:T(8,128)(2,1)} %bitcast.127), calls=%async_computation.6 | async-start | bytes 5013504 | tf_op jit(solution)/shard_map/all_to_all | solution.py:188
  437.2 37.7 %all-to-all-start.5 = ((bf16[2,72,4304]{2,1,0:T(8,128)(2,1)}), bf16[2,72,4304]{2,1,0:T(8,128)(2,1)}, u32[]{:S(2)}, u32[]{:S(2)}) async-start(bf16[2,72,4304]{2,1,0:T(8,128)(2,1)} %broadcast_in_dim.46), calls=%async_computation.7 | async-start | bytes 2506752 | tf_op jit(solution)/shard_map/all_to_all | solution.py:273
  441.7 48.9 %reduce-scatter.12.cloned.1.call-start = ((), (), s32[]{:S(2)}) async-start(), calls=%async_computation.19 | async-start | bytes 5160960 | tf_op jit(solution)/shard_map/reduce_scatter | solution.py:257
  442.5 100.9 %reduce-scatter.14.cloned.1.call-start = ((), (), s32[]{:S(2)}) async-start(), calls=%async_computation.20 | async-start | bytes 5160960 | tf_op jit(solution)/shard_map/reduce_scatter | solution.py:257
  458.3 15.3 %copy-start.16 = (bf16[2,736,1152]{2,1,0:T(8,128)(2,1)S(1)}, bf16[2,736,1152]{2,1,0:T(8,128)(2,1)}, u32[]{:S(2)}) copy-start(bf16[2,736,1152]{2,1,0:T(8,128)(2,1)} %copy-done.15) | copy-start | bytes 10174468
  458.3 15.8 %copy-start.19 = (bf16[2,3,576,736]{3,2,1,0:T(8,128)(2,1)S(1)}, bf16[2,3,576,736]{3,2,1,0:T(8,128)(2,1)}, u32[]{:S(2)}) copy-start(bf16[2,3,576,736]{3,2,1,0:T(8,128)(2,1)} %get-tuple-element.166) | copy-start | bytes 15261700
  494.8 43.7 %collective-permute-start.11 = (bf16[72,4304]{1,0:T(8,128)(2,1)S(1)}, bf16[72,4304]{1,0:T(8,128)(2,1)}, u32[]{:S(2)}, u32[]{:S(2)}) collective-permute-start(bf16[72,4304]{1,0:T(8,128)(2,1)S(1)} %fusion.37), channel_id=1, source_target_pairs={{0,12},{4,8},{8,4},{12,0},{16,28},{20,24},{24,20},{28,16},{1,13},{... | collective-permute-start | bytes 1859336 | tf_op jit(solution)/shard_map/ppermute | solution.py:178
  497.3 41.3 %collective-permute-start.10 = (bf16[72,4304]{1,0:T(8,128)(2,1)S(1)}, bf16[72,4304]{1,0:T(8,128)(2,1)}, u32[]{:S(2)}, u32[]{:S(2)}) collective-permute-start(bf16[72,4304]{1,0:T(8,128)(2,1)S(1)} %fusion.37), channel_id=1, source_target_pairs={{0,8},{4,12},{8,0},{12,4},{16,24},{20,28},{24,16},{28,20},{1,9},{5... | collective-permute-start | bytes 1859336 | tf_op jit(solution)/shard_map/ppermute | solution.py:178
  497.8 40.7 %collective-permute-start.9 = (bf16[72,4304]{1,0:T(8,128)(2,1)S(1)}, bf16[72,4304]{1,0:T(8,128)(2,1)}, u32[]{:S(2)}, u32[]{:S(2)}) collective-permute-start(bf16[72,4304]{1,0:T(8,128)(2,1)S(1)} %fusion.37), channel_id=1, source_target_pairs={{0,4},{4,0},{8,12},{12,8},{16,20},{20,16},{24,28},{28,24},{1,5},{5... | collective-permute-start | bytes 1859336 | tf_op jit(solution)/shard_map/ppermute | solution.py:178
  503.8 28.3 %slice-start = ((s8[6782976]{0:T(1024)(128)(4,1)}), s8[2588672]{0:T(1024)(128)(4,1)S(1)}, s32[]{:S(2)}) async-start(s8[6782976]{0:T(1024)(128)(4,1)} %bitcast.98), calls=%async_computation.21 | async-start | bytes 5177344
  503.8 39.6 %all-to-all-start.6 = ((bf16[4,72,2880]{2,1,0:T(8,128)(2,1)}), bf16[4,72,2880]{2,1,0:T(8,128)(2,1)}, u32[]{:S(2)}, u32[]{:S(2)}) async-start(bf16[4,72,2880]{2,1,0:T(8,128)(2,1)} %bitcast.120), calls=%async_computation.10 | async-start | bytes 3391488 | tf_op jit(solution)/shard_map/all_to_all | solution.py:188
  508.6 23.5 %slice-start.1 = ((s8[6782976]{0:T(1024)(128)(4,1)}), s8[4194304]{0:T(1024)(128)(4,1)S(1)}, s32[]{:S(2)}) async-start(s8[6782976]{0:T(1024)(128)(4,1)} %bitcast.98), calls=%async_computation.22 | async-start | bytes 8388608
  547.3 94.4 %all-to-all-start.7 = ((bf16[4,2,184,1152]{3,2,1,0:T(8,128)(2,1)}), bf16[4,2,184,1152]{3,2,1,0:T(8,128)(2,1)S(1)}, u32[]{:S(2)}, u32[]{:S(2)}) async-start(bf16[4,2,184,1152]{3,2,1,0:T(8,128)(2,1)} %bitcast.116), calls=%async_computation.12 | async-start | bytes 6782976 | tf_op jit(solution)/shard_map/all_to_all | solution.py:188
  556.6 11.1 %collective-permute-start.18 = (f32[4,3380]{1,0:T(4,128)S(1)}, f32[4,3380]{1,0:T(4,128)S(1)}, u32[]{:S(2)}, u32[]{:S(2)}) collective-permute-start(f32[4,3380]{1,0:T(4,128)S(1)} %concatenate.65), channel_id=1, source_target_pairs={{0,3},{1,2},{2,1},{3,0},{4,7},{5,6},{6,5},{7,4},{8,11},{9,10},{10,... | collective-permute-start | bytes 162248 | tf_op jit(solution)/shard_map/ppermute | solution.py:178
  556.7 11.6 %collective-permute-start.17 = (f32[4,3380]{1,0:T(4,128)S(1)}, f32[4,3380]{1,0:T(4,128)}, u32[]{:S(2)}, u32[]{:S(2)}) collective-permute-start(f32[4,3380]{1,0:T(4,128)S(1)} %concatenate.65), channel_id=1, source_target_pairs={{0,2},{1,3},{2,0},{3,1},{4,6},{5,7},{6,4},{7,5},{8,10},{9,11},{10,... | collective-permute-start | bytes 162248 | tf_op jit(solution)/shard_map/ppermute | solution.py:178
  558.3 12.0 %collective-permute-start.16 = (f32[4,3380]{1,0:T(4,128)S(1)}, f32[4,3380]{1,0:T(4,128)}, u32[]{:S(2)}, u32[]{:S(2)}) collective-permute-start(f32[4,3380]{1,0:T(4,128)S(1)} %concatenate.65), channel_id=1, source_target_pairs={{0,1},{1,0},{2,3},{3,2},{4,5},{5,4},{6,7},{7,6},{8,9},{9,8},{10,11... | collective-permute-start | bytes 162248 | tf_op jit(solution)/shard_map/ppermute | solution.py:178
  561.1 53.8 %copy-start.22 = (bf16[72,2880]{1,0:T(8,128)(2,1)S(1)}, bf16[72,2880]{1,0:T(8,128)(2,1)}, u32[]{:S(2)}) copy-start(bf16[72,2880]{1,0:T(8,128)(2,1)} %reduce_sum.216) | copy-start | bytes 1244164
  561.1 49.4 %collective-permute-start.12 = (bf16[72,2880]{1,0:T(8,128)(2,1)}, bf16[72,2880]{1,0:T(8,128)(2,1)S(1)}, u32[]{:S(2)}, u32[]{:S(2)}) collective-permute-start(bf16[72,2880]{1,0:T(8,128)(2,1)} %reduce_sum.216), channel_id=1, source_target_pairs={{0,16},{4,20},{8,24},{12,28},{16,0},{20,4},{24,8},{28,12},{1,17},{... | collective-permute-start | bytes 1244168 | tf_op jit(solution)/shard_map/ppermute | solution.py:178
  564.8 42.1 %collective-permute-start.15 = (bf16[72,1728]{1,0:T(8,128)(2,1)S(1)}, bf16[72,1728]{1,0:T(8,128)(2,1)S(1)}, u32[]{:S(2)}, u32[]{:S(2)}) collective-permute-start(bf16[72,1728]{1,0:T(8,128)(2,1)S(1)} %get-tuple-element.291), channel_id=1, source_target_pairs={{0,12},{4,8},{8,4},{12,0},{16,28},{20,24},{24,20},{28,16},{1,13},{... | collective-permute-start | bytes 746504 | tf_op jit(solution)/shard_map/ppermute | solution.py:178
  567.8 42.7 %copy-start.42 = (f32[4,3380]{1,0:T(4,128)}, f32[4,3380]{1,0:T(4,128)S(1)}, u32[]{:S(2)}) copy-start(f32[4,3380]{1,0:T(4,128)S(1)} %collective-permute-done.18) | copy-start | bytes 162244
  567.8 42.7 %collective-permute-start.14 = (bf16[72,1728]{1,0:T(8,128)(2,1)S(1)}, bf16[72,1728]{1,0:T(8,128)(2,1)S(1)}, u32[]{:S(2)}, u32[]{:S(2)}) collective-permute-start(bf16[72,1728]{1,0:T(8,128)(2,1)S(1)} %get-tuple-element.292), channel_id=1, source_target_pairs={{0,8},{4,12},{8,0},{12,4},{16,24},{20,28},{24,16},{28,20},{1,9},{5... | collective-permute-start | bytes 746504 | tf_op jit(solution)/shard_map/ppermute | solution.py:178
  568.3 42.2 %collective-permute-start.13 = (bf16[72,1728]{1,0:T(8,128)(2,1)S(1)}, bf16[72,1728]{1,0:T(8,128)(2,1)S(1)}, u32[]{:S(2)}, u32[]{:S(2)}) collective-permute-start(bf16[72,1728]{1,0:T(8,128)(2,1)S(1)} %get-tuple-element.293), channel_id=1, source_target_pairs={{0,4},{4,0},{8,12},{12,8},{16,20},{20,16},{24,28},{28,24},{1,5},{5... | collective-permute-start | bytes 746504 | tf_op jit(solution)/shard_map/ppermute | solution.py:178
  611.4 7.8 %collective-permute-start.25 = (f32[4,3380]{1,0:T(4,128)S(1)}, f32[4,3380]{1,0:T(4,128)S(1)}, u32[]{:S(2)}, u32[]{:S(2)}) collective-permute-start(f32[4,3380]{1,0:T(4,128)S(1)} %add_add_fusion.1), channel_id=1, source_target_pairs={{0,12},{4,8},{8,4},{12,0},{16,28},{20,24},{24,20},{28,16},{1,13},{... | collective-permute-start | bytes 162248 | tf_op jit(solution)/shard_map/ppermute | solution.py:178
  612.9 6.9 %collective-permute-start.24 = (f32[4,3380]{1,0:T(4,128)S(1)}, f32[4,3380]{1,0:T(4,128)S(1)}, u32[]{:S(2)}, u32[]{:S(2)}) collective-permute-start(f32[4,3380]{1,0:T(4,128)S(1)} %add_add_fusion.1), channel_id=1, source_target_pairs={{0,8},{4,12},{8,0},{12,4},{16,24},{20,28},{24,16},{28,20},{1,9},{5... | collective-permute-start | bytes 162248 | tf_op jit(solution)/shard_map/ppermute | solution.py:178
  614.4 11.0 %collective-permute-start.23 = (f32[4,3380]{1,0:T(4,128)S(1)}, f32[4,3380]{1,0:T(4,128)S(1)}, u32[]{:S(2)}, u32[]{:S(2)}) collective-permute-start(f32[4,3380]{1,0:T(4,128)S(1)} %add_add_fusion.1), channel_id=1, source_target_pairs={{0,4},{4,0},{8,12},{12,8},{16,20},{20,16},{24,28},{28,24},{1,5},{5... | collective-permute-start | bytes 162248 | tf_op jit(solution)/shard_map/ppermute | solution.py:178
  615.1 25.8 %copy-start.21 = (bf16[72,2880]{1,0:T(8,128)(2,1)}, bf16[72,2880]{1,0:T(8,128)(2,1)S(1)}, u32[]{:S(2)}) copy-start(bf16[72,2880]{1,0:T(8,128)(2,1)S(1)} %add_convert_fusion.6) | copy-start | bytes 1244164
  615.1 24.1 %collective-permute-start.21 = (bf16[72,2880]{1,0:T(8,128)(2,1)S(1)}, bf16[72,2880]{1,0:T(8,128)(2,1)S(1)}, u32[]{:S(2)}, u32[]{:S(2)}) collective-permute-start(bf16[72,2880]{1,0:T(8,128)(2,1)S(1)} %add_convert_fusion.6), channel_id=1, source_target_pairs={{0,12},{4,8},{8,4},{12,0},{16,28},{20,24},{24,20},{28,16},{1,13},{... | collective-permute-start | bytes 1244168 | tf_op jit(solution)/shard_map/ppermute | solution.py:178
  616.6 24.4 %collective-permute-start.20 = (bf16[72,2880]{1,0:T(8,128)(2,1)S(1)}, bf16[72,2880]{1,0:T(8,128)(2,1)S(1)}, u32[]{:S(2)}, u32[]{:S(2)}) collective-permute-start(bf16[72,2880]{1,0:T(8,128)(2,1)S(1)} %add_convert_fusion.6), channel_id=1, source_target_pairs={{0,8},{4,12},{8,0},{12,4},{16,24},{20,28},{24,16},{28,20},{1,9},{5... | collective-permute-start | bytes 1244168 | tf_op jit(solution)/shard_map/ppermute | solution.py:178
  619.2 21.8 %copy-start.24 = (bf16[72,1728]{1,0:T(8,128)(2,1)}, bf16[72,1728]{1,0:T(8,128)(2,1)S(1)}, u32[]{:S(2)}) copy-start(bf16[72,1728]{1,0:T(8,128)(2,1)S(1)} %add_convert_fusion.8) | copy-start | bytes 746500
  619.2 26.9 %copy-start.39 = (f32[4,3380]{1,0:T(4,128)}, f32[4,3380]{1,0:T(4,128)S(1)}, u32[]{:S(2)}) copy-start(f32[4,3380]{1,0:T(4,128)S(1)} %collective-permute-done.25) | copy-start | bytes 162244
  619.2 22.5 %collective-permute-start.19 = (bf16[72,2880]{1,0:T(8,128)(2,1)S(1)}, bf16[72,2880]{1,0:T(8,128)(2,1)}, u32[]{:S(2)}, u32[]{:S(2)}) collective-permute-start(bf16[72,2880]{1,0:T(8,128)(2,1)S(1)} %add_convert_fusion.6), channel_id=1, source_target_pairs={{0,4},{4,0},{8,12},{12,8},{16,20},{20,16},{24,28},{28,24},{1,5},{5... | collective-permute-start | bytes 1244168 | tf_op jit(solution)/shard_map/ppermute | solution.py:178
  620.5 18.7 %collective-permute-start.22 = (bf16[72,1728]{1,0:T(8,128)(2,1)S(1)}, bf16[72,1728]{1,0:T(8,128)(2,1)S(1)}, u32[]{:S(2)}, u32[]{:S(2)}) collective-permute-start(bf16[72,1728]{1,0:T(8,128)(2,1)S(1)} %add_convert_fusion.8), channel_id=1, source_target_pairs={{0,16},{4,20},{8,24},{12,28},{16,0},{20,4},{24,8},{28,12},{1,17},{... | collective-permute-start | bytes 746504 | tf_op jit(solution)/shard_map/ppermute | solution.py:178
  625.4 15.5 %copy-start.41 = (f32[4,3380]{1,0:T(4,128)}, f32[4,3380]{1,0:T(4,128)S(1)}, u32[]{:S(2)}) copy-start(f32[4,3380]{1,0:T(4,128)S(1)} %collective-permute-done.23) | copy-start | bytes 162244
  642.9 13.1 %collective-permute-start.28 = (bf16[72,1728]{1,0:T(8,128)(2,1)S(1)}, bf16[72,1728]{1,0:T(8,128)(2,1)S(1)}, u32[]{:S(2)}, u32[]{:S(2)}) collective-permute-start(bf16[72,1728]{1,0:T(8,128)(2,1)S(1)} %add_convert_fusion.7), channel_id=1, source_target_pairs={{0,12},{4,8},{8,4},{12,0},{16,28},{20,24},{24,20},{28,16},{1,13},{... | collective-permute-start | bytes 746504 | tf_op jit(solution)/shard_map/ppermute | solution.py:178
  646.0 10.8 %collective-permute-start.27 = (bf16[72,1728]{1,0:T(8,128)(2,1)S(1)}, bf16[72,1728]{1,0:T(8,128)(2,1)S(1)}, u32[]{:S(2)}, u32[]{:S(2)}) collective-permute-start(bf16[72,1728]{1,0:T(8,128)(2,1)S(1)} %add_convert_fusion.7), channel_id=1, source_target_pairs={{0,8},{4,12},{8,0},{12,4},{16,24},{20,28},{24,16},{28,20},{1,9},{5... | collective-permute-start | bytes 746504 | tf_op jit(solution)/shard_map/ppermute | solution.py:178
  646.1 10.6 %collective-permute-start.26 = (bf16[72,1728]{1,0:T(8,128)(2,1)S(1)}, bf16[72,1728]{1,0:T(8,128)(2,1)S(1)}, u32[]{:S(2)}, u32[]{:S(2)}) collective-permute-start(bf16[72,1728]{1,0:T(8,128)(2,1)S(1)} %add_convert_fusion.7), channel_id=1, source_target_pairs={{0,4},{4,0},{8,12},{12,8},{16,20},{20,16},{24,28},{28,24},{1,5},{5... | collective-permute-start | bytes 746504 | tf_op jit(solution)/shard_map/ppermute | solution.py:178
  648.4 7.5 %collective-permute-start.29 = (f32[4,3380]{1,0:T(4,128)S(1)}, f32[4,3380]{1,0:T(4,128)S(1)}, u32[]{:S(2)}, u32[]{:S(2)}) collective-permute-start(f32[4,3380]{1,0:T(4,128)S(1)} %add_add_fusion), channel_id=1, source_target_pairs={{0,16},{4,20},{8,24},{12,28},{16,0},{20,4},{24,8},{28,12},{1,17},{... | collective-permute-start | bytes 162248 | tf_op jit(solution)/shard_map/ppermute | solution.py:178
  (52 other events, 310.8 us)
Sparse Core Ops, SparseCore 0:
  10.4 64.4 all-gather.3
  76.4 67.6 all-gather.5
  145.7 67.5 all-gather.7
  215.8 82.2 reduce-scatter.5
  300.5 82.2 reduce-scatter.7
  385.8 34.8 reduce-scatter.9
  445.9 44.6 reduce-scatter.11
  493.7 44.0 reduce-scatter.13

commit v5 on v4

--- a/solution.py
+++ b/solution.py
@@ -474,15 +474,23 @@
     pre_grad, up_grad, output = flow.point((pre_grad, up_grad, output), "down")
     flow.start("up", reduce_chain([up_grad], group, (1, 2)))
     normed_two_grad = ein("itf,df->itd", pre_grad, up_full)
-    hidden_grad = out_grad_low.astype(f32) + norm_grad(
-        normed_two_grad, hat_two, scale_two, second_gain
-    )
-    second_gain_grad = jnp.sum(normed_two_grad * hat_two, (0, 1))
-    second_shift_grad = jnp.sum(normed_two_grad, (0, 1))
-    hidden_grad, output = flow.point((hidden_grad, output), "down")
+    scaled_grad = normed_two_grad * second_gain
+    norm_sums = (
+        jnp.mean(scaled_grad, -1, keepdims=True),
+        jnp.mean(scaled_grad * hat_two, -1, keepdims=True),
+        jnp.sum(normed_two_grad * hat_two, (0, 1)),
+        jnp.sum(normed_two_grad, (0, 1)),
+    )
+    normed_two_grad, norm_sums, output = flow.point((normed_two_grad, norm_sums, output), "down")
+    mean_grad, mean_hat_grad, second_gain_grad, second_shift_grad = norm_sums
+    hidden_grad = out_grad_low.astype(f32) + scale_two * (
+        normed_two_grad * second_gain - mean_grad - hat_two * mean_hat_grad
+    )
 
     attn_grad_low = hidden_grad.astype(bf16)
-    context_grad = ein("nd,itd->int", out_full, attn_grad_low).astype(bf16)
+    context_grad = with_layout_constraint(
+        ein("nd,itd->int", out_full, attn_grad_low).astype(bf16), Layout((0, 1, 2))
+    )
     out_grad = rows_first(ein("int,itd->nd", context, attn_grad_low).astype(bf16))
     context_grad, out_grad = flow.point((context_grad, out_grad), "down")
     grads, parts = None, []

time: 682 us -> 674 us (0.988)
    add x1 -> x0, other arithmetic: 8.12 us -> none  [body(): out_grad_low.astype(f32)]
    unnamed x142 -> x144, local copies, waits for them, and re-layouts: 19.3 us -> 20.2 us
where the time goes in v5:
time: 674 us; the launch traced here: 665 us
  matrix products  246 us (36%)
  waiting for transfers between devices  132 us (20%)
  Pallas kernels  86.7 us (13%)
  starting transfers between devices  73.8 us (11%)
  other arithmetic  70 us (10%)
  local copies, waits for them, and re-layouts  41.3 us (6%)
  between operations  15.6 us (2%)
    dot_general x13, matrix products, ein(): return jnp.einsum(spec, a, b, preferred_element_type=f32)  246 us
    ppermute x30, waiting for transfers between devices, swap(): lax.ppermute(values, axis, [(i, i ^ bits) for i in range(lax.axis_size(ax...  63.5 us
    pallas_call x4, Pallas kernels, attend_backward(): pl.pallas_call(attend_backward_kernel, grid=(images,), in_specs=sources +...  60 us
    all_to_all x7, waiting for transfers between devices, exchange(): return lax.all_to_all(blocks, 'seq', 0, 0, axis_index_groups=groups)  37.1 us
    ppermute x30, starting transfers between devices, swap(): lax.ppermute(values, axis, [(i, i ^ bits) for i in range(lax.axis_size(ax...  36.3 us
    all_to_all x7, starting transfers between devices, exchange(): return lax.all_to_all(blocks, 'seq', 0, 0, axis_index_groups=groups)  32.3 us
    pallas_call x1, Pallas kernels, attend_forward(): pl.pallas_call(attend_forward_kernel, grid=(images, steps), in_specs=sour...  26.8 us
    all_gather x3, waiting for transfers between devices, whole(): return lax.all_gather(weight, 'fsdp', axis=0, tiled=True)  23.3 us
  transfers between devices with their start and end apart: 46, of which 17 were waited for; matrix products, arithmetic and copies ran while one was open for 49% of the time, Pallas kernels for 13%

profile of v5, /device:TPU:0, one launch (start us, length us, event | category | flops | bytes accessed | tf_op | source)
XLA Modules:
  0.0 665.3 jit_solution(4695029843529432375)
XLA Ops:
  7.3 2.9 pad_maximum_fusion
  11.0 5.3 all-to-all-start
  23.1 31.9 %all-to-all-done = bf16[4,2,184,1152]{3,2,1,0:T(8,128)(2,1)S(1)} async-done(((bf16[4,2,184,1152]{3,2,1,0:T(8,128)(2,1)}), bf16[4,2,184,1152]{3,2,1,0:T(8,128)(2,1)S(1)}, u32[]{:S(2)}, u32[]{:S(2)}) %all-to-all-start) | async-done | bytes 3391520 | tf_op jit(solution)/shard_map/all_to_all | solution.py:188
  56.8 2.3 copy.61
  62.3 12.6 %all-gather.4.cloned.1.call-done = bf16[1152,3456]{1,0:T(8,128)(2,1)} async-done(((bf16[288,3456]{1,0:T(8,128)(2,1)}), bf16[1152,3456]{1,0:T(8,128)(2,1)}) %all-gather.4.cloned.1.call-update) | async-done | bytes 7962640 | tf_op jit(solution)/shard_map/all_gather | solution.py:422
  74.9 21.1 %fusion.19.q_ref.k_ref.v_ref = bf16[2,3456,736]{2,1,0:T(8,128)(2,1)} fusion(f32[3456]{0:T(1024)S(1)} %pad_maximum_fusion.7, bf16[1152,3456]{1,0:T(8,128)(2,1)} %all-gather.4.cloned.1.call-done, bf16[2,736,1152]{2,1,0:T(8,128)(2,1)S(1)} %bitcast.109, f32[1152]{0:T(1024)S(1)} %add.223, f32[1152]{0:T(1024)S(1)} %mul.167, f32[2,736]{1,0:T(2,128)S(1)} %add_rsqrt_fusion.1, ...), kind=kOutput, calls=%fused_computation.35 | convolution fusion | flops 11741331456 | bytes 21563392 | tf_op jit(solution)/shard_map/itd,dm->imt/dot_general | solution.py:357
  96.0 4.8 all-to-all-start.1
  101.7 26.8 %attend_forward.1 = (bf16[2,1152,736]{2,1,0:T(8,128)(2,1)S(1)}, f32[2,16,1,736]{3,2,1,0:T(1,128)S(1)}) custom-call(bf16[2,3456,736]{2,1,0:T(8,128)(2,1)} %fusion.19.q_ref.k_ref.v_ref, bf16[2,3456,736]{2,1,0:T(8,128)(2,1)} %fusion.19.q_ref.k_ref.v_ref, bf16[2,3456,736]{2,1,0:T(8,128)(2,1)} %fusion.19.q_ref.k_ref.v_ref, s32[2,1,736]{2,1,0:T(1,128)S(1)} %broadcast_in_dim.43.mask_ref), custom_call_target="tpu_custom_call" | custom-call | flops 17750294528 | bytes 13565952 | tf_op jit(solution)/shard_map/attend_forward/pallas_call | solution.py:78
  128.5 3.1 broadcast_select_fusion.7
  131.7 5.7 fusion.49
  137.4 2.9 copy-done.8
  141.2 3.0 all-gather.6.cloned.1.call-done
  144.1 36.2 %add_convert_fusion = (bf16[2,736,4304]{2,1,0:T(8,128)(2,1)}, bf16[2,736,4304]{2,1,0:T(8,128)(2,1)}) fusion(f32[4304]{0:T(1024)S(1)} %add.241, bf16[1152,4304]{1,0:T(8,128)(2,1)} %all-gather.6.cloned.1.call-done, f32[2,736,1152]{2,1,0:T(8,128)} %copy-done.8, f32[1152]{0:T(1024)S(1)} %add.238, f32[1152]{0:T(1024)S(1)} %mul.175, ...), kind=kOutput, calls=%fused_computation.4 | convolution fusion | flops 14725817344 | bytes 42079552 | tf_op jit(solution)/shard_map/itd,df->itf/dot_general | solution.py:357
  180.4 2.4 copy.65
  183.4 2.6 copy-done.68
  186.0 18.8 %fusion.1 = bf16[1152,4304]{1,0:T(8,128)(2,1)} fusion(bf16[2,736,1152]{2,1,0:T(8,128)(2,1)S(1)} %bitcast_select_fusion, bf16[2,736,4304]{2,1,0:T(8,128)(2,1)S(1)} %copy-done.68), kind=kOutput, calls=%fused_computation.9 | convolution fusion | flops 14601922560 | bytes 25978880 | tf_op jit(solution)/shard_map/itd,itf->df/dot_general | solution.py:357
  205.6 7.8 %all-gather.8.cloned.1.call-done = bf16[1152,4304]{1,0:T(8,128)(2,1)} async-done(((bf16[288,4304]{1,0:T(8,128)(2,1)}), bf16[1152,4304]{1,0:T(8,128)(2,1)}) %all-gather.8.cloned.1.call-update) | async-done | bytes 9916432 | tf_op jit(solution)/shard_map/all_gather | solution.py:422
  213.3 23.9 %add_convert_fusion.2 = bf16[2,736,1152]{2,1,0:T(8,128)(2,1)} fusion(f32[2,736,1152]{2,1,0:T(8,128)} %copy-done.8, bf16[2,736,4304]{2,1,0:T(8,128)(2,1)} %get-tuple-element.147, bf16[1152,4304]{1,0:T(8,128)(2,1)} %all-gather.8.cloned.1.call-done, f32[1152]{0:T(1024)S(1)} %add.250), kind=kOutput, calls=%fused_computation.54 | convolution fusion | flops 14602051584 | bytes 32766464 | tf_op jit(solution)/shard_map/itf,df->itd/dot_general | solution.py:357
  237.2 4.0 copy.82
  241.2 4.7 all-to-all-start.2
  246.0 24.8 %convert_reduce_fusion = (f32[4304]{0:T(1024)}, bf16[2,736,4304]{2,1,0:T(8,128)(2,1)}) fusion(bf16[2,736,4304]{2,1,0:T(8,128)(2,1)} %get-tuple-element.149, bf16[2,736,1152]{2,1,0:T(8,128)(2,1)S(1)} %bitcast_select_fusion, bf16[1152,4304]{1,0:T(8,128)(2,1)} %all-gather.8.cloned.1.call-done), kind=kOutput, calls=%fused_computation.2 | convolution fusion | flops 14628637696 | bytes 38667072 | tf_op jit(solution)/shard_map/itd,df->itf/dot_general | solution.py:357
  270.8 24.0 %fusion.2 = bf16[1152,4304]{1,0:T(8,128)(2,1)} fusion(bf16[2,736,4304]{2,1,0:T(8,128)(2,1)} %get-tuple-element.152, f32[2,736,1152]{2,1,0:T(8,128)} %copy-done.8, f32[1152]{0:T(1024)S(1)} %add.238, f32[1152]{0:T(1024)S(1)} %mul.175, f32[2,736]{1,0:T(2,128)S(1)} %add_rsqrt_fusion, f32[2,736]{1,0:T(2,128)S(1)} %broadcast_multiply_fusion.2), kind=kOutput, calls=%fused_computation.10 | convolution fusion | flops 14610401280 | bytes 29391360 | tf_op jit(solution)/shard_map/itd,itf->df/dot_general | solution.py:357
  294.8 3.3 reduce-scatter.6.cloned.1.call-done
  298.9 3.7 all-to-all-start.3
  302.6 28.2 %multiply_reduce_fusion = (f32[1152]{0:T(1024)}, f32[2,736]{1,0:T(2,128)S(1)}, f32[2,736]{1,0:T(2,128)S(1)}, f32[1152]{0:T(1024)}, f32[2,736,1152]{2,1,0:T(8,128)}) fusion(f32[2,736,1152]{2,1,0:T(8,128)} %copy-done.8, f32[2,736]{1,0:T(2,128)S(1)} %add_rsqrt_fusion, f32[2,736]{1,0:T(2,128)S(1)} %broadcast_multiply_fusion.2, f32[1152]{0:T(1024)S(1)} %mul.175, ...), kind=kOutput, calls=%fused_computation.52 | convolution fusion | flops 14612221952 | bytes 36190720 | tf_op jit(solution)/shard_map/itf,df->itd/dot_general | solution.py:357
  333.4 2.4 collective-permute-start.5
  335.8 7.4 %fusion.44 = bf16[2,736,1152]{2,1,0:T(8,128)(2,1)S(1)} fusion(f32[2,736]{1,0:T(2,128)} %bitcast.131, f32[2,736,1152]{2,1,0:T(8,128)} %copy-done.8, f32[2,736]{1,0:T(2,128)S(1)} %broadcast_multiply_fusion.2, f32[2,736]{1,0:T(2,128)} %bitcast.133, f32[2,736,1152]{2,1,0:T(8,128)} %get-tuple-element.156, f32[1152]{0:T(1024)S(1)} %mul.175, ...), kind=kLoop, calls=%fused_computation.161 | loop fusion | flops 16957440 | bytes 20377088 | tf_op jit(solution)/shard_map/convert_element_type | solution.py:490
  345.0 6.2 fusion.22
  351.2 9.3 %fusion.37.grad_ref = bf16[2,1152,736]{2,1,0:T(8,128)(2,1)} fusion(bf16[2,736,1152]{2,1,0:T(8,128)(2,1)} %copy-done.14, bf16[288,1152]{1,0:T(8,128)(2,1)} %copy-done.26, bf16[288,1152]{1,0:T(8,128)(2,1)} %copy-done.25, bf16[288,1152]{1,0:T(8,128)(2,1)} %copy-done.24, bf16[288,1152]{1,0:T(8,128)(2,1)} %copy-done.23), kind=kOutput, calls=%fused_computation.62 | convolution fusion | flops 3919306752 | bytes 9437184 | tf_op jit(solution)/shard_map/nd,itd->int/dot_general | solution.py:357
  360.5 2.7 collective-permute-done.5
  363.2 2.2 add_convert_fusion.5
  369.9 14.7 %attend_backward.4 = (bf16[2,3,1152,736]{3,2,1,0:T(8,128)(2,1)}, bf16[2,3,576,736]{3,2,1,0:T(8,128)(2,1)}) custom-call(bf16[2,3456,736]{2,1,0:T(8,128)(2,1)} %fusion.19.q_ref.k_ref.v_ref, bf16[2,3456,736]{2,1,0:T(8,128)(2,1)} %fusion.19.q_ref.k_ref.v_ref, bf16[2,3456,736]{2,1,0:T(8,128)(2,1)} %fusion.19.q_ref.k_ref.v_ref, ...), custom_call_target="tpu_custom_call" | custom-call | flops 110939340800 | bytes 9326592 | tf_op jit(solution)/shard_map/attend_backward/pallas_call | solution.py:148
  384.5 4.8 all-to-all-start.4
  390.2 15.2 %attend_backward.5 = (bf16[2,3,1152,736]{3,2,1,0:T(8,128)(2,1)}, bf16[2,3,576,736]{3,2,1,0:T(8,128)(2,1)}) custom-call(bf16[2,3456,736]{2,1,0:T(8,128)(2,1)} %fusion.19.q_ref.k_ref.v_ref, bf16[2,3456,736]{2,1,0:T(8,128)(2,1)} %fusion.19.q_ref.k_ref.v_ref, ...), custom_call_target="tpu_custom_call", output_to_operand_aliasing={{0}: (7, {}), {1}: (8, {})} | custom-call | flops 110939340800 | bytes 9326592 | tf_op jit(solution)/shard_map/attend_backward/pallas_call | solution.py:148
  405.4 12.2 %fusion.23 = bf16[1152,1728]{1,0:T(8,128)(2,1)} fusion(bf16[2,1728,736]{2,1,0:T(8,128)(2,1)} %bitcast.123, bf16[2,736,1152]{2,1,0:T(8,128)(2,1)S(1)} %bitcast.113, f32[1152]{0:T(1024)S(1)} %copy-done.55, f32[1152]{0:T(1024)S(1)} %copy-done.45, f32[2,736]{1,0:T(2,128)S(1)} %copy-done.50, f32[2,736]{1,0:T(2,128)S(1)} %copy-done.43), kind=kOutput, calls=%fused_computation.37 | convolution fusion | flops 5872656384 | bytes 12481024 | tf_op jit(solution)/shard_map/itd,imt->dm/dot_general | solution.py:357
  417.6 4.6 all-to-all-done.4
  422.2 3.1 reduce_sum.208
  425.3 2.2 broadcast_in_dim.46
  427.5 4.5 all-to-all-start.5
  433.7 14.9 %attend_backward.6 = (bf16[2,3,1152,736]{3,2,1,0:T(8,128)(2,1)}, bf16[2,3,576,736]{3,2,1,0:T(8,128)(2,1)}) custom-call(bf16[2,3456,736]{2,1,0:T(8,128)(2,1)} %fusion.19.q_ref.k_ref.v_ref, bf16[2,3456,736]{2,1,0:T(8,128)(2,1)} %fusion.19.q_ref.k_ref.v_ref, bf16[2,3456,736]{2,1,0:T(8,128)(2,1)} %fusion.19.q_ref.k_ref.v_ref, ...), custom_call_target="tpu_custom_call", output_to_operand_aliasing={{0}: (7, {})} | custom-call | flops 110939340800 | bytes 9326592 | tf_op jit(solution)/shard_map/attend_backward/pallas_call | solution.py:148
  448.6 15.2 %attend_backward.7 = (bf16[2,3,1152,736]{3,2,1,0:T(8,128)(2,1)}, bf16[2,3,576,736]{3,2,1,0:T(8,128)(2,1)}) custom-call(bf16[2,3456,736]{2,1,0:T(8,128)(2,1)} %fusion.19.q_ref.k_ref.v_ref, bf16[2,3456,736]{2,1,0:T(8,128)(2,1)} %fusion.19.q_ref.k_ref.v_ref, ...), custom_call_target="tpu_custom_call", output_to_operand_aliasing={{0}: (7, {}), {1}: (8, {})} | custom-call | flops 1109393408 | bytes 423936 | tf_op jit(solution)/shard_map/attend_backward/pallas_call | solution.py:148
  465.9 12.2 %fusion.24 = bf16[1152,1728]{1,0:T(8,128)(2,1)} fusion(bf16[2,1728,736]{2,1,0:T(8,128)(2,1)} %bitcast.115, bf16[2,736,1152]{2,1,0:T(8,128)(2,1)S(1)} %bitcast.114, f32[1152]{0:T(1024)S(1)} %copy-done.56, f32[1152]{0:T(1024)S(1)} %copy-done.46, f32[2,736]{1,0:T(2,128)S(1)} %copy-done.51, f32[2,736]{1,0:T(2,128)S(1)} %copy-done.43), kind=kOutput, calls=%fused_computation.38 | convolution fusion | flops 5872656384 | bytes 12481024 | tf_op jit(solution)/shard_map/itd,imt->dm/dot_general | solution.py:357
  478.1 2.6 reduce-scatter.12.cloned.1.call-done
  480.7 2.5 convert_reduce_fusion.4
  484.6 2.4 collective-permute-start.11
  488.2 4.0 convert_reduce_fusion.1
  493.7 4.8 all-to-all-start.6
  498.6 23.5 %fusion.32 = (f32[1152]{0:T(1024)S(1)}, f32[2,736]{1,0:T(2,128)S(1)}, f32[2,736]{1,0:T(2,128)S(1)}, f32[1152]{0:T(1024)S(1)}, f32[2,736,1152]{2,1,0:T(8,128)}) fusion(bf16[2,736,1152]{2,1,0:T(8,128)(2,1)} %bitcast.111, f32[2,736]{1,0:T(2,128)S(1)} %copy-done.51, f32[2,736]{1,0:T(2,128)S(1)} %copy-done.43, f32[1152]{0:T(1024)S(1)} %copy-done.46, ...), kind=kOutput, calls=%fused_computation.46 | convolution fusion | flops 11737935872 | bytes 28348928 | tf_op jit(solution)/shard_map/imt,dm->itd/dot_general | solution.py:357
  522.2 11.1 %fusion.31 = bf16[2,736,1152]{2,1,0:T(8,128)(2,1)} fusion(bf16[2,736,1152]{2,1,0:T(8,128)(2,1)} %bitcast.112, f32[2,736,1152]{2,1,0:T(8,128)} %get-tuple-element.319, f32[2,736]{1,0:T(2,128)S(1)} %broadcast_multiply_fusion, f32[2,736]{1,0:T(2,128)S(1)} %broadcast_multiply_fusion.1, f32[1152]{0:T(1024)S(1)} %copy-done.46, f32[2,736]{1,0:T(2,128)S(1)} %copy-done.51, ...), kind=kLoop, calls=%fused_computation.45 | loop fusion | flops 32219136 | bytes 30579712 | tf_op jit(solution)/shard_map/convert_element_type | solution.py:540
  533.3 4.0 copy.81
  537.3 4.3 all-to-all-start.7
  543.5 2.6 convert_bitcast_fusion
  548.9 2.6 reduce_sum.216
  551.5 2.4 collective-permute-start.12
  555.1 3.0 collective-permute-start.15
  560.7 36.6 %collective-permute-done.15 = bf16[72,1728]{1,0:T(8,128)(2,1)S(1)} collective-permute-done((bf16[72,1728]{1,0:T(8,128)(2,1)S(1)}, bf16[72,1728]{1,0:T(8,128)(2,1)S(1)}, u32[]{:S(2)}, u32[]{:S(2)}) %collective-permute-start.15) | collective-permute-done | bytes 248864 | tf_op jit(solution)/shard_map/ppermute | solution.py:178
  597.3 3.1 collective-permute-done.14
  610.4 2.4 collective-permute-start.22
  612.8 2.6 maximum_convert_fusion
  615.4 13.4 %collective-permute-done.22 = bf16[72,1728]{1,0:T(8,128)(2,1)S(1)} collective-permute-done((bf16[72,1728]{1,0:T(8,128)(2,1)S(1)}, bf16[72,1728]{1,0:T(8,128)(2,1)S(1)}, u32[]{:S(2)}, u32[]{:S(2)}) %collective-permute-start.22) | collective-permute-done | bytes 248864 | tf_op jit(solution)/shard_map/ppermute | solution.py:178
  628.8 2.1 collective-permute-done.20
  632.8 3.2 collective-permute-start.28
  642.7 3.2 collective-permute-done.29
  652.5 4.0 copy.90
  (290 shorter events, 69.0 us)
Async XLA Ops:
  7.3 67.6 %all-gather.4.cloned.1.call-start = ((), (), s32[]{:S(2)}) async-start(), calls=%async_computation.13 | async-start | bytes 9953280 | tf_op jit(solution)/shard_map/all_gather | solution.py:422
  10.3 133.9 %all-gather.6.cloned.1.call-start = ((), (), s32[]{:S(2)}) async-start(), calls=%async_computation.14 | async-start | bytes 12533760 | tf_op jit(solution)/shard_map/all_gather | solution.py:422
  11.0 44.0 %all-to-all-start = ((bf16[4,2,184,1152]{3,2,1,0:T(8,128)(2,1)}), bf16[4,2,184,1152]{3,2,1,0:T(8,128)(2,1)S(1)}, u32[]{:S(2)}, u32[]{:S(2)}) async-start(bf16[4,2,184,1152]{3,2,1,0:T(8,128)(2,1)} %bitcast.125), calls=%async_computation | async-start | bytes 6782976 | tf_op jit(solution)/shard_map/all_to_all | solution.py:188
  16.3 197.0 %all-gather.8.cloned.1.call-start = ((), (), s32[]{:S(2)}) async-start(), calls=%async_computation.15 | async-start | bytes 12533760 | tf_op jit(solution)/shard_map/all_gather | solution.py:422
  16.5 1.2 collective-permute-start
  17.8 3.8 collective-permute-start.1
  20.7 80.9 %copy-start.6 = (s32[2,1,736]{2,1,0:T(1,128)}, s32[2,1,736]{2,1,0:T(1,128)S(1)}, u32[]{:S(2)}) copy-start(s32[2,1,736]{2,1,0:T(1,128)S(1)} %broadcast_in_dim.43.mask_ref) | copy-start | bytes 17668
  22.6 313.2 %copy-start.32 = (f32[1152]{0:T(1024)}, f32[1152]{0:T(1024)S(1)}, u32[]{:S(2)}) copy-start(f32[1152]{0:T(1024)S(1)} %mul.175) | copy-start | bytes 13828
  22.7 52.2 %copy-start.44 = (f32[1152]{0:T(1024)}, f32[1152]{0:T(1024)S(1)}, u32[]{:S(2)}) copy-start(f32[1152]{0:T(1024)S(1)} %mul.167) | copy-start | bytes 13828
  22.8 52.1 %copy-start.54 = (f32[1152]{0:T(1024)}, f32[1152]{0:T(1024)S(1)}, u32[]{:S(2)}) copy-start(f32[1152]{0:T(1024)S(1)} %add.223) | copy-start | bytes 13828
  59.1 72.6 %copy-start.9 = (bf16[2,4,184,1152]{3,2,1,0:T(8,128)(2,1)}, bf16[2,4,184,1152]{3,2,1,0:T(8,128)(2,1)S(1)}, u32[]{:S(2)}) copy-start(bf16[2,4,184,1152]{3,2,1,0:T(8,128)(2,1)S(1)} %copy.61) | copy-start | bytes 10174468
  59.1 36.9 %collective-permute-start.3 = (bf16[288,1152]{1,0:T(8,128)(2,1)}, bf16[288,1152]{1,0:T(8,128)(2,1)}, u32[]{:S(2)}, u32[]{:S(2)}) collective-permute-start(bf16[288,1152]{1,0:T(8,128)(2,1)} %param.27), channel_id=1, source_target_pairs={{0,2},{1,3},{2,0},{3,1},{4,6},{5,7},{6,4},{7,5},{8,10},{9,11},{10,... | collective-permute-start | bytes 1990664 | tf_op jit(solution)/shard_map/ppermute | solution.py:178
  60.7 35.3 %collective-permute-start.2 = (bf16[288,1152]{1,0:T(8,128)(2,1)}, bf16[288,1152]{1,0:T(8,128)(2,1)}, u32[]{:S(2)}, u32[]{:S(2)}) collective-permute-start(bf16[288,1152]{1,0:T(8,128)(2,1)} %param.27), channel_id=1, source_target_pairs={{0,1},{1,0},{2,3},{3,2},{4,5},{5,4},{6,7},{7,6},{8,9},{9,8},{10,11... | collective-permute-start | bytes 1990664 | tf_op jit(solution)/shard_map/ppermute | solution.py:178
  61.3 34.7 %copy-start.42 = (f32[2,736]{1,0:T(2,128)}, f32[2,736]{1,0:T(2,128)S(1)}, u32[]{:S(2)}) copy-start(f32[2,736]{1,0:T(2,128)S(1)} %broadcast_multiply_fusion.3) | copy-start | bytes 17668
  62.3 33.7 %copy-start.49 = (f32[2,736]{1,0:T(2,128)}, f32[2,736]{1,0:T(2,128)S(1)}, u32[]{:S(2)}) copy-start(f32[2,736]{1,0:T(2,128)S(1)} %add_rsqrt_fusion.1) | copy-start | bytes 17668
  96.0 84.3 %all-to-all-start.1 = ((bf16[4,2,184,1152]{3,2,1,0:T(8,128)(2,1)}), bf16[4,2,184,1152]{3,2,1,0:T(8,128)(2,1)}, u32[]{:S(2)}, u32[]{:S(2)}) async-start(bf16[4,2,184,1152]{3,2,1,0:T(8,128)(2,1)} %bitcast.126), calls=%async_computation.1 | async-start | bytes 6782976 | tf_op jit(solution)/shard_map/all_to_all | solution.py:188
  100.8 197.3 %reduce-scatter.6.cloned.1.call-start = ((), (), s32[]{:S(2)}) async-start(), calls=%async_computation.16 | async-start | bytes 12533760 | tf_op jit(solution)/shard_map/reduce_scatter | solution.py:257
  101.3 27.1 %collective-permute-start.4 = (bf16[288,1152]{1,0:T(8,128)(2,1)}, bf16[288,1152]{1,0:T(8,128)(2,1)S(1)}, u32[]{:S(2)}, u32[]{:S(2)}) collective-permute-start(bf16[288,1152]{1,0:T(8,128)(2,1)} %collective-permute-done.3), channel_id=1, source_target_pairs={{0,1},{1,0},{2,3},{3,2},{4,5},{5,4},{6,7},{7,6},{8,9},{9,8},{10,11... | collective-permute-start | bytes 1990664 | tf_op jit(solution)/shard_map/ppermute | solution.py:178
  137.4 198.4 %copy-start.30 = (f32[2,736]{1,0:T(2,128)}, f32[2,736]{1,0:T(2,128)S(1)}, u32[]{:S(2)}) copy-start(f32[2,736]{1,0:T(2,128)S(1)} %broadcast_multiply_fusion.2) | copy-start | bytes 17668
  141.2 161.4 %copy-start.38 = (f32[2,736]{1,0:T(2,128)}, f32[2,736]{1,0:T(2,128)S(1)}, u32[]{:S(2)}) copy-start(f32[2,736]{1,0:T(2,128)S(1)} %add_rsqrt_fusion) | copy-start | bytes 17668
  186.0 59.9 %copy-start.12 = (bf16[2,736,1152]{2,1,0:T(8,128)(2,1)}, bf16[2,736,1152]{2,1,0:T(8,128)(2,1)S(1)}, u32[]{:S(2)}) copy-start(bf16[2,736,1152]{2,1,0:T(8,128)(2,1)S(1)} %bitcast_select_fusion) | copy-start | bytes 10174468
  241.2 53.6 %all-to-all-start.2 = ((bf16[4,2,184,1152]{3,2,1,0:T(8,128)(2,1)}), bf16[4,2,184,1152]{3,2,1,0:T(8,128)(2,1)}, u32[]{:S(2)}, u32[]{:S(2)}) async-start(bf16[4,2,184,1152]{3,2,1,0:T(8,128)(2,1)} %bitcast.119), calls=%async_computation.2 | async-start | bytes 6782976 | tf_op jit(solution)/shard_map/all_to_all | solution.py:188
  245.9 138.6 %reduce-scatter.8.cloned.1.call-start = ((), (), s32[]{:S(2)}) async-start(), calls=%async_computation.17 | async-start | bytes 12533760 | tf_op jit(solution)/shard_map/reduce_scatter | solution.py:257
  298.9 33.2 %all-to-all-start.3 = ((bf16[4,72,4304]{2,1,0:T(8,128)(2,1)}), bf16[4,72,4304]{2,1,0:T(8,128)(2,1)S(1)}, u32[]{:S(2)}, u32[]{:S(2)}) async-start(bf16[4,72,4304]{2,1,0:T(8,128)(2,1)} %bitcast.130), calls=%async_computation.4 | async-start | bytes 5013504 | tf_op jit(solution)/shard_map/all_to_all | solution.py:188
  302.6 175.5 %reduce-scatter.10.cloned.1.call-start = ((), (), s32[]{:S(2)}) async-start(), calls=%async_computation.18 | async-start | bytes 3317760 | tf_op jit(solution)/shard_map/reduce_scatter | solution.py:257
  333.4 29.8 %collective-permute-start.5 = (bf16[72,4304]{1,0:T(8,128)(2,1)}, bf16[72,4304]{1,0:T(8,128)(2,1)}, u32[]{:S(2)}, u32[]{:S(2)}) collective-permute-start(bf16[72,4304]{1,0:T(8,128)(2,1)} %reduce_sum.205), channel_id=1, source_target_pairs={{0,16},{4,20},{8,24},{12,28},{16,0},{20,4},{24,8},{28,12},{1,17},{... | collective-permute-start | bytes 1859336 | tf_op jit(solution)/shard_map/ppermute | solution.py:178
  365.5 83.1 %collective-permute-start.8 = (bf16[72,4304]{1,0:T(8,128)(2,1)}, bf16[72,4304]{1,0:T(8,128)(2,1)}, u32[]{:S(2)}, u32[]{:S(2)}) collective-permute-start(bf16[72,4304]{1,0:T(8,128)(2,1)} %add_convert_fusion.5), channel_id=1, source_target_pairs={{0,12},{4,8},{8,4},{12,0},{16,28},{20,24},{24,20},{28,16},{1,13},{... | collective-permute-start | bytes 1859336 | tf_op jit(solution)/shard_map/ppermute | solution.py:178
  366.7 81.9 %collective-permute-start.7 = (bf16[72,4304]{1,0:T(8,128)(2,1)}, bf16[72,4304]{1,0:T(8,128)(2,1)}, u32[]{:S(2)}, u32[]{:S(2)}) collective-permute-start(bf16[72,4304]{1,0:T(8,128)(2,1)} %add_convert_fusion.5), channel_id=1, source_target_pairs={{0,8},{4,12},{8,0},{12,4},{16,24},{20,28},{24,16},{28,20},{1,9},{5... | collective-permute-start | bytes 1859336 | tf_op jit(solution)/shard_map/ppermute | solution.py:178
  368.3 80.3 %collective-permute-start.6 = (bf16[72,4304]{1,0:T(8,128)(2,1)}, bf16[72,4304]{1,0:T(8,128)(2,1)}, u32[]{:S(2)}, u32[]{:S(2)}) collective-permute-start(bf16[72,4304]{1,0:T(8,128)(2,1)} %add_convert_fusion.5), channel_id=1, source_target_pairs={{0,4},{4,0},{8,12},{12,8},{16,20},{20,16},{24,28},{28,24},{1,5},{5... | collective-permute-start | bytes 1859336 | tf_op jit(solution)/shard_map/ppermute | solution.py:178
  384.5 37.7 %all-to-all-start.4 = ((bf16[4,72,4304]{2,1,0:T(8,128)(2,1)}), bf16[4,72,4304]{2,1,0:T(8,128)(2,1)}, u32[]{:S(2)}, u32[]{:S(2)}) async-start(bf16[4,72,4304]{2,1,0:T(8,128)(2,1)} %bitcast.129), calls=%async_computation.6 | async-start | bytes 5013504 | tf_op jit(solution)/shard_map/all_to_all | solution.py:188
  427.5 37.8 %all-to-all-start.5 = ((bf16[2,72,4304]{2,1,0:T(8,128)(2,1)}), bf16[2,72,4304]{2,1,0:T(8,128)(2,1)}, u32[]{:S(2)}, u32[]{:S(2)}) async-start(bf16[2,72,4304]{2,1,0:T(8,128)(2,1)} %broadcast_in_dim.46), calls=%async_computation.7 | async-start | bytes 2506752 | tf_op jit(solution)/shard_map/all_to_all | solution.py:273
  432.0 48.7 %reduce-scatter.12.cloned.1.call-start = ((), (), s32[]{:S(2)}) async-start(), calls=%async_computation.19 | async-start | bytes 5160960 | tf_op jit(solution)/shard_map/reduce_scatter | solution.py:257
  432.7 100.6 %reduce-scatter.14.cloned.1.call-start = ((), (), s32[]{:S(2)}) async-start(), calls=%async_computation.20 | async-start | bytes 5160960 | tf_op jit(solution)/shard_map/reduce_scatter | solution.py:257
  484.6 37.4 %copy-start.17 = (bf16[72,4304]{1,0:T(8,128)(2,1)}, bf16[72,4304]{1,0:T(8,128)(2,1)S(1)}, u32[]{:S(2)}) copy-start(bf16[72,4304]{1,0:T(8,128)(2,1)S(1)} %fusion.38) | copy-start | bytes 1859332
  484.6 48.6 %collective-permute-start.11 = (bf16[72,4304]{1,0:T(8,128)(2,1)S(1)}, bf16[72,4304]{1,0:T(8,128)(2,1)}, u32[]{:S(2)}, u32[]{:S(2)}) collective-permute-start(bf16[72,4304]{1,0:T(8,128)(2,1)S(1)} %fusion.38), channel_id=1, source_target_pairs={{0,12},{4,8},{8,4},{12,0},{16,28},{20,24},{24,20},{28,16},{1,13},{... | collective-permute-start | bytes 1859336 | tf_op jit(solution)/shard_map/ppermute | solution.py:178
  487.1 46.2 %collective-permute-start.10 = (bf16[72,4304]{1,0:T(8,128)(2,1)S(1)}, bf16[72,4304]{1,0:T(8,128)(2,1)}, u32[]{:S(2)}, u32[]{:S(2)}) collective-permute-start(bf16[72,4304]{1,0:T(8,128)(2,1)S(1)} %fusion.38), channel_id=1, source_target_pairs={{0,8},{4,12},{8,0},{12,4},{16,24},{20,28},{24,16},{28,20},{1,9},{5... | collective-permute-start | bytes 1859336 | tf_op jit(solution)/shard_map/ppermute | solution.py:178
  487.6 45.6 %collective-permute-start.9 = (bf16[72,4304]{1,0:T(8,128)(2,1)S(1)}, bf16[72,4304]{1,0:T(8,128)(2,1)}, u32[]{:S(2)}, u32[]{:S(2)}) collective-permute-start(bf16[72,4304]{1,0:T(8,128)(2,1)S(1)} %fusion.38), channel_id=1, source_target_pairs={{0,4},{4,0},{8,12},{12,8},{16,20},{20,16},{24,28},{28,24},{1,5},{5... | collective-permute-start | bytes 1859336 | tf_op jit(solution)/shard_map/ppermute | solution.py:178
  493.7 28.4 %slice-start = ((s8[6782976]{0:T(1024)(128)(4,1)}), s8[2588672]{0:T(1024)(128)(4,1)S(1)}, s32[]{:S(2)}) async-start(s8[6782976]{0:T(1024)(128)(4,1)} %bitcast.105), calls=%async_computation.21 | async-start | bytes 5177344
  493.7 39.6 %all-to-all-start.6 = ((bf16[4,72,2880]{2,1,0:T(8,128)(2,1)}), bf16[4,72,2880]{2,1,0:T(8,128)(2,1)}, u32[]{:S(2)}, u32[]{:S(2)}) async-start(bf16[4,72,2880]{2,1,0:T(8,128)(2,1)} %bitcast.122), calls=%async_computation.10 | async-start | bytes 3391488 | tf_op jit(solution)/shard_map/all_to_all | solution.py:188
  498.6 23.6 %slice-start.1 = ((s8[6782976]{0:T(1024)(128)(4,1)}), s8[4194304]{0:T(1024)(128)(4,1)S(1)}, s32[]{:S(2)}) async-start(s8[6782976]{0:T(1024)(128)(4,1)} %bitcast.105), calls=%async_computation.22 | async-start | bytes 8388608
  498.6 23.6 %copy-start.31 = (f32[2,736]{1,0:T(2,128)S(1)}, f32[2,736]{1,0:T(2,128)}, u32[]{:S(2)}) copy-start(f32[2,736]{1,0:T(2,128)} %copy-done.30) | copy-start | bytes 17668
  537.3 94.4 %all-to-all-start.7 = ((bf16[4,2,184,1152]{3,2,1,0:T(8,128)(2,1)}), bf16[4,2,184,1152]{3,2,1,0:T(8,128)(2,1)S(1)}, u32[]{:S(2)}, u32[]{:S(2)}) async-start(bf16[4,2,184,1152]{3,2,1,0:T(8,128)(2,1)} %bitcast.118), calls=%async_computation.12 | async-start | bytes 6782976 | tf_op jit(solution)/shard_map/all_to_all | solution.py:188
  547.0 11.2 %collective-permute-start.18 = (f32[4,3380]{1,0:T(4,128)S(1)}, f32[4,3380]{1,0:T(4,128)S(1)}, u32[]{:S(2)}, u32[]{:S(2)}) collective-permute-start(f32[4,3380]{1,0:T(4,128)S(1)} %concatenate.65), channel_id=1, source_target_pairs={{0,3},{1,2},{2,1},{3,0},{4,7},{5,6},{6,5},{7,4},{8,11},{9,10},{10,... | collective-permute-start | bytes 162248 | tf_op jit(solution)/shard_map/ppermute | solution.py:178
  547.0 11.7 %collective-permute-start.17 = (f32[4,3380]{1,0:T(4,128)S(1)}, f32[4,3380]{1,0:T(4,128)}, u32[]{:S(2)}, u32[]{:S(2)}) collective-permute-start(f32[4,3380]{1,0:T(4,128)S(1)} %concatenate.65), channel_id=1, source_target_pairs={{0,2},{1,3},{2,0},{3,1},{4,6},{5,7},{6,4},{7,5},{8,10},{9,11},{10,... | collective-permute-start | bytes 162248 | tf_op jit(solution)/shard_map/ppermute | solution.py:178
  548.2 12.5 %collective-permute-start.16 = (f32[4,3380]{1,0:T(4,128)S(1)}, f32[4,3380]{1,0:T(4,128)}, u32[]{:S(2)}, u32[]{:S(2)}) collective-permute-start(f32[4,3380]{1,0:T(4,128)S(1)} %concatenate.65), channel_id=1, source_target_pairs={{0,1},{1,0},{2,3},{3,2},{4,5},{5,4},{6,7},{7,6},{8,9},{9,8},{10,11... | collective-permute-start | bytes 162248 | tf_op jit(solution)/shard_map/ppermute | solution.py:178
  551.5 53.4 %copy-start.19 = (bf16[72,2880]{1,0:T(8,128)(2,1)S(1)}, bf16[72,2880]{1,0:T(8,128)(2,1)}, u32[]{:S(2)}) copy-start(bf16[72,2880]{1,0:T(8,128)(2,1)} %reduce_sum.216) | copy-start | bytes 1244164
  551.5 49.0 %collective-permute-start.12 = (bf16[72,2880]{1,0:T(8,128)(2,1)}, bf16[72,2880]{1,0:T(8,128)(2,1)S(1)}, u32[]{:S(2)}, u32[]{:S(2)}) collective-permute-start(bf16[72,2880]{1,0:T(8,128)(2,1)} %reduce_sum.216), channel_id=1, source_target_pairs={{0,16},{4,20},{8,24},{12,28},{16,0},{20,4},{24,8},{28,12},{1,17},{... | collective-permute-start | bytes 1244168 | tf_op jit(solution)/shard_map/ppermute | solution.py:178
  555.1 42.2 %collective-permute-start.15 = (bf16[72,1728]{1,0:T(8,128)(2,1)S(1)}, bf16[72,1728]{1,0:T(8,128)(2,1)S(1)}, u32[]{:S(2)}, u32[]{:S(2)}) collective-permute-start(bf16[72,1728]{1,0:T(8,128)(2,1)S(1)} %get-tuple-element.299), channel_id=1, source_target_pairs={{0,12},{4,8},{8,4},{12,0},{16,28},{20,24},{24,20},{28,16},{1,13},{... | collective-permute-start | bytes 746504 | tf_op jit(solution)/shard_map/ppermute | solution.py:178
  558.1 42.3 %copy-start.37 = (f32[4,3380]{1,0:T(4,128)}, f32[4,3380]{1,0:T(4,128)S(1)}, u32[]{:S(2)}) copy-start(f32[4,3380]{1,0:T(4,128)S(1)} %collective-permute-done.18) | copy-start | bytes 162244
  558.1 42.3 %collective-permute-start.14 = (bf16[72,1728]{1,0:T(8,128)(2,1)S(1)}, bf16[72,1728]{1,0:T(8,128)(2,1)S(1)}, u32[]{:S(2)}, u32[]{:S(2)}) collective-permute-start(bf16[72,1728]{1,0:T(8,128)(2,1)S(1)} %get-tuple-element.300), channel_id=1, source_target_pairs={{0,8},{4,12},{8,0},{12,4},{16,24},{20,28},{24,16},{28,20},{1,9},{5... | collective-permute-start | bytes 746504 | tf_op jit(solution)/shard_map/ppermute | solution.py:178
  558.7 41.7 %collective-permute-start.13 = (bf16[72,1728]{1,0:T(8,128)(2,1)S(1)}, bf16[72,1728]{1,0:T(8,128)(2,1)S(1)}, u32[]{:S(2)}, u32[]{:S(2)}) collective-permute-start(bf16[72,1728]{1,0:T(8,128)(2,1)S(1)} %get-tuple-element.301), channel_id=1, source_target_pairs={{0,4},{4,0},{8,12},{12,8},{16,20},{20,16},{24,28},{28,24},{1,5},{5... | collective-permute-start | bytes 746504 | tf_op jit(solution)/shard_map/ppermute | solution.py:178
  601.3 7.8 %collective-permute-start.25 = (f32[4,3380]{1,0:T(4,128)S(1)}, f32[4,3380]{1,0:T(4,128)S(1)}, u32[]{:S(2)}, u32[]{:S(2)}) collective-permute-start(f32[4,3380]{1,0:T(4,128)S(1)} %add_add_fusion.1), channel_id=1, source_target_pairs={{0,12},{4,8},{8,4},{12,0},{16,28},{20,24},{24,20},{28,16},{1,13},{... | collective-permute-start | bytes 162248 | tf_op jit(solution)/shard_map/ppermute | solution.py:178
  602.8 6.9 %collective-permute-start.24 = (f32[4,3380]{1,0:T(4,128)S(1)}, f32[4,3380]{1,0:T(4,128)S(1)}, u32[]{:S(2)}, u32[]{:S(2)}) collective-permute-start(f32[4,3380]{1,0:T(4,128)S(1)} %add_add_fusion.1), channel_id=1, source_target_pairs={{0,8},{4,12},{8,0},{12,4},{16,24},{20,28},{24,16},{28,20},{1,9},{5... | collective-permute-start | bytes 162248 | tf_op jit(solution)/shard_map/ppermute | solution.py:178
  604.3 11.0 %collective-permute-start.23 = (f32[4,3380]{1,0:T(4,128)S(1)}, f32[4,3380]{1,0:T(4,128)S(1)}, u32[]{:S(2)}, u32[]{:S(2)}) collective-permute-start(f32[4,3380]{1,0:T(4,128)S(1)} %add_add_fusion.1), channel_id=1, source_target_pairs={{0,4},{4,0},{8,12},{12,8},{16,20},{20,16},{24,28},{28,24},{1,5},{5... | collective-permute-start | bytes 162248 | tf_op jit(solution)/shard_map/ppermute | solution.py:178
  605.0 25.9 %copy-start.18 = (bf16[72,2880]{1,0:T(8,128)(2,1)}, bf16[72,2880]{1,0:T(8,128)(2,1)S(1)}, u32[]{:S(2)}) copy-start(bf16[72,2880]{1,0:T(8,128)(2,1)S(1)} %add_convert_fusion.6) | copy-start | bytes 1244164
  605.0 23.8 %collective-permute-start.21 = (bf16[72,2880]{1,0:T(8,128)(2,1)S(1)}, bf16[72,2880]{1,0:T(8,128)(2,1)S(1)}, u32[]{:S(2)}, u32[]{:S(2)}) collective-permute-start(bf16[72,2880]{1,0:T(8,128)(2,1)S(1)} %add_convert_fusion.6), channel_id=1, source_target_pairs={{0,12},{4,8},{8,4},{12,0},{16,28},{20,24},{24,20},{28,16},{1,13},{... | collective-permute-start | bytes 1244168 | tf_op jit(solution)/shard_map/ppermute | solution.py:178
  606.5 24.4 %collective-permute-start.20 = (bf16[72,2880]{1,0:T(8,128)(2,1)S(1)}, bf16[72,2880]{1,0:T(8,128)(2,1)S(1)}, u32[]{:S(2)}, u32[]{:S(2)}) collective-permute-start(bf16[72,2880]{1,0:T(8,128)(2,1)S(1)} %add_convert_fusion.6), channel_id=1, source_target_pairs={{0,8},{4,12},{8,0},{12,4},{16,24},{20,28},{24,16},{28,20},{1,9},{5... | collective-permute-start | bytes 1244168 | tf_op jit(solution)/shard_map/ppermute | solution.py:178
  609.1 26.9 %copy-start.34 = (f32[4,3380]{1,0:T(4,128)}, f32[4,3380]{1,0:T(4,128)S(1)}, u32[]{:S(2)}) copy-start(f32[4,3380]{1,0:T(4,128)S(1)} %collective-permute-done.25) | copy-start | bytes 162244
  609.1 22.6 %collective-permute-start.19 = (bf16[72,2880]{1,0:T(8,128)(2,1)S(1)}, bf16[72,2880]{1,0:T(8,128)(2,1)}, u32[]{:S(2)}, u32[]{:S(2)}) collective-permute-start(bf16[72,2880]{1,0:T(8,128)(2,1)S(1)} %add_convert_fusion.6), channel_id=1, source_target_pairs={{0,4},{4,0},{8,12},{12,8},{16,20},{20,16},{24,28},{28,24},{1,5},{5... | collective-permute-start | bytes 1244168 | tf_op jit(solution)/shard_map/ppermute | solution.py:178
  610.4 18.4 %collective-permute-start.22 = (bf16[72,1728]{1,0:T(8,128)(2,1)S(1)}, bf16[72,1728]{1,0:T(8,128)(2,1)S(1)}, u32[]{:S(2)}, u32[]{:S(2)}) collective-permute-start(bf16[72,1728]{1,0:T(8,128)(2,1)S(1)} %add_convert_fusion.8), channel_id=1, source_target_pairs={{0,16},{4,20},{8,24},{12,28},{16,0},{20,4},{24,8},{28,12},{1,17},{... | collective-permute-start | bytes 746504 | tf_op jit(solution)/shard_map/ppermute | solution.py:178
  632.8 13.1 %collective-permute-start.28 = (bf16[72,1728]{1,0:T(8,128)(2,1)S(1)}, bf16[72,1728]{1,0:T(8,128)(2,1)S(1)}, u32[]{:S(2)}, u32[]{:S(2)}) collective-permute-start(bf16[72,1728]{1,0:T(8,128)(2,1)S(1)} %add_convert_fusion.7), channel_id=1, source_target_pairs={{0,12},{4,8},{8,4},{12,0},{16,28},{20,24},{24,20},{28,16},{1,13},{... | collective-permute-start | bytes 746504 | tf_op jit(solution)/shard_map/ppermute | solution.py:178
  636.0 10.7 %collective-permute-start.27 = (bf16[72,1728]{1,0:T(8,128)(2,1)S(1)}, bf16[72,1728]{1,0:T(8,128)(2,1)S(1)}, u32[]{:S(2)}, u32[]{:S(2)}) collective-permute-start(bf16[72,1728]{1,0:T(8,128)(2,1)S(1)} %add_convert_fusion.7), channel_id=1, source_target_pairs={{0,8},{4,12},{8,0},{12,4},{16,24},{20,28},{24,16},{28,20},{1,9},{5... | collective-permute-start | bytes 746504 | tf_op jit(solution)/shard_map/ppermute | solution.py:178
  636.0 10.6 %collective-permute-start.26 = (bf16[72,1728]{1,0:T(8,128)(2,1)S(1)}, bf16[72,1728]{1,0:T(8,128)(2,1)S(1)}, u32[]{:S(2)}, u32[]{:S(2)}) collective-permute-start(bf16[72,1728]{1,0:T(8,128)(2,1)S(1)} %add_convert_fusion.7), channel_id=1, source_target_pairs={{0,4},{4,0},{8,12},{12,8},{16,20},{20,16},{24,28},{28,24},{1,5},{5... | collective-permute-start | bytes 746504 | tf_op jit(solution)/shard_map/ppermute | solution.py:178
  638.3 7.6 %collective-permute-start.29 = (f32[4,3380]{1,0:T(4,128)S(1)}, f32[4,3380]{1,0:T(4,128)S(1)}, u32[]{:S(2)}, u32[]{:S(2)}) collective-permute-start(f32[4,3380]{1,0:T(4,128)S(1)} %add_add_fusion), channel_id=1, source_target_pairs={{0,16},{4,20},{8,24},{12,28},{16,0},{20,4},{24,8},{28,12},{1,17},{... | collective-permute-start | bytes 162248 | tf_op jit(solution)/shard_map/ppermute | solution.py:178
  (53 other events, 475.6 us)
Sparse Core Ops, SparseCore 0:
  10.4 64.4 all-gather.3
  76.5 67.6 all-gather.5
  145.7 67.5 all-gather.7
  215.8 82.2 reduce-scatter.5
  300.6 82.2 reduce-scatter.7
  385.9 34.8 reduce-scatter.9
  436.2 44.4 reduce-scatter.11
  483.9 44.0 reduce-scatter.13
